TPU v7x, 32 devices: a whole 2x2x4 slice. The times are simulated.
32 devices in a mesh: seq: 4 (over y, core), shard: 8 (over z, x).
Axes of the slice: x: 2, y: 2, z: 4, core: 2. Of those that a mesh axis runs over, the one named last changes fastest.
Arguments:
- hidden_in: bfloat16 [8, 1024, 1024], P('shard', 'seq'), may hold values from -6 to 6
- norm_gain: float32 [1024], replicated, may hold values from 0.5 to 1.5
- in_weight: bfloat16 [1024, 4384], P('shard'), may hold values from -0.1875 to 0.1875
- conv_weight: float32 [4, 2304], replicated, may hold values from -3 to 3
- conv_bias: float32 [2304], replicated, may hold values from -0.5 to 0.5
- dt_bias: float32 [32], replicated, may hold values from -4 to -1
- a_log: float32 [32], replicated, may hold values from -6 to 1
- skip: float32 [32], replicated, may hold values from 0.5 to 1.5
- inner_gain: float32 [2048], replicated, may hold values from 0.5 to 1.5
- out_weight: bfloat16 [2048, 1024], P('shard'), may hold values from -0.125 to 0.125
- out_grad: float32 [8, 1024, 1024], P('shard', 'seq'), may hold values from -6 to 6
Outputs:
- block_out: float32 [8, 1024, 1024], P('shard', 'seq')
- input_grad: float32 [8, 1024, 1024], P('shard', 'seq')
- norm_gain_grad: float32 [1024], replicated
- in_weight_grad: float32 [1024, 4384], P('shard')
- conv_weight_grad: float32 [4, 2304], replicated
- conv_bias_grad: float32 [2304], replicated
- dt_bias_grad: float32 [32], replicated
- a_log_grad: float32 [32], replicated
- skip_grad: float32 [32], replicated
- inner_gain_grad: float32 [2048], replicated
- out_weight_grad: float32 [2048, 1024], P('shard')
All inputs are finite; a program needn't handle non-finite values.
Results may differ from a plain program's by a relative error of at most 0.015.
Values may be sent and summed in bfloat16 or wider, within the bound.
No kernel may reach another device: no remote copies, remote signals or barrier semaphores. Data moves between devices by JAX's collectives and lax.ppermute only.
A program may use at most 128 MiB of HBM per device.

v0:
```python
import jax
import jax.numpy as jnp
from jax import lax
from jax.sharding import PartitionSpec as P

STATE = 128
GROUP = 256


norm_eps = 1e-05
highest = lax.Precision.HIGHEST


def passed_along(block, axis, distance):
    devices = range(lax.axis_size(axis))
    route = [(i - distance, i) for i in devices if i - distance in devices]
    return lax.ppermute(block, axis, route)


def contract_rows(left, right):
    return lax.dot_general(
        left, right, (((0,), (0,)), ((), ())), preferred_element_type=jnp.float32
    )


def contract_cols(left, right):
    return lax.dot_general(
        left, right, (((1,), (1,)), ((), ())), preferred_element_type=jnp.float32
    )


def section_one(conv_ext, dt_raw, conv_weight, conv_bias, dt_bias, a_log):
    rows = dt_raw.shape[0]
    width = conv_weight.shape[0]
    conv_out = conv_bias + conv_weight[0] * conv_ext[0:rows]
    for offset in range(1, width):
        conv_out = conv_out + conv_weight[offset] * conv_ext[offset : offset + rows]
    active = jax.nn.silu(conv_out)
    inner = conv_out.shape[1] - 2 * STATE
    x_heads = active[:, :inner]
    b_proj = active[:, inner : inner + STATE]
    c_proj = active[:, inner + STATE :]
    step_size = jax.nn.softplus(dt_raw + dt_bias)
    log_decay = -step_size * jnp.exp(a_log)
    return (x_heads, b_proj, c_proj, step_size, log_decay)


def ssd_groups(x_heads, b_proj, c_proj, step_size, log_decay, h_start):
    rows, heads = step_size.shape
    head_dim = x_heads.shape[1] // heads
    state_dim = b_proj.shape[1]
    blocks = rows // GROUP
    lower = jnp.arange(GROUP)[:, None] >= jnp.arange(GROUP)[None, :]
    mask = lower[None, :, :]

    def ssd_advance(state, pieces):
        x_blk, b_blk, c_blk, dt_blk, ld_blk = pieces
        cumul = jnp.cumsum(ld_blk, axis=0)
        cum_t = cumul.T
        spread = cum_t[:, :, None] - cum_t[:, None, :]
        kernel = jnp.where(mask, jnp.exp(jnp.where(mask, spread, 0.0)), 0.0)
        intersection = jnp.dot(c_blk, b_blk.T, precision=highest)
        kernel = kernel * intersection[None, :, :] * dt_blk.T[:, None, :]
        output = jnp.einsum("hts,shp->thp", kernel, x_blk, precision=highest)
        output = output + jnp.exp(cumul)[:, :, None] * jnp.einsum(
            "hpn,tn->thp", state, c_blk, precision=highest
        )
        weight_tail = jnp.exp(cumul[-1][None, :] - cumul) * dt_blk
        fresh = jnp.einsum("sh,shp,sn->hpn", weight_tail, x_blk, b_blk, precision=highest)
        state = jnp.exp(cumul[-1])[:, None, None] * state + fresh
        return (state, output)

    pieces = (
        x_heads.reshape(blocks, GROUP, heads, head_dim),
        b_proj.reshape(blocks, GROUP, state_dim),
        c_proj.reshape(blocks, GROUP, state_dim),
        step_size.reshape(blocks, GROUP, heads),
        log_decay.reshape(blocks, GROUP, heads),
    )
    h_end, outputs = lax.scan(ssd_advance, h_start, pieces)
    return (outputs.reshape(rows, heads * head_dim), h_end)


def end_states(x_heads, b_proj, step_size, log_decay, h_start):
    rows, heads = step_size.shape
    head_dim = x_heads.shape[1] // heads
    state_dim = b_proj.shape[1]
    blocks = rows // GROUP

    def end_advance(state, pieces):
        x_blk, b_blk, dt_blk, ld_blk = pieces
        cumul = jnp.cumsum(ld_blk, axis=0)
        weight_tail = jnp.exp(cumul[-1][None, :] - cumul) * dt_blk
        fresh = jnp.einsum("sh,shp,sn->hpn", weight_tail, x_blk, b_blk, precision=highest)
        return (jnp.exp(cumul[-1])[:, None, None] * state + fresh, None)

    pieces = (
        x_heads.reshape(blocks, GROUP, heads, head_dim),
        b_proj.reshape(blocks, GROUP, state_dim),
        step_size.reshape(blocks, GROUP, heads),
        log_decay.reshape(blocks, GROUP, heads),
    )
    h_end, unused = lax.scan(end_advance, h_start, pieces)
    return h_end


def section_three(ssd_out, x_heads, gate_z, skip, inner_gain):
    rows = ssd_out.shape[0]
    heads = skip.shape[0]
    mixed = ssd_out + (x_heads.reshape(rows, heads, -1) * skip[None, :, None]).reshape(rows, -1)
    gated_in = mixed * jax.nn.silu(gate_z)
    scale = lax.rsqrt(jnp.mean(gated_in * gated_in, axis=-1, keepdims=True) + norm_eps)
    return gated_in * scale * inner_gain


def body(
    hidden_in,
    norm_gain,
    in_weight,
    conv_weight,
    conv_bias,
    dt_bias,
    a_log,
    skip,
    inner_gain,
    out_weight,
    out_grad,
):
    tokens = hidden_in[0]
    tokens_f = tokens.astype(jnp.float32)
    cotan = out_grad[0]
    inner = inner_gain.shape[0]
    conv_dim = conv_bias.shape[0]
    width = conv_weight.shape[0]
    heads = dt_bias.shape[0]
    head_dim = inner // heads
    rows = tokens.shape[0]
    edge = rows - (width - 1)
    full_in, full_out = (
        lax.all_gather(in_weight, "shard", axis=0, tiled=True),
        lax.all_gather(out_weight, "shard", axis=0, tiled=True),
    )
    rstat = lax.rsqrt(jnp.mean(tokens_f * tokens_f, axis=-1, keepdims=True) + norm_eps)
    normed = (tokens_f * rstat * norm_gain).astype(jnp.bfloat16)
    projected = jnp.dot(normed, full_in, preferred_element_type=jnp.float32)
    gate_z = projected[:, :inner]
    conv_in = projected[:, inner : inner + conv_dim].astype(jnp.bfloat16)
    dt_raw = projected[:, inner + conv_dim :]
    before = passed_along(conv_in[edge:], "seq", 1)
    conv_ext = jnp.concatenate([before, conv_in], axis=0).astype(jnp.float32)
    firsts, back_one = jax.vjp(
        section_one, conv_ext, dt_raw, conv_weight, conv_bias, dt_bias, a_log
    )
    x_heads, b_proj, c_proj, step_size, log_decay = firsts
    h_zero = jnp.zeros((heads, head_dim, b_proj.shape[1]), jnp.float32)
    local_state = end_states(x_heads, b_proj, step_size, log_decay, h_zero)
    passing = jnp.exp(jnp.sum(log_decay, axis=0))

    def relay_step(turn, incoming):
        return passed_along(passing[:, None, None] * incoming + local_state, "seq", 1)

    h_in = lax.fori_loop(0, lax.axis_size("seq") - 1, relay_step, h_zero)

    def scan_states(x_one, b_one, c_one, s_one, l_one):
        return ssd_groups(x_one, b_one, c_one, s_one, l_one, h_in)

    (ssd_out, unused), back_two = jax.vjp(
        scan_states, x_heads, b_proj, c_proj, step_size, log_decay
    )
    growth = jnp.exp(jnp.cumsum(log_decay, axis=0))
    gated_pre, back_three = jax.vjp(section_three, ssd_out, x_heads, gate_z, skip, inner_gain)
    gated = gated_pre.astype(jnp.bfloat16)
    block_out = tokens_f + jnp.dot(gated, full_out, preferred_element_type=jnp.float32)
    cot_b = cotan.astype(jnp.bfloat16)
    d_gated = contract_cols(cot_b, lax.all_gather(out_weight, "shard", axis=0, tiled=True))
    d_ssd, d_x_three, d_gate, skip_grad, inner_gain_grad = back_three(d_gated)
    d_heads = d_ssd.reshape(rows, heads, head_dim)
    pulled = jnp.einsum("th,thp,tn->hpn", growth, d_heads, c_proj, precision=highest)

    def back_step(turn, later):
        return passed_along(
            (pulled + passing[:, None, None] * later).astype(jnp.bfloat16), "seq", -1
        ).astype(jnp.float32)

    h_grad = lax.fori_loop(0, lax.axis_size("seq") - 1, back_step, h_zero)
    d_x_two, d_b, d_c, d_step, d_log = back_two((d_ssd, h_grad))
    d_ext, d_dt_raw, conv_weight_part, conv_bias_part, dt_bias_part, a_log_part = back_one(
        (d_x_two + d_x_three, d_b, d_c, d_step, d_log)
    )
    returned = passed_along(d_ext[: width - 1], "seq", -1)
    d_conv = d_ext[width - 1 :]
    d_conv = jnp.concatenate([d_conv[:edge], d_conv[edge:] + returned], axis=0)
    d_proj = jnp.concatenate([d_gate, d_conv, d_dt_raw], axis=1).astype(jnp.bfloat16)
    d_normed = contract_cols(d_proj, lax.all_gather(in_weight, "shard", axis=0, tiled=True))
    norm_part = jnp.sum(d_normed * tokens_f * rstat, axis=0)
    scaled = norm_gain * d_normed
    input_grad = (
        cotan
        + rstat * scaled
        - tokens_f * rstat * rstat * rstat * jnp.mean(scaled * tokens_f, axis=-1, keepdims=True)
    )
    in_share = lax.psum_scatter(
        contract_rows(normed, d_proj).astype(jnp.bfloat16), "shard", scatter_dimension=0, tiled=True
    )
    out_share = lax.psum_scatter(
        contract_rows(gated, cot_b).astype(jnp.bfloat16), "shard", scatter_dimension=0, tiled=True
    )
    in_weight_grad, out_weight_grad = (
        lax.psum(in_share, "seq").astype(jnp.float32),
        lax.psum(out_share, "seq").astype(jnp.float32),
    )
    smalls = lax.psum(
        (
            norm_part,
            conv_weight_part,
            conv_bias_part,
            dt_bias_part,
            a_log_part,
            skip_grad,
            inner_gain_grad,
        ),
        ("seq", "shard"),
    )
    (
        norm_gain_grad,
        conv_weight_grad,
        conv_bias_grad,
        dt_bias_grad,
        a_log_grad,
        skip_total,
        gain_total,
    ) = smalls
    return (
        block_out[None],
        input_grad[None],
        norm_gain_grad,
        in_weight_grad,
        conv_weight_grad,
        conv_bias_grad,
        dt_bias_grad,
        a_log_grad,
        skip_total,
        gain_total,
        out_weight_grad,
    )


def solution(mesh):
    placed = (
        P("shard", "seq", None),
        P(),
        P("shard", None),
        P(),
        P(),
        P(),
        P(),
        P(),
        P(),
        P("shard", None),
        P("shard", "seq", None),
    )
    return jax.shard_map(
        body,
        mesh=mesh,
        in_specs=placed,
        out_specs=(
            P("shard", "seq", None),
            P("shard", "seq", None),
            P(),
            P("shard", None),
            P(),
            P(),
            P(),
            P(),
            P(),
            P(),
            P("shard", None),
        ),
        check_vma=False,
    )
```

profile of v0, /device:TPU:0, one launch (start us, length us, event | category | flops | bytes accessed | tf_op | source)
XLA Modules:
  0.0 726.8 jit_solution(14364811259111382184)
XLA Ops:
  13.8 131.1 %all-gather.3.cloned.1.call-done = bf16[1024,4384]{0,1:T(8,128)(2,1)} async-done(((bf16[128,4384]{0,1:T(8,128)(2,1)}), bf16[1024,4384]{0,1:T(8,128)(2,1)}) %all-gather.3.cloned.1.call-update) | async-done | bytes 8978448 | tf_op jit(solution)/shard_map/all_gather | solution.py:140
  144.9 6.3 fusion.107
  172.7 4.4 fusion.40
  177.2 44.0 %while.17 = (s32[]{:T(128)}, f32[32,64,128]{2,1,0:T(8,128)S(1)}, f32[32]{0:T(128)S(1)}, f32[32,64,128]{2,1,0:T(8,128)}, s32[]{:T(128)}) while((s32[]{:T(128)}, f32[32,64,128]{2,1,0:T(8,128)S(1)}, f32[32]{0:T(128)S(1)}, f32[32,64,128]{2,1,0:T(8,128)}, s32[]{:T(128)}) %tuple.98), condition=%wide.region_5.6_spmd, body=%wide.region_4.5_spmd.sunk | while | flops 524290 | bytes 7340261 | solution.py:162
  179.6 4.1 collective-permute-start
  188.5 11.5 %collective-permute-start = (f32[32,64,128]{2,1,0:T(8,128)}, f32[32,64,128]{2,1,0:T(8,128)S(1)}, u32[]{:S(2)}, u32[]{:S(2)}) collective-permute-start(f32[32,64,128]{2,1,0:T(8,128)} %multiply_add_fusion.7), channel_id=1, source_target_pairs={{0,8},{8,16},{16,24},{1,9},{9,17},{17,25},{2,10},{10,18},{18,26},{... | collective-permute-start | bytes 3145736 | tf_op jit(solution)/shard_map/while/body/eval_jaxpr/ppermute | solution.py:17
  204.8 13.9 %collective-permute-start = (f32[32,64,128]{2,1,0:T(8,128)}, f32[32,64,128]{2,1,0:T(8,128)S(1)}, u32[]{:S(2)}, u32[]{:S(2)}) collective-permute-start(f32[32,64,128]{2,1,0:T(8,128)} %multiply_add_fusion.7), channel_id=1, source_target_pairs={{0,8},{8,16},{16,24},{1,9},{9,17},{17,25},{2,10},{10,18},{18,26},{... | collective-permute-start | bytes 3145736 | tf_op jit(solution)/shard_map/while/body/eval_jaxpr/ppermute | solution.py:17
  224.1 11.9 %bitcast_add_fusion.1 = f32[256,32,64]{0,2,1:T(8,128)} fusion(f32[256,32,64]{0,2,1:T(8,128)S(1)} %fusion.78, f32[256,32,64]{0,2,1:T(8,128)S(1)} %bitcast.138, f32[32,256]{1,0:T(8,128)S(1)} %copy-done.48, f32[256,256]{1,0:T(8,128)S(1)} %copy-done.29, f32[32,256]{1,0:T(8,128)S(1)} %copy-done.50, pred[256,256]{1,0:T(8,128)(4,1)S(1)} %copy-done.44, ...), kind=kOutput, calls=%fused_computation.48 | convolution fusion | flops 1622147072 | bytes 6717440 | tf_op jit(solution)/shard_map/jvp()/while/body/eval_jaxpr/hts,shp->thp/dot_general | solution.py:64
  239.1 4.9 multiply_reduce_fusion.11
  245.2 5.6 multiply_reduce_fusion.7
  250.9 4.6 multiply_reduce_fusion.8
  258.5 3.4 multiply_reduce_fusion.9
  261.9 3.7 fusion.29
  265.6 51.5 %while.18 = (s32[]{:T(128)}, f32[32,64,128]{2,1,0:T(8,128)}, f32[32]{0:T(128)}, f32[32,64,128]{2,1,0:T(8,128)}, s32[]{:T(128)}, /*index=5*/s32[]{:T(128)}) while((s32[]{:T(128)}, f32[32,64,128]{2,1,0:T(8,128)}, f32[32]{0:T(128)}, f32[32,64,128]{2,1,0:T(8,128)}, s32[]{:T(128)}, /*index=5*/s32[]{:T(128)}) %tuple.115), condition=%wide.region_10.11_spmd.clone, body=%wide.region_9.10_spmd.clone.sunk | while | flops 1310723 | bytes 6291703 | solution.py:185
  269.1 14.3 %collective-permute-done.1 = bf16[32,64,128]{2,1,0:T(8,128)(2,1)} collective-permute-done((bf16[32,64,128]{2,1,0:T(8,128)(2,1)}, bf16[32,64,128]{2,1,0:T(8,128)(2,1)}, u32[]{:S(2)}, u32[]{:S(2)}) %collective-permute-start.1) | collective-permute-done | bytes 524320 | tf_op jit(solution)/shard_map/while/body/eval_jaxpr/ppermute | solution.py:17
  289.3 10.2 %collective-permute-done.1 = bf16[32,64,128]{2,1,0:T(8,128)(2,1)} collective-permute-done((bf16[32,64,128]{2,1,0:T(8,128)(2,1)}, bf16[32,64,128]{2,1,0:T(8,128)(2,1)}, u32[]{:S(2)}, u32[]{:S(2)}) %collective-permute-start.1) | collective-permute-done | bytes 524320 | tf_op jit(solution)/shard_map/while/body/eval_jaxpr/ppermute | solution.py:17
  305.5 9.5 %collective-permute-done.1 = bf16[32,64,128]{2,1,0:T(8,128)(2,1)} collective-permute-done((bf16[32,64,128]{2,1,0:T(8,128)(2,1)}, bf16[32,64,128]{2,1,0:T(8,128)(2,1)}, u32[]{:S(2)}, u32[]{:S(2)}) %collective-permute-start.1) | collective-permute-done | bytes 524320 | tf_op jit(solution)/shard_map/while/body/eval_jaxpr/ppermute | solution.py:17
  317.1 3.8 multiply_reduce_fusion.6
  322.6 4.1 fusion.46
  326.7 14.6 %fusion.10 = (f32[32,256]{1,0:T(8,128)}, f32[32,256]{1,0:T(8,128)}, f32[32,256]{1,0:T(8,128)}, f32[256,256]{1,0:T(8,128)}) fusion(f32[32,256]{1,0:T(8,128)S(1)} %copy-done.49, f32[256,256]{1,0:T(8,128)S(1)} %copy-done.30, f32[32,256]{1,0:T(8,128)S(1)} %copy-done.51, pred[256,256]{1,0:T(8,128)(4,1)S(1)} %copy-done.45, f32[32,64,256]{2,1,0:T(8,128)S(1)} %bitcast.142, ...), kind=kOutput, calls=%fused_computation.15 | convolution fusion | flops 1641979904 | bytes 4947968 | tf_op jit(solution)/shard_map/transpose(jvp())/while/body/eval_jaxpr/hts,shp->thp/dot_general | solution.py:64
  341.3 8.8 %bitcast_add_fusion = f32[256,32,64]{0,2,1:T(8,128)} fusion(f32[256,32,64]{0,2,1:T(8,128)S(1)} %get-tuple-element.505, f32[32,64,256]{2,1,0:T(8,128)S(1)} %bitcast.143, f32[32,256]{1,0:T(8,128)S(1)} %copy-done.49, f32[256,256]{1,0:T(8,128)S(1)} %copy-done.30, f32[32,256]{1,0:T(8,128)S(1)} %copy-done.51, pred[256,256]{1,0:T(8,128)(4,1)S(1)} %copy-done.45, ...), kind=kOutput, calls=%fused_computation.47 | convolution fusion | flops 1622147072 | bytes 6717440 | tf_op jit(solution)/shard_map/transpose(jvp())/while/body/eval_jaxpr/hts,shp->thp/dot_general | solution.py:64
  352.9 5.8 fusion.106
  361.7 5.2 convolution_bitcast_fusion
  387.7 5.7 collective-permute-done.3
  394.4 6.1 convolution_convert_fusion
  400.6 11.8 %copy.162 = bf16[1024,4384]{1,0:T(8,128)(2,1)} copy(bf16[1024,4384]{0,1:T(8,128)(2,1)} %convolution_convert_fusion) | data formatting | bytes 17956864
  414.2 3.4 convolution_convert_fusion.1
  418.6 4.7 fusion.43
  423.2 149.3 %reduce-scatter.7.cloned.1.call-done = bf16[128,4384]{1,0:T(8,128)(2,1)} async-done(((bf16[1024,4384]{1,0:T(8,128)(2,1)}), bf16[128,4384]{1,0:T(8,128)(2,1)}) %reduce-scatter.7.cloned.1.call-update) | async-done | bytes 1122320
  574.9 88.6 %reduce-scatter.5.cloned.1.call-done = bf16[256,1024]{1,0:T(8,128)(2,1)} async-done(((bf16[2048,1024]{1,0:T(8,128)(2,1)}), bf16[256,1024]{1,0:T(8,128)(2,1)}) %reduce-scatter.5.cloned.1.call-update) | async-done | bytes 524304 | tf_op jit(solution)/shard_map/reduce_scatter | solution.py:205
  663.5 7.6 %fusion.57 = (f32[1024]{0:T(1024)S(1)}, f32[256]{0:T(256)S(1)}, f32[256,1024]{1,0:T(8,128)}) fusion(bf16[1,256,1024]{2,1,0:T(8,128)(2,1)S(1)} %copy-done.23, f32[256]{0:T(256)S(1)} %copy-done.64, f32[1024]{0:T(1024)S(1)} %copy-done.57, bf16[1024,4384]{0,1:T(8,128)(2,1)} %all-gather.3.cloned.1.call-done, bf16[256,32]{1,0:T(8,128)(2,1)S(1)} %get-tuple-element.482, ...), kind=kOutput, calls=%fused_computation.92 | convolution fusion | flops 2309290752 | bytes 12806144 | tf_op jit(solution)/shard_map/dot_general | solution.py:27
  671.1 42.5 %all-reduce.13 = (f32[1024]{0:T(1024)}, f32[4,2304]{1,0:T(4,128)}, f32[2304]{0:T(1024)}, f32[32]{0:T(128)}, f32[32]{0:T(128)}, /*index=5*/f32[32]{0:T(128)}, f32[2048]{0:T(1024)}) all-reduce(f32[1024]{0:T(1024)S(1)} %get-tuple-element.448, f32[4,2304]{1,0:T(4,128)S(1)} %pad_add_fusion.2, ...), channel_id=1, replica_groups=mesh['seq'=4,'shard'=8] {'seq','shard'}, use_global_device_ids=true, to_apply=%region_21.22 | all-reduce | flops 14688 | bytes 117504 | tf_op jit(solution)/shard_map/psum | solution.py:212
  (251 shorter events, 110.6 us)
Async XLA Ops:
  7.2 137.8 %copy-start.21 = (bf16[1,256,1024]{2,1,0:T(8,128)(2,1)S(1)}, bf16[1,256,1024]{2,1,0:T(8,128)(2,1)}, u32[]{:S(2)}) copy-start(bf16[1,256,1024]{2,1,0:T(8,128)(2,1)} %param.15) | copy-start | bytes 1572868
  7.2 137.8 %copy-start.56 = (f32[1024]{0:T(1024)S(1)}, f32[1024]{0:T(1024)}, u32[]{:S(2)}) copy-start(f32[1024]{0:T(1024)} %param.16) | copy-start | bytes 12292
  7.2 137.7 %all-gather.3.cloned.1.call-start = ((), (), s32[]{:S(2)}) async-start(), calls=%async_computation.2 | async-start | bytes 10100736 | tf_op jit(solution)/shard_map/all_gather | solution.py:140
  7.9 237.2 %all-gather.5.cloned.1.call-start = ((), (), s32[]{:S(2)}) async-start(), calls=%async_computation.3 | async-start | bytes 4718592 | tf_op jit(solution)/shard_map/all_gather | solution.py:141
  8.7 563.9 %reduce-scatter.7.cloned.1.call-start = ((), (), s32[]{:S(2)}) async-start(), calls=%async_computation.5 | async-start | bytes 10321920
  9.4 143.6 %copy-start.67 = (f32[32]{0:T(128)}, f32[32]{0:T(128)S(1)}, u32[]{:S(2)}) copy-start(f32[32]{0:T(128)S(1)} %exp.120) | copy-start | bytes 388
  12.5 149.3 %copy-start.34 = (f32[2304]{0:T(1024)}, f32[2304]{0:T(1024)S(1)}, u32[]{:S(2)}) copy-start(f32[2304]{0:T(1024)S(1)} %get-tuple-element.450) | copy-start | bytes 27652
  12.5 149.3 %copy-start.36 = (f32[2304]{0:T(1024)}, f32[2304]{0:T(1024)S(1)}, u32[]{:S(2)}) copy-start(f32[2304]{0:T(1024)S(1)} %get-tuple-element.451) | copy-start | bytes 27652
  12.5 149.3 %copy-start.38 = (f32[2304]{0:T(1024)}, f32[2304]{0:T(1024)S(1)}, u32[]{:S(2)}) copy-start(f32[2304]{0:T(1024)S(1)} %get-tuple-element.452) | copy-start | bytes 27652
  12.5 149.3 %copy-start.40 = (f32[2304]{0:T(1024)}, f32[2304]{0:T(1024)S(1)}, u32[]{:S(2)}) copy-start(f32[2304]{0:T(1024)S(1)} %get-tuple-element.453) | copy-start | bytes 27652
  13.8 137.4 %copy-start.63 = (f32[256]{0:T(256)}, f32[256]{0:T(256)S(1)}, u32[]{:S(2)}) copy-start(f32[256]{0:T(256)S(1)} %add_rsqrt_fusion) | copy-start | bytes 3076
  13.8 139.5 %copy-start.58 = (f32[32]{0:T(128)S(1)}, f32[32]{0:T(128)}, u32[]{:S(2)}) copy-start(f32[32]{0:T(128)} %param.20) | copy-start | bytes 388
  151.2 9.0 %collective-permute-start.2 = (bf16[3,2304]{1,0:T(4,128)(2,1)S(1)}, bf16[3,2304]{1,0:T(4,128)(2,1)S(1)}, u32[]{:S(2)}, u32[]{:S(2)}) collective-permute-start(bf16[3,2304]{1,0:T(4,128)(2,1)S(1)} %slice.123), channel_id=1, source_target_pairs={{0,8},{8,16},{16,24},{1,9},{9,17},{17,25},{2,10},{10,18},{18,26},{... | collective-permute-start | bytes 41480 | tf_op jit(solution)/shard_map/ppermute | solution.py:17
  179.6 6.5 collective-permute-start
  188.5 13.9 %collective-permute-start = (f32[32,64,128]{2,1,0:T(8,128)}, f32[32,64,128]{2,1,0:T(8,128)S(1)}, u32[]{:S(2)}, u32[]{:S(2)}) collective-permute-start(f32[32,64,128]{2,1,0:T(8,128)} %multiply_add_fusion.7), channel_id=1, source_target_pairs={{0,8},{8,16},{16,24},{1,9},{9,17},{17,25},{2,10},{10,18},{18,26},{... | collective-permute-start | bytes 3145736 | tf_op jit(solution)/shard_map/while/body/eval_jaxpr/ppermute | solution.py:17
  204.8 16.3 %collective-permute-start = (f32[32,64,128]{2,1,0:T(8,128)}, f32[32,64,128]{2,1,0:T(8,128)S(1)}, u32[]{:S(2)}, u32[]{:S(2)}) collective-permute-start(f32[32,64,128]{2,1,0:T(8,128)} %multiply_add_fusion.7), channel_id=1, source_target_pairs={{0,8},{8,16},{16,24},{1,9},{9,17},{17,25},{2,10},{10,18},{18,26},{... | collective-permute-start | bytes 3145736 | tf_op jit(solution)/shard_map/while/body/eval_jaxpr/ppermute | solution.py:17
  221.1 14.9 %copy-start.46 = (f32[32]{0:T(128)}, f32[32]{0:T(128)S(1)}, u32[]{:S(2)}) copy-start(f32[32]{0:T(128)S(1)} %get-tuple-element.620) | copy-start | bytes 388
  224.1 11.9 %copy-start.17 = (f32[256,32,64]{0,2,1:T(8,128)}, f32[256,32,64]{0,2,1:T(8,128)S(1)}, u32[]{:S(2)}) copy-start(f32[256,32,64]{0,2,1:T(8,128)S(1)} %fusion.78) | copy-start | bytes 6291460
  267.8 15.6 %collective-permute-start.1 = (bf16[32,64,128]{2,1,0:T(8,128)(2,1)}, bf16[32,64,128]{2,1,0:T(8,128)(2,1)}, u32[]{:S(2)}, u32[]{:S(2)}) collective-permute-start(bf16[32,64,128]{2,1,0:T(8,128)(2,1)} %fusion.132), channel_id=1, source_target_pairs={{8,0},{16,8},{24,16},{9,1},{17,9},{25,17},{10,2},{18,10},{26,18},{... | collective-permute-start | bytes 1572872 | tf_op jit(solution)/shard_map/while/body/eval_jaxpr/ppermute | solution.py:17
  288.1 11.4 %collective-permute-start.1 = (bf16[32,64,128]{2,1,0:T(8,128)(2,1)}, bf16[32,64,128]{2,1,0:T(8,128)(2,1)}, u32[]{:S(2)}, u32[]{:S(2)}) collective-permute-start(bf16[32,64,128]{2,1,0:T(8,128)(2,1)} %fusion.132), channel_id=1, source_target_pairs={{8,0},{16,8},{24,16},{9,1},{17,9},{25,17},{10,2},{18,10},{26,18},{... | collective-permute-start | bytes 1572872 | tf_op jit(solution)/shard_map/while/body/eval_jaxpr/ppermute | solution.py:17
  304.2 10.8 %collective-permute-start.1 = (bf16[32,64,128]{2,1,0:T(8,128)(2,1)}, bf16[32,64,128]{2,1,0:T(8,128)(2,1)}, u32[]{:S(2)}, u32[]{:S(2)}) collective-permute-start(bf16[32,64,128]{2,1,0:T(8,128)(2,1)} %fusion.132), channel_id=1, source_target_pairs={{8,0},{16,8},{24,16},{9,1},{17,9},{25,17},{10,2},{18,10},{26,18},{... | collective-permute-start | bytes 1572872 | tf_op jit(solution)/shard_map/while/body/eval_jaxpr/ppermute | solution.py:17
  361.7 8.2 %copy-start.15 = (f32[256,2304]{1,0:T(8,128)S(1)}, f32[256,2304]{1,0:T(8,128)}, u32[]{:S(2)}) copy-start(f32[256,2304]{1,0:T(8,128)} %get-tuple-element.487) | copy-start | bytes 7077892
  361.7 8.2 %copy-start.18 = (f32[256,2048]{1,0:T(8,128)S(1)}, f32[256,2048]{1,0:T(8,128)}, u32[]{:S(2)}) copy-start(f32[256,2048]{1,0:T(8,128)} %get-tuple-element.499) | copy-start | bytes 6291460
  378.0 7.0 copy-start.68
  383.5 9.9 %copy-start.6 = (f32[256,2304]{1,0:T(8,128)S(1)}, f32[256,2304]{1,0:T(8,128)}, u32[]{:S(2)}) copy-start(f32[256,2304]{1,0:T(8,128)} %copy-done.5) | copy-start | bytes 7077892
  383.5 9.9 %collective-permute-start.3 = (f32[3,2304]{1,0:T(4,128)S(1)}, f32[3,2304]{1,0:T(4,128)S(1)}, u32[]{:S(2)}, u32[]{:S(2)}) collective-permute-start(f32[3,2304]{1,0:T(4,128)S(1)} %pad_add_fusion.1), channel_id=1, source_target_pairs={{8,0},{16,8},{24,16},{9,1},{17,9},{25,17},{10,2},{18,10},{26,18},{... | collective-permute-start | bytes 82952 | tf_op jit(solution)/shard_map/ppermute | solution.py:17
  387.6 6.8 copy-start.24
  412.4 251.1 %reduce-scatter.5.cloned.1.call-start = ((), (), s32[]{:S(2)}) async-start(), calls=%async_computation.4 | async-start | bytes 4718592 | tf_op jit(solution)/shard_map/reduce_scatter | solution.py:205
  417.6 298.5 %all-reduce.17.cloned.1.call-start = ((), (), s32[]{:S(2)}) async-start(), calls=%async_computation.6 | async-start | bytes 3293184 | tf_op jit(solution)/shard_map/psum | solution.py:209
  423.2 240.3 %copy-start.23 = (bf16[1,256,1024]{2,1,0:T(8,128)(2,1)S(1)}, bf16[1,256,1024]{2,1,0:T(8,128)(2,1)}, u32[]{:S(2)}) copy-start(bf16[1,256,1024]{2,1,0:T(8,128)(2,1)} %param.15) | copy-start | bytes 1572868
  423.2 240.3 %copy-start.25 = (bf16[253,2304]{1,0:T(8,128)(2,1)S(1)}, bf16[253,2304]{1,0:T(8,128)(2,1)}, u32[]{:S(2)}) copy-start(bf16[253,2304]{1,0:T(8,128)(2,1)} %copy-done.24) | copy-start | bytes 3497476
  663.5 7.6 %copy-start.55 = (f32[2048]{0:T(1024)S(1)}, f32[2048]{0:T(1024)}, u32[]{:S(2)}) copy-start(f32[2048]{0:T(1024)} %get-tuple-element.445) | copy-start | bytes 24580
  (52 other events, 180.5 us)
Sparse Core Ops, SparseCore 0:
  10.1 134.8 all-gather.2
  147.1 71.0 all-gather.4
  412.5 160.0 reduce-scatter.6
  576.1 87.3 reduce-scatter.4
  666.4 44.9 all-reduce.16
where the time goes:
time: 731 us; the launch traced here: 727 us
  waiting for transfers between devices  417 us (57%)
  matrix products  97.9 us (13%)
  other arithmetic  67.7 us (9%)
  local copies, waits for them, and re-layouts  49.5 us (7%)
  blocking collectives  42.5 us (6%)
  starting transfers between devices  36.7 us (5%)
  between operations  14.9 us (2%)
    unnamed x6, waiting for transfers between devices  151 us
    all_gather x1, waiting for transfers between devices, body(): lax.all_gather(in_weight, 'shard', axis=0, tiled=True)  131 us
    reduce_scatter x1, waiting for transfers between devices, body(): lax.psum_scatter(contract_rows(gated, cot_b).astype(jnp.bfloat16), 'shard...  88.6 us
    ppermute x8, waiting for transfers between devices, passed_along(): return lax.ppermute(block, axis, route)  46.9 us
    psum x1, blocking collectives, body(): lax.psum((norm_part, conv_weight_part, conv_bias_part, dt_bias_part, a_lo...  42.5 us
    ppermute x8, starting transfers between devices, passed_along(): return lax.ppermute(block, axis, route)  36.5 us
    dot_general x3, matrix products, ssd_advance(): output = jnp.einsum('hts,shp->thp', kernel, x_blk, precision=highest)  35.2 us
    unnamed x144, local copies, waits for them, and re-layouts  22.5 us
  transfers between devices with their start and end apart: 13, of which 10 were waited for; matrix products, arithmetic and copies ran while one was open for 12% of the time, Pallas kernels for 0%

commit v1 on v0

v1 whole, which is shorter than its diff:
```python
import functools

import jax
import jax.numpy as jnp
from jax import lax
from jax.experimental import pallas as pl
from jax.experimental.pallas import tpu as pltpu
from jax.sharding import PartitionSpec as P

bf16 = jnp.bfloat16
f32 = jnp.float32
highest = lax.Precision.HIGHEST
norm_eps = 1e-05
LANES = 128
CHUNK = 128
HALO = 8

VMEM = pl.BlockSpec(memory_space=pltpu.VMEM)
SMEM = pl.BlockSpec(memory_space=pltpu.SMEM)
ANY = pl.BlockSpec(memory_space=pl.ANY)


def swap(block, axis, distance):
    n = lax.axis_size(axis)
    return lax.ppermute(block, axis, [(i, i ^ distance) for i in range(n)])


def seq_gather(block):
    n = lax.axis_size("seq")
    blocks = {0: block}
    d = n // 2
    while d >= 1:
        for o in list(blocks):
            blocks[o ^ d] = swap(blocks[o], "seq", d)
        d //= 2
    return [blocks[o] for o in range(n)]


def seq_sorted(blocks):
    me = lax.axis_index("seq")
    d = 1
    while d < len(blocks):
        odd = (me // d) % 2 == 1
        blocks = [jnp.where(odd, blocks[o ^ d], blocks[o]) for o in range(len(blocks))]
        d *= 2
    return blocks


def seq_scatter(parts):
    n = lax.axis_size("seq")
    me = lax.axis_index("seq")
    d = 1
    while d < n:
        m = parts.shape[0]
        pairs = parts.reshape((m // 2, 2) + parts.shape[1:])
        bit = (me // d) % 2
        keep = lax.dynamic_index_in_dim(pairs, bit, 1, keepdims=False)
        send = lax.dynamic_index_in_dim(pairs, 1 - bit, 1, keepdims=False)
        parts = keep.astype(f32) + swap(send.astype(bf16), "seq", d).astype(f32)
        d *= 2
    return parts[0]


def all_sum(block, axis):
    n = lax.axis_size(axis)
    d = 1
    while d < n:
        block = block + swap(block, axis, d)
        d *= 2
    return block


def ring_index(place, n):
    place = lax.rem(place + 2 * n, n)
    return jnp.where(place < n // 2, 2 * place, 2 * (n - place) - 1)


def ring_place(shard, n):
    return jnp.where(shard % 2 == 0, shard // 2, n - (shard + 1) // 2)


def ring_routes(n):
    order = list(range(0, n, 2)) + list(range(n - 1, 0, -2))
    ahead = [(order[p], order[(p + 1) % n]) for p in range(n)]
    return ahead, [(b, a) for a, b in ahead]


def ring_gather(block, cut):
    n = lax.axis_size("shard")
    ahead, back = ring_routes(n)
    place = ring_place(lax.axis_index("shard"), n)
    found = [(block, lax.axis_index("shard"), 0)]
    a = b = block
    for k in range(1, n // 2):
        a = lax.ppermute(a, "shard", ahead)
        b = lax.ppermute(b, "shard", back)
        found.append((a, ring_index(place - k, n), 0))
        found.append((b, ring_index(place + k, n), 0))
    owner = ring_index(place - n // 2, n)
    found.append((lax.ppermute(a[:, :cut], "shard", ahead), owner, 0))
    found.append((lax.ppermute(b[:, cut:], "shard", back), owner, cut))
    return found


def ring_scatter(parts, cut):
    n = lax.axis_size("shard")
    ahead, back = ring_routes(n)
    place = ring_place(lax.axis_index("shard"), n)

    def pick(p, lo, hi):
        return lax.dynamic_index_in_dim(parts, ring_index(p, n), 0, keepdims=False)[:, lo:hi]

    width = parts.shape[2]
    a = pick(place - 1, 0, cut).astype(bf16)
    b = pick(place + 1, cut, width).astype(bf16)
    for k in range(1, n):
        a = lax.ppermute(a, "shard", ahead)
        b = lax.ppermute(b, "shard", back)
        a = (a.astype(f32) + pick(place - 1 - k, 0, cut)).astype(bf16)
        b = (b.astype(f32) + pick(place + 1 + k, cut, width)).astype(bf16)
    return a, b


def sigmoid(v):
    return 1.0 / (1.0 + jnp.exp(-v))


def softplus(v):
    return jnp.maximum(v, 0.0) + jnp.log1p(jnp.exp(-jnp.abs(v)))


def dot(left, right, l, r, precision=None):
    return lax.dot_general(
        left, right, (((l,), (r,)), ((), ())), preferred_element_type=f32, precision=precision
    )


def spread(per_head, hd, cols):
    rows = per_head.shape[0]
    lane = lax.broadcasted_iota(jnp.int32, (rows, LANES), 1)
    tiles = []
    per = LANES // hd
    for j in range(cols // LANES):
        tile = jnp.broadcast_to(per_head[:, j * per : j * per + 1], (rows, LANES))
        for i in range(1, per):
            h = j * per + i
            tile = jnp.where(
                lane >= i * hd, jnp.broadcast_to(per_head[:, h : h + 1], (rows, LANES)), tile
            )
        tiles.append(tile)
    return jnp.concatenate(tiles, axis=1) if len(tiles) > 1 else tiles[0]


def decay_rows(cum_t, hd, heads, state):
    last = cum_t.shape[1] - 1
    return jnp.concatenate(
        [
            jnp.broadcast_to(jnp.exp(cum_t[h : h + 1, last : last + 1]), (hd, state))
            for h in range(heads)
        ],
        axis=0,
    )


def assemble(index, copies, sems):
    handles = []
    for i, (src, dst, slot, col) in enumerate(copies):
        rows, cols = src.shape
        place = pl.multiple_of(index[slot] * rows, rows)
        handle = pltpu.make_async_copy(
            src, dst.at[pl.ds(place, rows), col : col + cols], sems.at[i]
        )
        handle.start()
        handles.append(handle)
    for handle in handles:
        handle.wait()


def decays(dt_raw, dt_bias, a_log):
    rows = dt_raw.shape[0]
    row = lax.broadcasted_iota(jnp.int32, (rows, rows), 0)
    col = lax.broadcasted_iota(jnp.int32, (rows, rows), 1)
    lower = jnp.where(row >= col, 1.0, 0.0).astype(f32)
    step = softplus(dt_raw + dt_bias)
    log_decay = -step * jnp.exp(a_log)
    cum = dot(lower, log_decay, 1, 0, highest)
    cum_t = dot(log_decay, lower, 0, 1, highest)
    return step, log_decay, cum, cum_t


def front_kernel(dims, index, *refs):
    hd, heads, cols, state, n_tok, w_cols = dims
    n_w = len(w_cols)
    tok_refs = refs[:n_tok]
    w_refs = refs[n_tok : n_tok + n_w]
    gain, conv_w, conv_b, dt_bias, a_log = refs[n_tok + n_w : n_tok + n_w + 5]
    normed, w_all, conv_in, conv_out, dt_raw, scan_out, states = refs[n_tok + n_w + 5 : -4]
    tokens, held, halo, sems = refs[-4:]
    conv_cols = cols + 2 * state
    width = 4 if conv_w.shape[0] == 4 else conv_w.shape[0]
    assemble(
        index,
        [(r, tokens, i, 0) for i, r in enumerate(tok_refs)]
        + [(r, w_all, n_tok + i, w_cols[i]) for i, r in enumerate(w_refs)],
        sems,
    )
    held[...] = jnp.zeros_like(held)
    halo[...] = jnp.zeros_like(halo)
    row = lax.broadcasted_iota(jnp.int32, (CHUNK, CHUNK), 0)
    col = lax.broadcasted_iota(jnp.int32, (CHUNK, CHUNK), 1)
    mask = row >= col
    per = LANES // hd

    @pl.loop(0, tokens.shape[0] // CHUNK)
    def _(c):
        at = pl.ds(pl.multiple_of(c * CHUNK, CHUNK), CHUNK)
        tok = tokens[at, :].astype(f32)
        rstat = lax.rsqrt(jnp.mean(tok * tok, axis=1, keepdims=True) + norm_eps)
        nrm = (tok * rstat * gain[...]).astype(bf16)
        normed[at, :] = nrm
        proj = dot(nrm, w_all[...], 1, 0)
        narrow = proj[:, :conv_cols].astype(bf16)
        conv_in[at, :] = narrow
        wide = narrow.astype(f32)
        both = jnp.concatenate([halo[...], wide], axis=0)
        halo[...] = wide[CHUNK - HALO :, :]
        first = HALO - (width - 1)
        v = conv_b[...] + conv_w[0:1, :] * both[first : first + CHUNK, :]
        for k in range(1, width):
            v = v + conv_w[k : k + 1, :] * both[first + k : first + k + CHUNK, :]
        conv_out[at, :] = v
        active = v * sigmoid(v)
        raw = proj[:, conv_cols:]
        dt_raw[at, :] = raw
        step, log_decay, cum, cum_t = decays(raw, dt_bias[...], a_log[...])
        xd = active[:, :cols] * spread(step, hd, cols)
        xd_b = xd.astype(bf16)
        b_b = active[:, cols : cols + state].astype(bf16)
        c_b = active[:, cols + state :].astype(bf16)
        cross = dot(c_b, b_b, 1, 1)
        before = held[...]
        before_b = before.astype(bf16)
        states[c] = before_b
        tiles = []
        for j in range(cols // LANES):
            tile = None
            for i in range(per):
                h = j * per + i
                gap = cum[:, h : h + 1] - cum_t[h : h + 1, :]
                kern = (jnp.exp(jnp.where(mask, gap, -1e30)) * cross).astype(bf16)
                out = dot(kern, xd_b[:, j * LANES : (j + 1) * LANES], 1, 0)
                tile = out if tile is None else jnp.where(col >= i * hd, out, tile)
            tiles.append(tile)
        intra = jnp.concatenate(tiles, axis=1) if len(tiles) > 1 else tiles[0]
        inter = spread(jnp.exp(cum), hd, cols) * dot(c_b, before_b, 1, 1)
        scan_out[at, :] = intra + inter
        tail = jnp.exp(cum[CHUNK - 1 : CHUNK, :] - cum)
        xt = (xd * spread(tail, hd, cols)).astype(bf16)
        held[...] = decay_rows(cum_t, hd, heads, state) * before + dot(xt, b_b, 0, 0)


def gate_kernel(dims, index, *refs):
    cols, n_tok, w_cols, z_width = dims
    n_w = len(w_cols)
    cot_refs = refs[:n_tok]
    w_refs = refs[n_tok : n_tok + n_w]
    normed, conv_out, scan_out, skip, gain = refs[n_tok + n_w : n_tok + n_w + 5]
    cotan, wz, wo, gate, gated_in, d_gated, sums = refs[n_tok + n_w + 5 : -1]
    sems = refs[-1]
    copies = [(r, cotan, i, 0) for i, r in enumerate(cot_refs)]
    assemble_two(index, copies, w_refs, w_cols, n_tok, wz, wo, sems)
    lane = lax.broadcasted_iota(jnp.int32, (CHUNK, CHUNK), 1)

    @pl.loop(0, normed.shape[0] // CHUNK)
    def _(c):
        at = pl.ds(pl.multiple_of(c * CHUNK, CHUNK), CHUNK)
        z = dot(normed[at, :], wz[...], 1, 0)
        dg = dot(cotan[at, :], wo[...], 1, 1)
        v = conv_out[at, :cols]
        mixed = scan_out[at, :] + skip[...] * (v * sigmoid(v))
        gi = mixed * (z * sigmoid(z))
        gate[at, :] = z
        gated_in[at, :] = gi
        d_gated[at, :] = dg
        squares = jnp.sum(gi * gi, axis=1, keepdims=True)
        slopes = jnp.sum(gi * dg * gain[...], axis=1, keepdims=True)
        both = jnp.where(lane == 0, squares, jnp.where(lane == 1, slopes, 0.0))
        sums[:, at] = jnp.transpose(both)[:8, :]


def assemble_two(index, copies, w_refs, w_cols, first, wz, wo, sems):
    rows = w_refs[0].shape[0]
    z_width = wz.shape[1]
    handles = []

    def start(src, dst):
        handle = pltpu.make_async_copy(src, dst, sems.at[len(handles)])
        handle.start()
        handles.append(handle)

    for src, dst, slot, col in copies:
        size = src.shape[0]
        start(src, dst.at[pl.ds(pl.multiple_of(index[slot] * size, size), size), :])
    half = z_width // 2
    steps = wo.shape[1] // half
    per = wo.shape[0] // (2 * rows)
    for i, src in enumerate(w_refs):
        owner = index[first + i]
        col = w_cols[i]
        if col == 0:
            part = src if src.shape[1] == z_width else src.at[:, 0:z_width]
            start(part, wz.at[pl.ds(pl.multiple_of(owner * rows, rows), rows), :])
        if col + src.shape[1] == 2 * z_width:
            at = 0 if col else z_width
            band = pl.multiple_of(lax.rem(owner, per) * (2 * rows), 2 * rows)
            column = pl.multiple_of(lax.div(owner, per) * half, half)
            for t in range(2):
                start(
                    src.at[:, at + t * half : at + (t + 1) * half],
                    wo.at[pl.ds(band + t * rows, rows), pl.ds(column, half)],
                )
    for handle in handles:
        handle.wait()


def turn_kernel(dims, gate, gated_in, d_gated, conv_out, scan_out, sums, skip, gain, *outs):
    cols, inner = dims
    gated, d_gate, d_mixed, gain_grad = outs
    gain_grad[...] = jnp.zeros_like(gain_grad)

    @pl.loop(0, gate.shape[0] // CHUNK)
    def _(c):
        at = pl.ds(pl.multiple_of(c * CHUNK, CHUNK), CHUNK)
        stat = jnp.transpose(sums[:, at])
        scale = lax.rsqrt(stat[:, 0:1] / inner + norm_eps)
        slope = scale * scale * scale * (stat[:, 1:2] / inner)
        gi = gated_in[at, :]
        dg = d_gated[at, :]
        scaled = gi * scale
        gated[at, :] = (scaled * gain[...]).astype(bf16)
        gain_grad[...] += jnp.sum(dg * scaled, axis=0, keepdims=True)
        d_gi = scale * (gain[...] * dg) - gi * slope
        z = gate[at, :]
        sig = sigmoid(z)
        v = conv_out[at, :cols]
        mixed = scan_out[at, :] + skip[...] * (v * sigmoid(v))
        d_mixed[at, :] = d_gi * (z * sig)
        d_gate[at, :] = (d_gi * mixed * (sig * (1.0 + z * (1.0 - sig)))).astype(bf16)


def back_kernel(dims, *refs):
    hd, heads, cols, state = dims
    conv_in, conv_out, dt_raw, scan_out, states, d_mixed = refs[:6]
    conv_w, dt_bias, a_log, skip, picks = refs[6:11]
    d_proj, conv_grad, head_grad = refs[11:14]
    held, halo = refs[14:]
    conv_cols = cols + 2 * state
    width = conv_w.shape[0]
    held[...] = jnp.zeros_like(held)
    halo[...] = jnp.zeros_like(halo)
    conv_grad[...] = jnp.zeros_like(conv_grad)
    head_grad[...] = jnp.zeros_like(head_grad)
    row = lax.broadcasted_iota(jnp.int32, (CHUNK, CHUNK), 0)
    col = lax.broadcasted_iota(jnp.int32, (CHUNK, CHUNK), 1)
    mask = row >= col
    upper = jnp.where(row <= col, 1.0, 0.0).astype(f32)
    per = LANES // hd
    chunks = conv_in.shape[0] // CHUNK

    @pl.loop(0, chunks)
    def _(turn):
        c = chunks - 1 - turn
        at = pl.ds(pl.multiple_of(c * CHUNK, CHUNK), CHUNK)
        v = conv_out[at, :]
        sig = sigmoid(v)
        active = v * sig
        raw = dt_raw[at, :]
        step, log_decay, cum, cum_t = decays(raw, dt_bias[...], a_log[...])
        step_s = spread(step, hd, cols)
        x = active[:, :cols]
        xd = x * step_s
        xd_b = xd.astype(bf16)
        b_b = active[:, cols : cols + state].astype(bf16)
        c_b = active[:, cols + state :].astype(bf16)
        cross = dot(c_b, b_b, 1, 1)
        dm = d_mixed[at, :]
        dy_b = dm.astype(bf16)
        before_b = states[c]
        later = held[...]
        later_b = later.astype(bf16)
        d_cross = jnp.zeros((CHUNK, CHUNK), f32)
        tiles = []
        for j in range(cols // LANES):
            tile = None
            dm_tile = dm[:, j * LANES : (j + 1) * LANES]
            for i in range(per):
                h = j * per + i
                gap = cum[:, h : h + 1] - cum_t[h : h + 1, :]
                fall = jnp.exp(jnp.where(mask, gap, -1e30))
                kern = (fall * cross).astype(bf16)
                out = dot(kern, dy_b[:, j * LANES : (j + 1) * LANES], 0, 0)
                tile = out if tile is None else jnp.where(col >= i * hd, out, tile)
                own = (col >= i * hd) & (col < (i + 1) * hd)
                dy_h = jnp.where(own, dm_tile, 0.0).astype(bf16)
                d_cross = d_cross + fall * dot(dy_h, xd_b[:, j * LANES : (j + 1) * LANES], 1, 1)
            tiles.append(tile)
        intra = jnp.concatenate(tiles, axis=1) if len(tiles) > 1 else tiles[0]
        d_cross_b = d_cross.astype(bf16)
        grown = spread(jnp.exp(cum), hd, cols)
        dy_g = (dm * grown).astype(bf16)
        tail_s = spread(jnp.exp(cum[CHUNK - 1 : CHUNK, :] - cum), hd, cols)
        xt = (xd * tail_s).astype(bf16)
        d_c = dot(d_cross_b, b_b, 1, 0) + dot(dy_g, before_b, 1, 0)
        d_b = dot(d_cross_b, c_b, 0, 0) + dot(xt, later_b, 1, 0)
        inter = tail_s * dot(b_b, later_b, 1, 1)
        held[...] = decay_rows(cum_t, hd, heads, state) * later + dot(dy_g, c_b, 0, 0)
        d_xd = intra + inter
        carried = xd * inter
        change = (
            dy_b.astype(f32) * scan_out[at, :] - xd_b.astype(f32) * intra - carried
        )
        change_h = dot(change, picks[...], 1, 0, highest)
        step_h = dot(x * d_xd, picks[...], 1, 0, highest)
        skip_h = dot(jnp.sum(dm * x, axis=0, keepdims=True), picks[...], 1, 0, highest)
        ones = jnp.ones((8, state), f32)
        kept = dot(ones, before_b.astype(f32) * later, 1, 1, highest)
        kept_h = dot(kept, picks[...], 1, 0, highest)[0:1, :]
        carried_h = dot(jnp.sum(carried, axis=0, keepdims=True), picks[...], 1, 0, highest)
        d_log = (
            dot(upper, change_h, 1, 0, highest)
            + jnp.exp(cum[CHUNK - 1 : CHUNK, :]) * kept_h
            + carried_h
        )
        d_step = step_h - d_log * jnp.exp(a_log[...])
        d_raw = jnp.where(col < heads, d_step * sigmoid(raw + dt_bias[...]), 0.0)
        head_grad[0:1, :] += jnp.sum(d_raw, axis=0, keepdims=True)
        head_grad[1:2, :] += jnp.sum(d_log * log_decay, axis=0, keepdims=True)
        head_grad[2:3, :] += skip_h
        d_x = step_s * d_xd + skip[...] * dm
        d_active = jnp.concatenate([d_x, d_b, d_c], axis=1)
        d_v = d_active * (sig * (1.0 + v * (1.0 - sig)))
        both = jnp.concatenate([d_v, halo[...]], axis=0)
        halo[...] = d_v[:HALO, :]
        entered = conv_in[at, :].astype(f32)
        d_in = None
        for k in range(width):
            shifted = both[width - 1 - k : width - 1 - k + CHUNK, :]
            term = conv_w[k : k + 1, :] * shifted
            d_in = term if d_in is None else d_in + term
            conv_grad[k : k + 1, :] += jnp.sum(entered * shifted, axis=0, keepdims=True)
        conv_grad[width : width + 1, :] += jnp.sum(d_v, axis=0, keepdims=True)
        d_proj[at, :conv_cols] = d_in.astype(bf16)
        d_proj[at, conv_cols:] = d_raw.astype(bf16)


def shaped(shape, kind):
    return jax.ShapeDtypeStruct(shape, kind)


def body(
    hidden_in,
    norm_gain,
    in_weight,
    conv_weight,
    conv_bias,
    dt_bias,
    a_log,
    skip,
    inner_gain,
    out_weight,
    out_grad,
):
    n_seq = lax.axis_size("seq")
    n_shard = lax.axis_size("shard")
    me = lax.axis_index("seq")
    own = hidden_in[0]
    cotan_own = out_grad[0]
    rows, model = own.shape
    length = rows * n_seq
    inner = inner_gain.shape[0]
    conv_dim = conv_bias.shape[0]
    width = conv_weight.shape[0]
    heads_all = dt_bias.shape[0]
    hd = inner // heads_all
    state = (conv_dim - inner) // 2
    cols = inner // n_seq
    heads = heads_all // n_seq
    deep = in_weight.shape[0]
    conv_cols = cols + 2 * state
    one = conv_cols + LANES
    chunks = length // CHUNK

    def columns(array, start, size):
        return lax.dynamic_slice_in_dim(array, start, size, axis=array.ndim - 1)

    w_dt = columns(in_weight, inner + conv_dim + me * heads, heads)
    slab_one = jnp.concatenate(
        [
            columns(in_weight, inner + me * cols, cols),
            in_weight[:, 2 * inner : 2 * inner + 2 * state],
            jnp.pad(w_dt, ((0, 0), (0, LANES - heads))),
        ],
        axis=1,
    )
    bands = n_shard // n_seq
    strip = model // n_seq
    route = [
        (q * n_shard + s, (s // bands) * n_shard + q * bands + s % bands)
        for s in range(n_shard)
        for q in range(n_seq)
    ]
    out_rows = out_weight.shape[0]
    strips = out_weight.reshape(out_rows, n_seq, strip)
    sent = lax.dynamic_index_in_dim(strips, me, 1, keepdims=False)
    tile = lax.ppermute(sent, ("seq", "shard"), route)
    slab_two = jnp.concatenate(
        [columns(in_weight, me * cols, cols), tile[:deep], tile[deep:]], axis=1
    )

    tok_blocks = seq_gather(own)
    cut_one = one // LANES // 2 * LANES
    ring_one = ring_gather(slab_one, cut_one)
    cot_blocks = seq_gather(cotan_own.astype(bf16))
    ring_two = ring_gather(slab_two, cols)

    places = [me ^ o for o in range(n_seq)]
    conv_w = jnp.concatenate([columns(conv_weight, me * cols, cols), conv_weight[:, inner:]], 1)
    conv_b = jnp.concatenate([columns(conv_bias, me * cols, cols), conv_bias[inner:]])[None]
    pad_heads = lambda a: jnp.pad(columns(a, me * heads, heads), (0, LANES - heads))[None]
    dt_bias_h = pad_heads(dt_bias)
    a_log_h = pad_heads(a_log)
    skip_s = jnp.repeat(columns(skip, me * heads, heads), hd)[None]
    gain_s = columns(inner_gain, me * cols, cols)[None]
    picks = jnp.where(jnp.arange(cols)[:, None] // hd == jnp.arange(LANES)[None, :], 1.0, 0.0)
    picks = picks.astype(f32)

    index_one = jnp.stack(places + [o for _, o, _ in ring_one]).astype(jnp.int32)
    n_one = len(ring_one)
    normed, w_one, conv_in, conv_out, dt_raw, scan_out, states = pl.pallas_call(
        functools.partial(
            front_kernel, (hd, heads, cols, state, n_seq, tuple(c for _, _, c in ring_one))
        ),
        name="front",
        in_specs=[SMEM] + [ANY] * (n_seq + n_one) + [VMEM] * 5,
        out_specs=[VMEM] * 7,
        out_shape=[
            shaped((length, model), bf16),
            shaped((model, one), bf16),
            shaped((length, conv_cols), bf16),
            shaped((length, conv_cols), f32),
            shaped((length, LANES), f32),
            shaped((length, cols), f32),
            shaped((chunks, cols, state), bf16),
        ],
        scratch_shapes=[
            pltpu.VMEM((length, model), bf16),
            pltpu.VMEM((cols, state), f32),
            pltpu.VMEM((HALO, conv_cols), f32),
            pltpu.SemaphoreType.DMA((n_seq + n_one,)),
        ],
        cost_estimate=pl.CostEstimate(
            flops=2 * length * model * one + 8 * length * CHUNK * cols,
            bytes_accessed=12 * length * model,
            transcendentals=length * CHUNK * heads,
        ),
    )(
        index_one,
        *tok_blocks,
        *[b for b, _, _ in ring_one],
        norm_gain[None],
        conv_w,
        conv_b,
        dt_bias_h,
        a_log_h,
    )

    index_two = jnp.stack(places + [o for _, o, _ in ring_two]).astype(jnp.int32)
    n_two = len(ring_two)
    cotan, w_z, w_o, gate, gated_in, d_gated, sums = pl.pallas_call(
        functools.partial(
            gate_kernel, (cols, n_seq, tuple(c for _, _, c in ring_two), cols)
        ),
        name="gate",
        in_specs=[SMEM] + [ANY] * (n_seq + n_two) + [VMEM] * 5,
        out_specs=[VMEM] * 7,
        out_shape=[
            shaped((length, model), bf16),
            shaped((model, cols), bf16),
            shaped((cols, model), bf16),
            shaped((length, cols), f32),
            shaped((length, cols), f32),
            shaped((length, cols), f32),
            shaped((8, length), f32),
        ],
        scratch_shapes=[pltpu.SemaphoreType.DMA((n_seq + 3 * n_two,))],
        cost_estimate=pl.CostEstimate(
            flops=4 * length * model * cols,
            bytes_accessed=14 * length * model,
            transcendentals=2 * length * cols,
        ),
    )(
        index_two,
        *cot_blocks,
        *[b for b, _, _ in ring_two],
        normed,
        conv_out,
        scan_out,
        skip_s,
        gain_s,
    )

    sums = all_sum(sums, "seq")
    gated, d_gate, d_mixed, gain_part = pl.pallas_call(
        functools.partial(turn_kernel, (cols, inner)),
        name="turn",
        in_specs=[VMEM] * 8,
        out_specs=[VMEM] * 4,
        out_shape=[
            shaped((length, cols), bf16),
            shaped((length, cols), bf16),
            shaped((length, cols), f32),
            shaped((1, cols), f32),
        ],
        cost_estimate=pl.CostEstimate(
            flops=30 * length * cols, bytes_accessed=30 * length * cols, transcendentals=0
        ),
    )(gate, gated_in, d_gated, conv_out, scan_out, sums, skip_s, gain_s)

    out_parts = jnp.dot(gated, w_o, preferred_element_type=f32)
    block_out = own.astype(f32) + seq_scatter(out_parts.reshape(n_seq, rows, model))

    z_grad = dot(normed, d_gate, 0, 0).reshape(n_shard, deep, cols)
    o_grad = dot(gated, cotan, 0, 0)
    o_grad = o_grad.reshape(bands, 2, deep, n_seq, strip).transpose(3, 0, 2, 1, 4)
    o_grad = o_grad.reshape(n_shard, deep, cols)
    z_own, o_own = ring_scatter(jnp.concatenate([z_grad, o_grad], axis=2), cols)
    o_own = jnp.concatenate([o_own[:, :strip], o_own[:, strip:]], axis=0)
    o_own = lax.ppermute(o_own, ("seq", "shard"), [(b, a) for a, b in route])
    o_all = seq_sorted(seq_gather(o_own))
    z_all = seq_sorted(seq_gather(z_own))
    out_weight_grad = jnp.concatenate(o_all, axis=1).astype(f32)

    d_proj, conv_part, head_part = pl.pallas_call(
        functools.partial(back_kernel, (hd, heads, cols, state)),
        name="back",
        in_specs=[VMEM] * 11,
        out_specs=[VMEM] * 3,
        out_shape=[
            shaped((length, one), bf16),
            shaped((8, conv_cols), f32),
            shaped((8, LANES), f32),
        ],
        scratch_shapes=[pltpu.VMEM((cols, state), f32), pltpu.VMEM((HALO, conv_cols), f32)],
        cost_estimate=pl.CostEstimate(
            flops=20 * length * CHUNK * cols,
            bytes_accessed=14 * length * model,
            transcendentals=length * CHUNK * heads,
        ),
    )(
        conv_in,
        conv_out,
        dt_raw,
        scan_out,
        states,
        d_mixed,
        conv_w,
        dt_bias_h,
        a_log_h,
        skip_s,
        picks,
    )

    one_parts = dot(normed, d_proj, 0, 0).reshape(n_shard, deep, one)
    one_a, one_b = ring_scatter(one_parts, cut_one)
    one_all = seq_sorted(seq_gather(jnp.concatenate([one_a, one_b], axis=1)))

    d_normed = dot(d_proj, w_one, 1, 1) + dot(d_gate, w_z, 1, 1)
    norm_part = jnp.sum(d_normed * normed.astype(f32), axis=0) / norm_gain
    d_own = seq_scatter(d_normed.reshape(n_seq, rows, model))
    own_f = own.astype(f32)
    rstat = lax.rsqrt(jnp.mean(own_f * own_f, axis=-1, keepdims=True) + norm_eps)
    scaled = norm_gain * d_own
    input_grad = (
        cotan_own
        + rstat * scaled
        - own_f * rstat * rstat * rstat * jnp.mean(scaled * own_f, axis=-1, keepdims=True)
    )

    packed = jnp.concatenate(
        [
            conv_part.reshape(-1),
            head_part.reshape(-1),
            gain_part.reshape(-1),
            norm_part,
        ]
    ).reshape(-1, LANES)
    packs = [p.reshape(-1) for p in seq_sorted(seq_gather(all_sum(packed, "shard")))]
    edges = [8 * conv_cols, 8 * LANES, cols, model]
    convs, head_parts, gains, norms = [], [], [], []
    for p in packs:
        at = 0
        for size, bin_ in zip(edges, (convs, head_parts, gains, norms)):
            bin_.append(p[at : at + size])
            at += size
    convs = [c.reshape(8, conv_cols) for c in convs]
    head_parts = [h.reshape(8, LANES) for h in head_parts]
    conv_all = jnp.concatenate([c[:, :cols] for c in convs] + [sum(c[:, cols:] for c in convs)], 1)
    head_all = jnp.concatenate([h[:, :heads] for h in head_parts], axis=1)

    shared = sum(o[:, cols:conv_cols].astype(f32) for o in one_all)
    in_weight_grad = jnp.concatenate(
        [z.astype(f32) for z in z_all]
        + [o[:, :cols].astype(f32) for o in one_all]
        + [shared]
        + [o[:, conv_cols : conv_cols + heads].astype(f32) for o in one_all],
        axis=1,
    )
    return (
        block_out[None],
        input_grad[None],
        sum(norms),
        in_weight_grad,
        conv_all[:width],
        conv_all[width],
        head_all[0],
        head_all[1],
        head_all[2],
        jnp.concatenate(gains),
        out_weight_grad,
    )


def solution(mesh):
    tokens = P("shard", "seq", None)
    rows = P("shard", None)
    return jax.shard_map(
        body,
        mesh=mesh,
        in_specs=(tokens, P(), rows, P(), P(), P(), P(), P(), P(), rows, tokens),
        out_specs=(tokens, tokens, P(), rows, P(), P(), P(), P(), P(), P(), rows),
        check_vma=False,
    )
```

time: 731 us -> 328 us (0.45)
  waiting for transfers between devices: 417 us -> 51.5 us
  matrix products: 97.9 us -> 16.1 us
  Pallas kernels: 0 us -> 77.3 us
  starting transfers between devices: 36.7 us -> 89.8 us
  blocking collectives: 42.5 us -> 0 us
  other arithmetic: 67.7 us -> 37.4 us
  between operations: 14.9 us -> 1.96 us
    unnamed x6 -> x0, waiting for transfers between devices: 151 us -> none
    all_gather x2 -> x0, waiting for transfers between devices: 131 us -> none  [the longest x1 131 us: body(): lax.all_gather(in_weight, 'shard', axis=0, tiled=True)]
    reduce_scatter x1 -> x0, waiting for transfers between devices: 88.6 us -> none  [body(): lax.psum_scatter(contract_rows(gated, cot_b).astype(jnp.bfloat16), 'shard...]
    dot_general x18 -> x6, matrix products: 97.9 us -> 16.1 us  [the longest x5 13.6 us: dot(): lax.dot_general(left, right, (((l,), (r,)), ((), ())), preferred_element_...]
    pallas_call x0 -> x4, Pallas kernels: none -> 77.3 us  [the longest x1 31.9 us: body(): pl.pallas_call(functools.partial(back_kernel, (hd, heads, cols, state)),...]
    ppermute x8 -> x73, starting transfers between devices: 36.5 us -> 89.8 us  [the longest x27 29.9 us: swap(): return lax.ppermute(block, axis, [(i, i ^ distance) for i in range(n)])]
    psum x1 -> x0, blocking collectives: 42.5 us -> none  [body(): lax.psum((norm_part, conv_weight_part, conv_bias_part, dt_bias_part, a_lo...]
    reduce_sum x10 -> x1, other arithmetic: 19.7 us -> 1.7 us  [body(): jnp.mean(own_f * own_f, axis=-1, keepdims=True) + norm_eps]
  transfers between devices with their start and end apart: 13 -> 73, of which waited for: 10 -> 31; matrix products, arithmetic and copies ran while one was open for 12% -> 19% of each run, Pallas kernels for 0% -> 6%
where the time goes in v1:
time: 328 us; the launch traced here: 326 us
  starting transfers between devices  89.8 us (27%)
  Pallas kernels  77.3 us (24%)
  local copies, waits for them, and re-layouts  52.3 us (16%)
  waiting for transfers between devices  51.5 us (16%)
  other arithmetic  37.4 us (11%)
  matrix products  16.1 us (5%)
    pallas_call x1, Pallas kernels, body(): pl.pallas_call(functools.partial(back_kernel, (hd, heads, cols, state)),...  31.9 us
    ppermute x27, starting transfers between devices, swap(): return lax.ppermute(block, axis, [(i, i ^ distance) for i in range(n)])  29.9 us
    pallas_call x1, Pallas kernels, body(): pl.pallas_call(functools.partial(front_kernel, (hd, heads, cols, state, n...  20.4 us
    ppermute x14, starting transfers between devices, ring_scatter(): b = lax.ppermute(b, 'shard', back)  15.6 us
    pallas_call x1, Pallas kernels, body(): pl.pallas_call(functools.partial(gate_kernel, (cols, n_seq, tuple((c for...  15.4 us
    ppermute x6, starting transfers between devices, ring_gather(): b = lax.ppermute(b, 'shard', back)  14.9 us
    ppermute x14, starting transfers between devices, ring_scatter(): a = lax.ppermute(a, 'shard', ahead)  14.6 us
    unnamed x136, local copies, waits for them, and re-layouts  14 us
  transfers between devices with their start and end apart: 73, of which 31 were waited for; matrix products, arithmetic and copies ran while one was open for 19% of the time, Pallas kernels for 6%

profile of v1, /device:TPU:0, one launch (start us, length us, event | category | flops | bytes accessed | tf_op | source)
XLA Modules:
  0.0 326.3 jit_solution(9061009035642609454)
XLA Ops:
  1.2 2.6 collective-permute-start.13
  6.9 3.1 collective-permute-start.15
  10.1 3.5 %collective-permute-start.4 = (bf16[128,1024]{1,0:T(8,128)(2,1)S(1)}, bf16[128,1024]{1,0:T(8,128)(2,1)S(1)}, u32[]{:S(2)}, u32[]{:S(2)}) collective-permute-start(bf16[128,1024]{1,0:T(8,128)(2,1)S(1)} %pad_maximum_fusion.refs_4_), channel_id=1, source_target_pairs={{0,2},{2,4},{4,6},{6,7},{7,5},{5,3},{3,1},{1,0},{8,10},{10,12},{12... | collective-permute-start | bytes 786440 | tf_op jit(solution)/shard_map/ppermute | solution.py:95
  16.0 5.5 %collective-permute-start.5 = (bf16[128,1024]{1,0:T(8,128)(2,1)S(1)}, bf16[128,1024]{1,0:T(8,128)(2,1)S(1)}, u32[]{:S(2)}, u32[]{:S(2)}) collective-permute-start(bf16[128,1024]{1,0:T(8,128)(2,1)S(1)} %pad_maximum_fusion.refs_4_), channel_id=1, source_target_pairs={{2,0},{4,2},{6,4},{7,6},{5,7},{3,5},{1,3},{0,1},{10,8},{12,10},{14... | collective-permute-start | bytes 786440 | tf_op jit(solution)/shard_map/ppermute | solution.py:96
  22.2 2.7 collective-permute-start.17
  24.9 2.4 collective-permute-done.5.refs_6_
  27.4 2.5 collective-permute-start.18
  29.8 3.2 collective-permute-done.17.refs_7_
  34.5 2.5 collective-permute-start.7
  39.1 3.4 %collective-permute-done.6.refs_7_ = bf16[128,1024]{1,0:T(8,128)(2,1)} collective-permute-done((bf16[128,1024]{1,0:T(8,128)(2,1)S(1)}, bf16[128,1024]{1,0:T(8,128)(2,1)}, u32[]{:S(2)}, u32[]{:S(2)}) %collective-permute-start.6) | collective-permute-done | bytes 262176 | tf_op jit(solution)/shard_map/ppermute | solution.py:95
  43.8 2.5 collective-permute-start.9
  59.9 3.1 collective-permute-done.21.refs_11_
  65.6 20.4 %front.1 = (bf16[1024,1024]{1,0:T(8,128)(2,1)}, bf16[1024,896]{1,0:T(8,128)(2,1)}, bf16[1024,768]{1,0:T(8,128)(2,1)}, f32[1024,768]{1,0:T(8,128)}, f32[1024,128]...) custom-call(s32[13]{0:T(128)} %stack.66.index, bf16[256,1024]{1,0:T(8,128)(2,1)} %bitcast.164, ...), custom_call_target="tpu_custom_call" | custom-call | flops 2415919104 | bytes 12582912 | tf_op jit(solution)/shard_map/front/pallas_call | solution.py:539
  86.9 15.4 %gate.1 = (bf16[1024,1024]{1,0:T(8,128)(2,1)}, bf16[1024,512]{1,0:T(8,128)(2,1)}, bf16[512,1024]{1,0:T(8,128)(2,1)}, f32[1024,512]{1,0:T(8,128)}, f32[1024,512]{...) custom-call(s32[13]{0:T(128)} %stack.66.index, bf16[256,1024]{1,0:T(8,128)(2,1)} %copy-done.11, ...), custom_call_target="tpu_custom_call" | custom-call | flops 2147483648 | bytes 14680064 | tf_op jit(solution)/shard_map/gate/pallas_call | solution.py:579
  109.4 9.6 %turn.1 = (bf16[1024,512]{1,0:T(8,128)(2,1)}, bf16[1024,512]{1,0:T(8,128)(2,1)}, f32[1024,512]{1,0:T(8,128)}, f32[1,512]{1,0:T(1,128)}) custom-call(f32[1024,512]{1,0:T(8,128)} %get-tuple-element.35.gate, f32[1024,512]{1,0:T(8,128)} %get-tuple-element.36.gated_in, f32[1024,512]{1,0:T(8,128)} %get-tuple-element.37.d_gated, ...), custom_call_target="tpu_custom_call" | custom-call | flops 15728640 | bytes 15728640 | tf_op jit(solution)/shard_map/turn/pallas_call | solution.py:613
  119.1 4.0 %fusion.84 = f32[1024,512]{1,0:T(8,128)} fusion(bf16[1024,1024]{1,0:T(8,128)(2,1)S(1)} %copy-done.9, bf16[1024,512]{1,0:T(8,128)(2,1)} %get-tuple-element.47), kind=kOutput, calls=%fused_computation.260 | convolution fusion | flops 1073741824 | bytes 5242880 | tf_op jit(solution)/shard_map/dot_general | solution.py:133
  126.3 4.6 %copy.36 = f32[4,2,128,2,256]{4,3,2,1,0:T(2,128)} copy(f32[4,2,128,2,256]{4,0,2,3,1:T(4,128)} %bitcast.157) | data formatting | bytes 4194304 | tf_op jit(solution)/shard_map/transpose | solution.py:634
  130.9 2.9 reshape.211
  133.8 31.9 %back.1 = (bf16[1024,896]{1,0:T(8,128)(2,1)}, f32[8,768]{1,0:T(8,128)}, f32[8,128]{1,0:T(8,128)}) custom-call(bf16[1024,768]{1,0:T(8,128)(2,1)} %get-tuple-element.41.refs_0_, f32[1024,768]{1,0:T(8,128)} %get-tuple-element.33.refs_14_.conv_out.refs_1_, f32[1024,128]{1,0:T(8,128)} %get-tuple-element.42.refs_2_, ...), custom_call_target="tpu_custom_call" | custom-call | flops 1342177280 | bytes 14680064 | tf_op jit(solution)/shard_map/back/pallas_call | solution.py:643
  165.8 4.7 %fusion.86 = f32[1024,896]{1,0:T(8,128)S(1)} fusion(bf16[1024,1024]{1,0:T(8,128)(2,1)} %get-tuple-element.32.refs_13_, bf16[1024,896]{1,0:T(8,128)(2,1)} %get-tuple-element.45), kind=kOutput, calls=%fused_computation.262 | convolution fusion | flops 1879048192 | bytes 7602176 | tf_op jit(solution)/shard_map/dot_general | solution.py:133
  175.6 2.8 dynamic-slice_bitcast_fusion.13
  189.3 2.5 fusion.82
  200.5 3.4 %collective-permute-done.45 = bf16[128,384]{1,0:T(8,128)(2,1)S(1)} collective-permute-done((bf16[128,384]{1,0:T(8,128)(2,1)S(1)}, bf16[128,384]{1,0:T(8,128)(2,1)S(1)}, u32[]{:S(2)}, u32[]{:S(2)}) %collective-permute-start.45) | collective-permute-done | bytes 98336 | tf_op jit(solution)/shard_map/ppermute | solution.py:117
  203.9 2.9 collective-permute-start.31
  249.9 4.0 %collective-permute-done.49 = bf16[128,384]{1,0:T(8,128)(2,1)S(1)} collective-permute-done((bf16[128,384]{1,0:T(8,128)(2,1)S(1)}, bf16[128,384]{1,0:T(8,128)(2,1)S(1)}, u32[]{:S(2)}, u32[]{:S(2)}) %collective-permute-start.49) | collective-permute-done | bytes 98336 | tf_op jit(solution)/shard_map/ppermute | solution.py:117
  257.7 2.5 collective-permute-done.65
  290.5 7.0 %collective-permute-start.70 = (bf16[256,256]{1,0:T(8,128)(2,1)S(1)}, bf16[256,256]{1,0:T(8,128)(2,1)S(1)}, u32[]{:S(2)}, u32[]{:S(2)}) collective-permute-start(bf16[256,256]{1,0:T(8,128)(2,1)S(1)} %collective-permute-done.69), channel_id=1, source_target_pairs={{0,16},{8,24},{16,0},{24,8},{1,17},{9,25},{17,1},{25,9},{2,18},{10... | collective-permute-start | bytes 393224 | tf_op jit(solution)/shard_map/ppermute | solution.py:25
  302.5 2.5 collective-permute-start.26
  311.5 3.6 %concatenate.46 = f32[128,4384]{1,0:T(8,128)} concatenate(f32[128,512]{1,0:T(8,128)} %get-tuple-element.122, f32[128,512]{1,0:T(8,128)} %get-tuple-element.120, f32[128,512]{1,0:T(8,128)} %get-tuple-element.121, f32[128,512]{1,0:T(8,128)} %get-tuple-element.119, f32[128,512]{1,0:T(8,128)S(1)} %slice_convert_fusion.3, f32[128,512]{1,0:T(8,128)} %slice_convert_fusion.2, ...), dimensions={1} | concatenate | bytes 4489216 | tf_op jit(solution)/shard_map/concatenate | solution.py:711
  315.1 3.0 copy.37
  319.9 3.2 collective-permute-done.26
  323.1 3.2 fusion.3
  (393 shorter events, 153.2 us)
Async XLA Ops:
  0.7 36.4 %collective-permute-start.12 = (bf16[256,1024]{1,0:T(8,128)(2,1)}, bf16[256,1024]{1,0:T(8,128)(2,1)}, u32[]{:S(2)}, u32[]{:S(2)}) collective-permute-start(bf16[256,1024]{1,0:T(8,128)(2,1)} %bitcast.162), channel_id=1, source_target_pairs={{0,8},{8,0},{16,24},{24,16},{1,9},{9,1},{17,25},{25,17},{2,10},{10... | collective-permute-start | bytes 1572872 | tf_op jit(solution)/shard_map/ppermute | solution.py:25
  1.2 35.8 %collective-permute-start.13 = (bf16[256,1024]{1,0:T(8,128)(2,1)}, bf16[256,1024]{1,0:T(8,128)(2,1)}, u32[]{:S(2)}, u32[]{:S(2)}) collective-permute-start(bf16[256,1024]{1,0:T(8,128)(2,1)} %bitcast.163), channel_id=1, source_target_pairs={{0,16},{8,24},{16,0},{24,8},{1,17},{9,25},{17,1},{25,9},{2,18},{10... | collective-permute-start | bytes 1572872 | tf_op jit(solution)/shard_map/ppermute | solution.py:25
  10.0 11.6 %collective-permute-start.16 = (bf16[128,896]{1,0:T(8,128)(2,1)S(1)}, bf16[128,896]{1,0:T(8,128)(2,1)}, u32[]{:S(2)}, u32[]{:S(2)}) collective-permute-start(bf16[128,896]{1,0:T(8,128)(2,1)S(1)} %fusion.65.refs_4_), channel_id=1, source_target_pairs={{2,0},{4,2},{6,4},{7,6},{5,7},{3,5},{1,3},{0,1},{10,8},{12,10},{14... | collective-permute-start | bytes 688136 | tf_op jit(solution)/shard_map/ppermute | solution.py:96
  10.1 12.1 %collective-permute-start.4 = (bf16[128,1024]{1,0:T(8,128)(2,1)S(1)}, bf16[128,1024]{1,0:T(8,128)(2,1)S(1)}, u32[]{:S(2)}, u32[]{:S(2)}) collective-permute-start(bf16[128,1024]{1,0:T(8,128)(2,1)S(1)} %pad_maximum_fusion.refs_4_), channel_id=1, source_target_pairs={{0,2},{2,4},{4,6},{6,7},{7,5},{5,3},{3,1},{1,0},{8,10},{10,12},{12... | collective-permute-start | bytes 786440 | tf_op jit(solution)/shard_map/ppermute | solution.py:95
  16.0 11.4 %collective-permute-start.5 = (bf16[128,1024]{1,0:T(8,128)(2,1)S(1)}, bf16[128,1024]{1,0:T(8,128)(2,1)S(1)}, u32[]{:S(2)}, u32[]{:S(2)}) collective-permute-start(bf16[128,1024]{1,0:T(8,128)(2,1)S(1)} %pad_maximum_fusion.refs_4_), channel_id=1, source_target_pairs={{2,0},{4,2},{6,4},{7,6},{5,7},{3,5},{1,3},{0,1},{10,8},{12,10},{14... | collective-permute-start | bytes 786440 | tf_op jit(solution)/shard_map/ppermute | solution.py:96
  21.5 17.5 %collective-permute-start.1 = (bf16[256,1024]{1,0:T(8,128)(2,1)S(1)}, bf16[256,1024]{1,0:T(8,128)(2,1)S(1)}, u32[]{:S(2)}, u32[]{:S(2)}) collective-permute-start(bf16[256,1024]{1,0:T(8,128)(2,1)S(1)} %convert_bitcast_fusion.refs_0_), channel_id=1, source_target_pairs={{0,16},{8,24},{16,0},{24,8},{1,17},{9,25},{17,1},{25,9},{2,18},{10... | collective-permute-start | bytes 1572872 | tf_op jit(solution)/shard_map/ppermute | solution.py:25
  22.2 10.9 %collective-permute-start.17 = (bf16[128,896]{1,0:T(8,128)(2,1)S(1)}, bf16[128,896]{1,0:T(8,128)(2,1)}, u32[]{:S(2)}, u32[]{:S(2)}) collective-permute-start(bf16[128,896]{1,0:T(8,128)(2,1)S(1)} %collective-permute-done.15.refs_5_), channel_id=1, source_target_pairs={{0,2},{2,4},{4,6},{6,7},{7,5},{5,3},{3,1},{1,0},{8,10},{10,12},{12... | collective-permute-start | bytes 688136 | tf_op jit(solution)/shard_map/ppermute | solution.py:95
  37.0 10.4 %collective-permute-start.19 = (bf16[128,896]{1,0:T(8,128)(2,1)}, bf16[128,896]{1,0:T(8,128)(2,1)}, u32[]{:S(2)}, u32[]{:S(2)}) collective-permute-start(bf16[128,896]{1,0:T(8,128)(2,1)} %collective-permute-done.17.refs_7_), channel_id=1, source_target_pairs={{0,2},{2,4},{4,6},{6,7},{7,5},{5,3},{3,1},{1,0},{8,10},{10,12},{12... | collective-permute-start | bytes 688136 | tf_op jit(solution)/shard_map/ppermute | solution.py:95
  37.0 11.7 %collective-permute-start.20 = (bf16[128,896]{1,0:T(8,128)(2,1)}, bf16[128,896]{1,0:T(8,128)(2,1)}, u32[]{:S(2)}, u32[]{:S(2)}) collective-permute-start(bf16[128,896]{1,0:T(8,128)(2,1)} %collective-permute-done.18.refs_8_), channel_id=1, source_target_pairs={{2,0},{4,2},{6,4},{7,6},{5,7},{3,5},{1,3},{0,1},{10,8},{12,10},{14... | collective-permute-start | bytes 688136 | tf_op jit(solution)/shard_map/ppermute | solution.py:96
  39.1 26.6 %collective-permute-start.14 = (bf16[256,1024]{1,0:T(8,128)(2,1)}, bf16[256,1024]{1,0:T(8,128)(2,1)}, u32[]{:S(2)}, u32[]{:S(2)}) collective-permute-start(bf16[256,1024]{1,0:T(8,128)(2,1)} %collective-permute-done.13.refs_2_), channel_id=1, source_target_pairs={{0,8},{8,0},{16,24},{24,16},{1,9},{9,1},{17,25},{25,17},{2,10},{10... | collective-permute-start | bytes 1572872 | tf_op jit(solution)/shard_map/ppermute | solution.py:25
  43.8 14.2 %collective-permute-start.9 = (bf16[128,1024]{1,0:T(8,128)(2,1)}, bf16[128,1024]{1,0:T(8,128)(2,1)S(1)}, u32[]{:S(2)}, u32[]{:S(2)}) collective-permute-start(bf16[128,1024]{1,0:T(8,128)(2,1)} %collective-permute-done.7.refs_8_), channel_id=1, source_target_pairs={{2,0},{4,2},{6,4},{7,6},{5,7},{3,5},{1,3},{0,1},{10,8},{12,10},{14... | collective-permute-start | bytes 786440 | tf_op jit(solution)/shard_map/ppermute | solution.py:96
  47.4 38.7 %collective-permute-start = (bf16[256,1024]{1,0:T(8,128)(2,1)S(1)}, bf16[256,1024]{1,0:T(8,128)(2,1)S(1)}, u32[]{:S(2)}, u32[]{:S(2)}) collective-permute-start(bf16[256,1024]{1,0:T(8,128)(2,1)S(1)} %convert_bitcast_fusion.refs_0_), channel_id=1, source_target_pairs={{0,8},{8,0},{16,24},{24,16},{1,9},{9,1},{17,25},{25,17},{2,10},{10... | collective-permute-start | bytes 1572872 | tf_op jit(solution)/shard_map/ppermute | solution.py:25
  48.7 37.4 %collective-permute-start.2 = (bf16[256,1024]{1,0:T(8,128)(2,1)S(1)}, bf16[256,1024]{1,0:T(8,128)(2,1)}, u32[]{:S(2)}, u32[]{:S(2)}) collective-permute-start(bf16[256,1024]{1,0:T(8,128)(2,1)S(1)} %collective-permute-done.1.refs_2_), channel_id=1, source_target_pairs={{0,8},{8,0},{16,24},{24,16},{1,9},{9,1},{17,25},{25,17},{2,10},{10... | collective-permute-start | bytes 1572872 | tf_op jit(solution)/shard_map/ppermute | solution.py:25
  51.4 12.5 %collective-permute-start.22 = (bf16[128,512]{1,0:T(8,128)(2,1)}, bf16[128,512]{1,0:T(8,128)(2,1)}, u32[]{:S(2)}, u32[]{:S(2)}) collective-permute-start(bf16[128,512]{1,0:T(8,128)(2,1)} %slice.381), channel_id=1, source_target_pairs={{2,0},{4,2},{6,4},{7,6},{5,7},{3,5},{1,3},{0,1},{10,8},{12,10},{14... | collective-permute-start | bytes 393224 | tf_op jit(solution)/shard_map/ppermute | solution.py:101
  63.6 22.5 %collective-permute-start.10 = (bf16[128,512]{1,0:T(8,128)(2,1)}, bf16[128,512]{1,0:T(8,128)(2,1)S(1)}, u32[]{:S(2)}, u32[]{:S(2)}) collective-permute-start(bf16[128,512]{1,0:T(8,128)(2,1)} %slice.378), channel_id=1, source_target_pairs={{0,2},{2,4},{4,6},{6,7},{7,5},{5,3},{3,1},{1,0},{8,10},{10,12},{12... | collective-permute-start | bytes 393224 | tf_op jit(solution)/shard_map/ppermute | solution.py:100
  63.9 22.2 %collective-permute-start.11 = (bf16[128,512]{1,0:T(8,128)(2,1)}, bf16[128,512]{1,0:T(8,128)(2,1)}, u32[]{:S(2)}, u32[]{:S(2)}) collective-permute-start(bf16[128,512]{1,0:T(8,128)(2,1)} %slice.379), channel_id=1, source_target_pairs={{2,0},{4,2},{6,4},{7,6},{5,7},{3,5},{1,3},{0,1},{10,8},{12,10},{14... | collective-permute-start | bytes 393224 | tf_op jit(solution)/shard_map/ppermute | solution.py:101
  188.6 95.6 %collective-permute-start.27 = (bf16[2,256,1024]{2,1,0:T(8,128)(2,1)}, bf16[2,256,1024]{2,1,0:T(8,128)(2,1)}, u32[]{:S(2)}, u32[]{:S(2)}) collective-permute-start(bf16[2,256,1024]{2,1,0:T(8,128)(2,1)} %fusion.7), channel_id=1, source_target_pairs={{0,8},{8,0},{16,24},{24,16},{1,9},{9,1},{17,25},{25,17},{2,10},{10... | collective-permute-start | bytes 3145736 | tf_op jit(solution)/shard_map/ppermute | solution.py:25
  195.8 90.2 %collective-permute-start.25 = (bf16[2,256,1024]{2,1,0:T(8,128)(2,1)}, bf16[2,256,1024]{2,1,0:T(8,128)(2,1)}, u32[]{:S(2)}, u32[]{:S(2)}) collective-permute-start(bf16[2,256,1024]{2,1,0:T(8,128)(2,1)} %fusion.6), channel_id=1, source_target_pairs={{0,8},{8,0},{16,24},{24,16},{1,9},{9,1},{17,25},{25,17},{2,10},{10... | collective-permute-start | bytes 3145736 | tf_op jit(solution)/shard_map/ppermute | solution.py:25
  195.8 13.8 %collective-permute-start.35 = (bf16[128,512]{1,0:T(8,128)(2,1)S(1)}, bf16[128,512]{1,0:T(8,128)(2,1)S(1)}, u32[]{:S(2)}, u32[]{:S(2)}) collective-permute-start(bf16[128,512]{1,0:T(8,128)(2,1)S(1)} %slice.386), channel_id=1, source_target_pairs={{0,2},{2,4},{4,6},{6,7},{7,5},{5,3},{3,1},{1,0},{8,10},{10,12},{12... | collective-permute-start | bytes 393224 | tf_op jit(solution)/shard_map/ppermute | solution.py:117
  196.0 14.9 %collective-permute-start.52 = (bf16[128,512]{1,0:T(8,128)(2,1)S(1)}, bf16[128,512]{1,0:T(8,128)(2,1)S(1)}, u32[]{:S(2)}, u32[]{:S(2)}) collective-permute-start(bf16[128,512]{1,0:T(8,128)(2,1)S(1)} %slice.402), channel_id=1, source_target_pairs={{2,0},{4,2},{6,4},{7,6},{5,7},{3,5},{1,3},{0,1},{10,8},{12,10},{14... | collective-permute-start | bytes 393224 | tf_op jit(solution)/shard_map/ppermute | solution.py:118
  209.6 22.2 %collective-permute-start.46 = (bf16[128,384]{1,0:T(8,128)(2,1)}, bf16[128,384]{1,0:T(8,128)(2,1)}, u32[]{:S(2)}, u32[]{:S(2)}) collective-permute-start(bf16[128,384]{1,0:T(8,128)(2,1)} %fusion.74), channel_id=1, source_target_pairs={{0,2},{2,4},{4,6},{6,7},{7,5},{5,3},{3,1},{1,0},{8,10},{10,12},{12... | collective-permute-start | bytes 294920 | tf_op jit(solution)/shard_map/ppermute | solution.py:117
  215.6 18.0 %collective-permute-start.36 = (bf16[128,512]{1,0:T(8,128)(2,1)S(1)}, bf16[128,512]{1,0:T(8,128)(2,1)}, u32[]{:S(2)}, u32[]{:S(2)}) collective-permute-start(bf16[128,512]{1,0:T(8,128)(2,1)S(1)} %fusion.61), channel_id=1, source_target_pairs={{0,2},{2,4},{4,6},{6,7},{7,5},{5,3},{3,1},{1,0},{8,10},{10,12},{12... | collective-permute-start | bytes 393224 | tf_op jit(solution)/shard_map/ppermute | solution.py:117
  217.1 18.7 %collective-permute-start.53 = (bf16[128,512]{1,0:T(8,128)(2,1)S(1)}, bf16[128,512]{1,0:T(8,128)(2,1)}, u32[]{:S(2)}, u32[]{:S(2)}) collective-permute-start(bf16[128,512]{1,0:T(8,128)(2,1)S(1)} %fusion.54), channel_id=1, source_target_pairs={{2,0},{4,2},{6,4},{7,6},{5,7},{3,5},{1,3},{0,1},{10,8},{12,10},{14... | collective-permute-start | bytes 393224 | tf_op jit(solution)/shard_map/ppermute | solution.py:118
  244.7 11.4 %collective-permute-start.38 = (bf16[128,512]{1,0:T(8,128)(2,1)S(1)}, bf16[128,512]{1,0:T(8,128)(2,1)S(1)}, u32[]{:S(2)}, u32[]{:S(2)}) collective-permute-start(bf16[128,512]{1,0:T(8,128)(2,1)S(1)} %fusion.59), channel_id=1, source_target_pairs={{0,2},{2,4},{4,6},{6,7},{7,5},{5,3},{3,1},{1,0},{8,10},{10,12},{12... | collective-permute-start | bytes 393224 | tf_op jit(solution)/shard_map/ppermute | solution.py:117
  278.0 10.4 %collective-permute-start.42 = (bf16[128,512]{1,0:T(8,128)(2,1)S(1)}, bf16[128,512]{1,0:T(8,128)(2,1)S(1)}, u32[]{:S(2)}, u32[]{:S(2)}) collective-permute-start(bf16[128,512]{1,0:T(8,128)(2,1)S(1)} %fusion.55), channel_id=1, source_target_pairs={{0,16},{8,24},{16,0},{24,8},{1,17},{9,25},{17,1},{25,9},{2,18},{10... | collective-permute-start | bytes 393224 | tf_op jit(solution)/shard_map/ppermute | solution.py:25
  280.4 18.9 %collective-permute-start.44 = (bf16[128,512]{1,0:T(8,128)(2,1)S(1)}, bf16[128,512]{1,0:T(8,128)(2,1)S(1)}, u32[]{:S(2)}, u32[]{:S(2)}) collective-permute-start(bf16[128,512]{1,0:T(8,128)(2,1)S(1)} %fusion.55), channel_id=1, source_target_pairs={{0,8},{8,0},{16,24},{24,16},{1,9},{9,1},{17,25},{25,17},{2,10},{10... | collective-permute-start | bytes 393224 | tf_op jit(solution)/shard_map/ppermute | solution.py:25
  282.1 20.4 %collective-permute-start.59 = (bf16[128,896]{1,0:T(8,128)(2,1)S(1)}, bf16[128,896]{1,0:T(8,128)(2,1)S(1)}, u32[]{:S(2)}, u32[]{:S(2)}) collective-permute-start(bf16[128,896]{1,0:T(8,128)(2,1)S(1)} %pad_maximum_fusion.1), channel_id=1, source_target_pairs={{0,16},{8,24},{16,0},{24,8},{1,17},{9,25},{17,1},{25,9},{2,18},{10... | collective-permute-start | bytes 688136 | tf_op jit(solution)/shard_map/ppermute | solution.py:25
  284.2 22.2 %collective-permute-start.61 = (bf16[128,896]{1,0:T(8,128)(2,1)S(1)}, bf16[128,896]{1,0:T(8,128)(2,1)S(1)}, u32[]{:S(2)}, u32[]{:S(2)}) collective-permute-start(bf16[128,896]{1,0:T(8,128)(2,1)S(1)} %pad_maximum_fusion.1), channel_id=1, source_target_pairs={{0,8},{8,0},{16,24},{24,16},{1,9},{9,1},{17,25},{25,17},{2,10},{10... | collective-permute-start | bytes 688136 | tf_op jit(solution)/shard_map/ppermute | solution.py:25
  288.4 10.9 %collective-permute-start.43 = (bf16[128,512]{1,0:T(8,128)(2,1)S(1)}, bf16[128,512]{1,0:T(8,128)(2,1)S(1)}, u32[]{:S(2)}, u32[]{:S(2)}) collective-permute-start(bf16[128,512]{1,0:T(8,128)(2,1)S(1)} %collective-permute-done.42), channel_id=1, source_target_pairs={{0,8},{8,0},{16,24},{24,16},{1,9},{9,1},{17,25},{25,17},{2,10},{10... | collective-permute-start | bytes 393224 | tf_op jit(solution)/shard_map/ppermute | solution.py:25
  290.5 10.9 %collective-permute-start.70 = (bf16[256,256]{1,0:T(8,128)(2,1)S(1)}, bf16[256,256]{1,0:T(8,128)(2,1)S(1)}, u32[]{:S(2)}, u32[]{:S(2)}) collective-permute-start(bf16[256,256]{1,0:T(8,128)(2,1)S(1)} %collective-permute-done.69), channel_id=1, source_target_pairs={{0,16},{8,24},{16,0},{24,8},{1,17},{9,25},{17,1},{25,9},{2,18},{10... | collective-permute-start | bytes 393224 | tf_op jit(solution)/shard_map/ppermute | solution.py:25
  299.3 18.8 %collective-permute-start.28 = (bf16[1,256,1024]{2,1,0:T(8,128)(2,1)}, bf16[1,256,1024]{2,1,0:T(8,128)(2,1)}, u32[]{:S(2)}, u32[]{:S(2)}) collective-permute-start(bf16[1,256,1024]{2,1,0:T(8,128)(2,1)} %dynamic-slice_convert_fusion), channel_id=1, source_target_pairs={{0,16},{8,24},{16,0},{24,8},{1,17},{9,25},{17,1},{25,9},{2,18},{10... | collective-permute-start | bytes 1572872 | tf_op jit(solution)/shard_map/ppermute | solution.py:25
  302.5 20.6 %collective-permute-start.26 = (bf16[1,256,1024]{2,1,0:T(8,128)(2,1)}, bf16[1,256,1024]{2,1,0:T(8,128)(2,1)}, u32[]{:S(2)}, u32[]{:S(2)}) collective-permute-start(bf16[1,256,1024]{2,1,0:T(8,128)(2,1)} %dynamic-slice_convert_fusion.1), channel_id=1, source_target_pairs={{0,16},{8,24},{16,0},{24,8},{1,17},{9,25},{17,1},{25,9},{2,18},{10... | collective-permute-start | bytes 1572872 | tf_op jit(solution)/shard_map/ppermute | solution.py:25
  (107 other events, 1472.3 us)

commit v2 on v1

v2 whole, which is shorter than its diff:
```python
import functools

import jax
import jax.numpy as jnp
from jax import lax
from jax.experimental import pallas as pl
from jax.experimental.pallas import tpu as pltpu
from jax.sharding import PartitionSpec as P


bf16 = jnp.bfloat16
f32 = jnp.float32
norm_eps = 1e-05
LANES = 128
CHUNK = 128
HALO = 8
FRONT_PIECES = 4
BACK_PIECES = 2

VMEM = pl.BlockSpec(memory_space=pltpu.VMEM)
SMEM = pl.BlockSpec(memory_space=pltpu.SMEM)
ANY = pl.BlockSpec(memory_space=pl.ANY)


def swap(block, axis, distance):
    n = lax.axis_size(axis)
    return lax.ppermute(block, axis, [(i, i ^ distance) for i in range(n)])


def seq_gather(block):
    n = lax.axis_size("seq")
    blocks = {0: block}
    d = n // 2
    while d >= 1:
        for o in list(blocks):
            blocks[o ^ d] = swap(blocks[o], "seq", d)
        d //= 2
    return [blocks[o] for o in range(n)]


def seq_scatter(parts):
    n = lax.axis_size("seq")
    me = lax.axis_index("seq")
    d = 1
    while d < n:
        m = parts.shape[0]
        pairs = parts.reshape((m // 2, 2) + parts.shape[1:])
        bit = (me // d) % 2
        keep = lax.dynamic_index_in_dim(pairs, bit, 1, keepdims=False)
        send = lax.dynamic_index_in_dim(pairs, 1 - bit, 1, keepdims=False)
        got = swap(send.astype(bf16), "seq", d)
        parts = keep.astype(f32) + got.astype(f32)
        d *= 2
    return parts[0]


def all_sum(block, axis):
    n = lax.axis_size(axis)
    d = 1
    while d < n:
        got = swap(block, axis, d)
        block = block + got
        d *= 2
    return block


def ring_index(place, n):
    place = lax.rem(place + 2 * n, n)
    return jnp.where(place < n // 2, 2 * place, 2 * (n - place) - 1)


def ring_place(shard, n):
    return jnp.where(shard % 2 == 0, shard // 2, n - (shard + 1) // 2)


def ring_routes(n):
    order = list(range(0, n, 2)) + list(range(n - 1, 0, -2))
    ahead = [(order[p], order[(p + 1) % n]) for p in range(n)]
    return ahead, [(b, a) for a, b in ahead]


class RingGather:
    def __init__(self, block, cut):
        n = lax.axis_size("shard")
        self.n, self.cut, self.hop = n, cut, 0
        self.ahead, self.back = ring_routes(n)
        self.place = ring_place(lax.axis_index("shard"), n)
        self.a = self.b = block
        self.found = [(block, lax.axis_index("shard"), 0)]

    def step(self):
        if self.hop == self.n // 2:
            return []
        self.hop += 1
        k, n = self.hop, self.n
        if k == n // 2:
            self.a = lax.ppermute(self.a[:, : self.cut], "shard", self.ahead)
            self.b = lax.ppermute(self.b[:, self.cut :], "shard", self.back)
            owner = ring_index(self.place - k, n)
            self.found += [(self.a, owner, 0), (self.b, owner, self.cut)]
        else:
            self.a = lax.ppermute(self.a, "shard", self.ahead)
            self.b = lax.ppermute(self.b, "shard", self.back)
            self.found.append((self.a, ring_index(self.place - k, n), 0))
            self.found.append((self.b, ring_index(self.place + k, n), 0))
        return [self.a, self.b]


def bit_orders(n):
    bits = list(range(n.bit_length() - 1))
    return bits, [bits[1], bits[0]] + bits[2:]


def slot(owner, bits):
    place = 0
    for b in bits:
        place = 2 * place + ((owner >> b) & 1)
    return place


class Halving:
    def __init__(self, slabs):
        self.slabs = list(slabs)
        self.orders = bit_orders(lax.axis_size("shard"))
        self.hop = 0

    def step(self):
        if self.hop == len(self.orders[0]):
            return []
        me = lax.axis_index("shard")
        for i, slab in enumerate(self.slabs):
            b = self.orders[i][self.hop]
            pair = slab.reshape((2, slab.shape[0] // 2) + slab.shape[1:])
            bit = (me >> b) & 1
            keep = lax.dynamic_index_in_dim(pair, bit, 0, keepdims=False)
            send = lax.dynamic_index_in_dim(pair, 1 - bit, 0, keepdims=False)
            got = swap(send, "shard", 1 << b)
            self.slabs[i] = (keep.astype(f32) + got.astype(f32)).astype(bf16)
        self.hop += 1
        return self.slabs

    def finish(self):
        while self.step():
            pass
        return [s[0] for s in self.slabs]


def sigmoid(v):
    return 1.0 / (1.0 + jnp.exp(-v))


def softplus(v):
    return jnp.maximum(v, 0.0) + jnp.log1p(jnp.exp(-jnp.abs(v)))


def dot(left, right, l, r, precision=None):
    return lax.dot_general(
        left, right, (((l,), (r,)), ((), ())), preferred_element_type=f32, precision=precision
    )


def exact(left, right, l, r):
    total = None
    whole, ones = (right, left) if left.dtype == bf16 else (left, right)
    for _ in range(3):
        piece = whole.astype(bf16)
        whole = whole - piece.astype(f32)
        pair = (ones, piece) if left.dtype == bf16 else (piece, ones)
        term = dot(*pair, l, r)
        total = term if total is None else total + term
    return total


def spread(per_head, hd, cols):
    rows = per_head.shape[0]
    lane = lax.broadcasted_iota(jnp.int32, (rows, LANES), 1)
    tiles = []
    per = LANES // hd
    for j in range(cols // LANES):
        tile = jnp.broadcast_to(per_head[:, j * per : j * per + 1], (rows, LANES))
        for i in range(1, per):
            h = j * per + i
            tile = jnp.where(
                lane >= i * hd, jnp.broadcast_to(per_head[:, h : h + 1], (rows, LANES)), tile
            )
        tiles.append(tile)
    return jnp.concatenate(tiles, axis=1) if len(tiles) > 1 else tiles[0]


def decay_rows(cum_t, hd, heads, state):
    last = cum_t.shape[1] - 1
    return jnp.concatenate(
        [
            jnp.broadcast_to(jnp.exp(cum_t[h : h + 1, last : last + 1]), (hd, state))
            for h in range(heads)
        ],
        axis=0,
    )


def assemble(copies, sems):
    handles = []
    for i, (src, dst, owner, col) in enumerate(copies):
        rows, cols = src.shape
        place = pl.multiple_of(owner * rows, rows)
        handle = pltpu.make_async_copy(
            src, dst.at[pl.ds(place, rows), col : col + cols], sems.at[i]
        )
        handle.start()
        handles.append(handle)
    for handle in handles:
        handle.wait()


def ring_owners(shard, n, cut):
    place = ring_place(shard, n)
    found = [(shard, 0)]
    for k in range(1, n // 2):
        found.append((ring_index(place - k, n), 0))
        found.append((ring_index(place + k, n), 0))
    last = ring_index(place - n // 2, n)
    return found + [(last, 0), (last, cut)]


def own_heads(table, me, heads):
    return pltpu.roll(table[...], lax.rem(LANES - me * heads, LANES), 1)


def own_columns(ref, me, cols, inner):
    mine = ref[:, pl.ds(pl.multiple_of(me * cols, LANES), cols)]
    if inner == ref.shape[1]:
        return mine
    return jnp.concatenate([mine, ref[:, inner:]], axis=1)


def decays(dt_raw, dt_bias, a_log):
    rows = dt_raw.shape[0]
    row = lax.broadcasted_iota(jnp.int32, (rows, rows), 0)
    col = lax.broadcasted_iota(jnp.int32, (rows, rows), 1)
    lower = jnp.where(row >= col, 1.0, 0.0).astype(bf16)
    step = softplus(dt_raw + dt_bias)
    log_decay = -step * jnp.exp(a_log)
    cum = exact(lower, log_decay, 1, 0)
    cum_t = jnp.transpose(cum)
    return step, log_decay, cum, cum_t


def front_kernel(dims, ids, *refs):
    hd, heads, cols, state, inner, n_seq, n_shard, w_cut, n_skip = dims
    conv_cols = cols + 2 * state
    me = ids[0]
    step = pl.program_id(0)
    if n_skip is None:
        n_w = n_shard + 1
        tok_refs = refs[:n_seq]
        w_refs = refs[n_seq : n_seq + n_w]
        gain, conv_w_all, conv_b_all, table = refs[n_seq + n_w : n_seq + n_w + 4]
        tokens_all, w_all = refs[n_seq + n_w + 4 : n_seq + n_w + 6]
        normed, conv_in, conv_out, dt_raw, scan_out, states, held, halo = refs[-10:-2]
        sems, projected = refs[-2:]

        @pl.when(step == 0)
        def _():
            owners = ring_owners(ids[1], n_shard, w_cut)
            assemble(
                [(r, tokens_all, me ^ o, 0) for o, r in enumerate(tok_refs)]
                + [(r, w_all, o, c) for r, (o, c) in zip(w_refs, owners)],
                sems,
            )
            held[...] = jnp.zeros_like(held)
            halo[...] = jnp.zeros_like(halo)

        size = normed.shape[0]
        tok = tokens_all[pl.ds(pl.multiple_of(step * size, size), size), :].astype(f32)
    else:
        tokens, w_all, gain, conv_w_all, conv_b_all, table, held_in, halo_in = refs[:8]
        normed, conv_in, conv_out, dt_raw, scan_out, states, held, halo, projected = refs[
            8 + n_skip :
        ]

        @pl.when(step == 0)
        def _():
            held[...] = held_in[...]
            halo[...] = halo_in[...]

        tok = tokens[...].astype(f32)
    conv_w = own_columns(conv_w_all, me, cols, inner)
    conv_b = own_columns(conv_b_all, me, cols, inner)
    by_head = own_heads(table, me, heads)
    dt_bias, a_log = by_head[0:1, :], by_head[1:2, :]
    width = conv_w.shape[0]
    row = lax.broadcasted_iota(jnp.int32, (CHUNK, CHUNK), 0)
    col = lax.broadcasted_iota(jnp.int32, (CHUNK, CHUNK), 1)
    mask = row >= col
    per = LANES // hd

    rstat = lax.rsqrt(jnp.mean(tok * tok, axis=1, keepdims=True) + norm_eps)
    nrm = (tok * rstat * gain[...]).astype(bf16)
    normed[...] = nrm
    projected[...] = dot(nrm, w_all[...], 1, 0)

    @pl.loop(0, normed.shape[0] // CHUNK)
    def _(c):
        at = pl.ds(pl.multiple_of(c * CHUNK, CHUNK), CHUNK)
        proj = projected[at, :]
        narrow = proj[:, :conv_cols].astype(bf16)
        conv_in[at, :] = narrow
        wide = narrow.astype(f32)
        both = jnp.concatenate([halo[...], wide], axis=0)
        halo[...] = wide[CHUNK - HALO :, :]
        first = HALO - (width - 1)
        v = conv_b + conv_w[0:1, :] * both[first : first + CHUNK, :]
        for k in range(1, width):
            v = v + conv_w[k : k + 1, :] * both[first + k : first + k + CHUNK, :]
        conv_out[at, :] = v
        active = v * sigmoid(v)
        raw = proj[:, conv_cols:]
        dt_raw[at, :] = raw
        step, _, cum, cum_t = decays(raw, dt_bias, a_log)
        xd = active[:, :cols] * spread(step, hd, cols)
        xd_b = xd.astype(bf16)
        b_b = active[:, cols : cols + state].astype(bf16)
        c_b = active[:, cols + state :].astype(bf16)
        cross = dot(c_b, b_b, 1, 1)
        before = held[...]
        before_b = before.astype(bf16)
        states[c] = before_b
        tiles = []
        for j in range(cols // LANES):
            tile = None
            for i in range(per):
                h = j * per + i
                gap = cum[:, h : h + 1] - cum_t[h : h + 1, :]
                kern = (jnp.exp(jnp.where(mask, gap, -1e30)) * cross).astype(bf16)
                out = dot(kern, xd_b[:, j * LANES : (j + 1) * LANES], 1, 0)
                tile = out if tile is None else jnp.where(col >= i * hd, out, tile)
            tiles.append(tile)
        intra = jnp.concatenate(tiles, axis=1) if len(tiles) > 1 else tiles[0]
        inter = spread(jnp.exp(cum), hd, cols) * dot(c_b, before_b, 1, 1)
        scan_out[at, :] = intra + inter
        tail = jnp.exp(cum[CHUNK - 1 : CHUNK, :] - cum)
        xt = (xd * spread(tail, hd, cols)).astype(bf16)
        held[...] = decay_rows(cum_t, hd, heads, state) * before + dot(xt, b_b, 0, 0)


def gate_kernel(dims, ids, *refs):
    cols, heads, hd, n_seq, n_shard = dims
    n_w = n_shard + 1
    me = ids[0]
    cot_refs = refs[:n_seq]
    w_refs = refs[n_seq : n_seq + n_w]
    normed, conv_out, scan_out, table, gain_all = refs[n_seq + n_w : n_seq + n_w + 5]
    cotan, wz, wo, gate, mixed_out, d_gated, sums, sems = refs[n_seq + n_w + 5 :]
    step = pl.program_id(0)

    @pl.when(step == 0)
    def _():
        copies = [(r, cotan, me ^ o) for o, r in enumerate(cot_refs)]
        assemble_two(copies, w_refs, ring_owners(ids[1], n_shard, cols), wz, wo, sems)

    skip = spread(own_heads(table, me, heads), hd, cols)[2:3, :]
    gain = own_columns(gain_all, me, cols, gain_all.shape[1])
    size = normed.shape[0]
    lane = lax.broadcasted_iota(jnp.int32, (size, LANES), 1)
    z = dot(normed[...], wz[...], 1, 0)
    dg = dot(cotan[pl.ds(pl.multiple_of(step * size, size), size), :], wo[...], 1, 1)
    v = conv_out[...]
    mixed = scan_out[...] + skip * (v * sigmoid(v))
    gi = mixed * (z * sigmoid(z))
    gate[...] = z
    mixed_out[...] = mixed
    d_gated[...] = dg
    squares = jnp.sum(gi * gi, axis=1, keepdims=True)
    slopes = jnp.sum(gi * dg * gain, axis=1, keepdims=True)
    both = jnp.where(lane == 0, squares, jnp.where(lane == 1, slopes, 0.0))
    sums[...] = jnp.transpose(both)[:8, :]


def assemble_two(copies, w_refs, owners, wz, wo, sems):
    rows = w_refs[0].shape[0]
    z_width = wz.shape[1]
    handles = []

    def start(src, dst):
        handle = pltpu.make_async_copy(src, dst, sems.at[len(handles)])
        handle.start()
        handles.append(handle)

    for src, dst, place in copies:
        size = src.shape[0]
        start(src, dst.at[pl.ds(pl.multiple_of(place * size, size), size), :])
    half = z_width // 2
    per = wo.shape[0] // (2 * rows)
    for src, (owner, col) in zip(w_refs, owners):
        if col == 0:
            part = src if src.shape[1] == z_width else src.at[:, 0:z_width]
            start(part, wz.at[pl.ds(pl.multiple_of(owner * rows, rows), rows), :])
        if col + src.shape[1] == 2 * z_width:
            at = 0 if col else z_width
            band = pl.multiple_of(lax.rem(owner, per) * (2 * rows), 2 * rows)
            column = pl.multiple_of(lax.div(owner, per) * half, half)
            for t in range(2):
                start(
                    src.at[:, at + t * half : at + (t + 1) * half],
                    wo.at[pl.ds(band + t * rows, rows), pl.ds(column, half)],
                )
    for handle in handles:
        handle.wait()


def turn_kernel(dims, ids, *refs):
    cols, inner, _, _ = dims
    gate, mixed_in, d_gated, sums, gain_all, normed, cotan, w_o = refs[:8]
    gated, d_gate, d_mixed, gain_grad, out_part, z_slab, o_slab = refs[8:]
    step = pl.program_id(0)
    gain = own_columns(gain_all, ids[0], cols, inner)

    @pl.when(step == 0)
    def _():
        gain_grad[...] = jnp.zeros_like(gain_grad)

    size = gate.shape[0]
    at = pl.ds(pl.multiple_of(step * size, size), size)
    stat = jnp.transpose(sums[...])
    scale = lax.rsqrt(stat[:, 0:1] / inner + norm_eps)
    slope = scale * scale * scale * (stat[:, 1:2] / inner)
    z = gate[...]
    sig = sigmoid(z)
    mixed = mixed_in[...]
    gi = mixed * (z * sig)
    dg = d_gated[...]
    scaled = gi * scale
    gated_c = (scaled * gain).astype(bf16)
    gated[at, :] = gated_c
    gain_grad[...] += jnp.sum(dg * scaled, axis=0, keepdims=True)
    d_gi = scale * (gain * dg) - gi * slope
    d_mixed[...] = d_gi * (z * sig)
    d_gate[at, :] = (d_gi * mixed * (sig * (1.0 + z * (1.0 - sig)))).astype(bf16)
    out_part[...] = dot(gated_c, w_o[...], 1, 0).astype(bf16)

    @pl.when(step == pl.num_programs(0) - 1)
    def _():
        turn_slabs(dims, gated, d_gate, normed, cotan, z_slab, o_slab)


def turn_slabs(dims, gated, d_gate, normed, cotan, z_slab, o_slab):
    cols, _, shards, deep = dims
    first, second = bit_orders(shards)
    rows_slab(normed, d_gate[...], z_slab, None, deep, first, None, 0)
    model = cotan.shape[1]
    strip = cols // 2
    bands = shards * strip // model
    size = max(2 * deep, LANES)
    for g in range(cols // size):
        left = gated[:, g * size : (g + 1) * size]
        for a in range(model // strip):
            part = dot(left, cotan[:, a * strip : (a + 1) * strip], 0, 0).astype(bf16)
            for i in range(size // deep):
                r, t = divmod(g * size // deep + i, 2)
                o_slab[slot(a * bands + r, second), :, t * strip : (t + 1) * strip] = part[
                    i * deep : (i + 1) * deep, :
                ]


def rows_slab(left, right, a_slab, b_slab, deep, first, second, cut):
    size = max(deep, LANES)
    for g in range(left.shape[1] // size):
        part = dot(left[:, g * size : (g + 1) * size], right, 0, 0).astype(bf16)
        for i in range(size // deep):
            owner = g * size // deep + i
            mine = part[i * deep : (i + 1) * deep, :]
            if b_slab is None:
                a_slab[slot(owner, first)] = mine
            else:
                a_slab[slot(owner, first)] = mine[:, :cut]
                b_slab[slot(owner, second)] = mine[:, cut:]


def weight_kernel(dims, normed, d_proj, a_slab, b_slab):
    shards, deep, cut = dims
    first, second = bit_orders(shards)
    rows_slab(normed, d_proj[...], a_slab, b_slab, deep, first, second, cut)


def entry_kernel(d_proj, d_gate, w_one, w_z, normed, gain, after, d_normed, norm_grad):
    step = pl.program_id(0)

    @pl.when(step == 0)
    def _():
        norm_grad[...] = jnp.zeros_like(norm_grad)

    part = dot(d_proj[...], w_one[...], 1, 1) + dot(d_gate[...], w_z[...], 1, 1)
    d_normed[...] = part.astype(bf16)
    norm_grad[...] += jnp.sum(part * normed[...].astype(f32), axis=0, keepdims=True)

    @pl.when(step == pl.num_programs(0) - 1)
    def _():
        norm_grad[...] = norm_grad[...] / gain[...]


def finish_kernel(dims, ids, *refs):
    cols, state, heads, n_seq = dims
    zo, one = refs[:n_seq], refs[n_seq : 2 * n_seq]
    in_grad, out_grad = refs[2 * n_seq :]
    inner = cols * n_seq
    strip = cols // 2
    deep = in_grad.shape[1]
    conv_cols = cols + 2 * state
    shared = None
    steps = None
    for o in range(n_seq):
        q = ids[0] ^ o
        block = pl.ds(pl.multiple_of(q * cols, LANES), cols)
        in_grad[block, :] = jnp.transpose(zo[o][:, :cols].astype(f32))
        block = pl.ds(pl.multiple_of(inner + q * cols, LANES), cols)
        in_grad[block, :] = jnp.transpose(one[o][:, :cols].astype(f32))
        band = one[o][:, cols:conv_cols].astype(f32)
        shared = band if shared is None else shared + band
        turned = pltpu.roll(one[o][:, conv_cols:].astype(f32), q * heads, 1)
        steps = turned if steps is None else steps + turned
        block = pl.ds(pl.multiple_of(q * strip, LANES), strip)
        out_grad[:deep, block] = zo[o][:, cols : cols + strip].astype(f32)
        out_grad[deep:, block] = zo[o][:, cols + strip :].astype(f32)
    in_grad[2 * inner : 2 * inner + 2 * state, :] = jnp.transpose(shared)
    in_grad[2 * inner + 2 * state :, :] = jnp.transpose(steps)[: heads * n_seq, :]


def back_kernel(dims, *refs):
    hd, heads, cols, state, inner = dims
    ids, conv_in, conv_out, dt_raw, scan_out, states, d_mixed, conv_w_all, table, picks = refs[:10]
    d_proj, held, halo, conv_grad, head_grad = refs[-5:]
    conv_cols = cols + 2 * state

    @pl.when(pl.program_id(0) == 0)
    def _():
        for start, carried in zip(refs[10:14], (held, halo, conv_grad, head_grad)):
            carried[...] = start[...]

    conv_w = own_columns(conv_w_all, ids[0], cols, inner)
    width = conv_w.shape[0]
    by_head = own_heads(table, ids[0], heads)
    dt_bias, a_log = by_head[0:1, :], by_head[1:2, :]
    skip = spread(by_head, hd, cols)[2:3, :]
    row = lax.broadcasted_iota(jnp.int32, (CHUNK, CHUNK), 0)
    col = lax.broadcasted_iota(jnp.int32, (CHUNK, CHUNK), 1)
    mask = row >= col
    upper = jnp.where(row <= col, 1.0, 0.0).astype(bf16)
    per = LANES // hd
    chunks = conv_in.shape[0] // CHUNK

    @pl.loop(0, chunks)
    def _(turn):
        c = chunks - 1 - turn
        at = pl.ds(pl.multiple_of(c * CHUNK, CHUNK), CHUNK)
        v = conv_out[at, :]
        sig = sigmoid(v)
        active = v * sig
        raw = dt_raw[at, :]
        step, log_decay, cum, cum_t = decays(raw, dt_bias, a_log)
        step_s = spread(step, hd, cols)
        x = active[:, :cols]
        xd = x * step_s
        xd_b = xd.astype(bf16)
        b_b = active[:, cols : cols + state].astype(bf16)
        c_b = active[:, cols + state :].astype(bf16)
        cross = dot(c_b, b_b, 1, 1)
        dm = d_mixed[at, :]
        dy_b = dm.astype(bf16)
        before_b = states[c]
        later = held[...]
        later_b = later.astype(bf16)
        d_cross = jnp.zeros((CHUNK, CHUNK), f32)
        tiles = []
        for j in range(cols // LANES):
            tile = None
            dm_tile = dm[:, j * LANES : (j + 1) * LANES]
            for i in range(per):
                h = j * per + i
                gap = cum[:, h : h + 1] - cum_t[h : h + 1, :]
                fall = jnp.exp(jnp.where(mask, gap, -1e30))
                kern = (fall * cross).astype(bf16)
                out = dot(kern, dy_b[:, j * LANES : (j + 1) * LANES], 0, 0)
                tile = out if tile is None else jnp.where(col >= i * hd, out, tile)
                own = (col >= i * hd) & (col < (i + 1) * hd)
                dy_h = jnp.where(own, dm_tile, 0.0).astype(bf16)
                d_cross = d_cross + fall * dot(dy_h, xd_b[:, j * LANES : (j + 1) * LANES], 1, 1)
            tiles.append(tile)
        intra = jnp.concatenate(tiles, axis=1) if len(tiles) > 1 else tiles[0]
        d_cross_b = d_cross.astype(bf16)
        grown = spread(jnp.exp(cum), hd, cols)
        dy_g = (dm * grown).astype(bf16)
        tail_s = spread(jnp.exp(cum[CHUNK - 1 : CHUNK, :] - cum), hd, cols)
        xt = (xd * tail_s).astype(bf16)
        d_c = dot(d_cross_b, b_b, 1, 0) + dot(dy_g, before_b, 1, 0)
        d_b = dot(d_cross_b, c_b, 0, 0) + dot(xt, later_b, 1, 0)
        inter = tail_s * dot(b_b, later_b, 1, 1)
        held[...] = decay_rows(cum_t, hd, heads, state) * later + dot(dy_g, c_b, 0, 0)
        d_xd = intra + inter
        carried = xd * inter
        change = (
            dy_b.astype(f32) * scan_out[at, :] - xd_b.astype(f32) * intra - carried
        )
        first_row = lax.broadcasted_iota(jnp.int32, (8, cols), 0)
        sums = jnp.where(
            first_row == 0,
            jnp.sum(dm * x, axis=0, keepdims=True),
            jnp.where(first_row == 1, jnp.sum(carried, axis=0, keepdims=True), 0.0),
        )
        by_head = exact(jnp.concatenate([change, x * d_xd, sums], axis=0), picks[...], 1, 0)
        change_h = by_head[:CHUNK]
        step_h = by_head[CHUNK : 2 * CHUNK]
        skip_h = by_head[2 * CHUNK : 2 * CHUNK + 1]
        carried_h = by_head[2 * CHUNK + 1 : 2 * CHUNK + 2]
        kept = before_b.astype(f32) * later
        lane = lax.broadcasted_iota(jnp.int32, (1, LANES), 1)
        kept_h = jnp.zeros((1, LANES), f32)
        for h in range(heads):
            own = jnp.sum(kept[h * hd : (h + 1) * hd, :], axis=0, keepdims=True)
            kept_h = jnp.where(lane == h, jnp.sum(own, axis=1, keepdims=True), kept_h)
        d_log = (
            exact(upper, change_h, 1, 0)
            + jnp.exp(cum[CHUNK - 1 : CHUNK, :]) * kept_h
            + carried_h
        )
        d_step = step_h - d_log * jnp.exp(a_log)
        d_raw = jnp.where(col < heads, d_step * sigmoid(raw + dt_bias), 0.0)
        head_grad[0:1, :] += jnp.sum(d_raw, axis=0, keepdims=True)
        head_grad[1:2, :] += jnp.sum(d_log * log_decay, axis=0, keepdims=True)
        head_grad[2:3, :] += skip_h
        d_x = step_s * d_xd + skip * dm
        d_active = jnp.concatenate([d_x, d_b, d_c], axis=1)
        d_v = d_active * (sig * (1.0 + v * (1.0 - sig)))
        both = jnp.concatenate([d_v, halo[...]], axis=0)
        halo[...] = d_v[:HALO, :]
        entered = conv_in[at, :].astype(f32)
        d_in = None
        for k in range(width):
            shifted = both[width - 1 - k : width - 1 - k + CHUNK, :]
            term = conv_w[k : k + 1, :] * shifted
            d_in = term if d_in is None else d_in + term
            conv_grad[k : k + 1, :] += jnp.sum(entered * shifted, axis=0, keepdims=True)
        conv_grad[width : width + 1, :] += jnp.sum(d_v, axis=0, keepdims=True)
        d_proj[at, :conv_cols] = d_in.astype(bf16)
        d_proj[at, conv_cols:] = d_raw.astype(bf16)


def shaped(shape, kind):
    return jax.ShapeDtypeStruct(shape, kind)


def body(
    hidden_in,
    norm_gain,
    in_weight,
    conv_weight,
    conv_bias,
    dt_bias,
    a_log,
    skip,
    inner_gain,
    out_weight,
    out_grad,
):
    n_seq = lax.axis_size("seq")
    n_shard = lax.axis_size("shard")
    me = lax.axis_index("seq")
    own = hidden_in[0]
    cotan_own = out_grad[0]
    rows, model = own.shape
    length = rows * n_seq
    inner = inner_gain.shape[0]
    conv_dim = conv_bias.shape[0]
    width = conv_weight.shape[0]
    heads_all = dt_bias.shape[0]
    hd = inner // heads_all
    state = (conv_dim - inner) // 2
    cols = inner // n_seq
    heads = heads_all // n_seq
    deep = in_weight.shape[0]
    conv_cols = cols + 2 * state
    one = conv_cols + LANES
    chunks = length // CHUNK

    def columns(array, start, size):
        return lax.dynamic_slice_in_dim(array, start, size, axis=array.ndim - 1)

    w_dt = columns(in_weight, inner + conv_dim + me * heads, heads)
    slab_one = jnp.concatenate(
        [
            columns(in_weight, inner + me * cols, cols),
            in_weight[:, 2 * inner : 2 * inner + 2 * state],
            jnp.pad(w_dt, ((0, 0), (0, LANES - heads))),
        ],
        axis=1,
    )
    bands = n_shard // n_seq
    strip = model // n_seq
    route = [
        (q * n_shard + s, (s // bands) * n_shard + q * bands + s % bands)
        for s in range(n_shard)
        for q in range(n_seq)
    ]
    out_rows = out_weight.shape[0]
    sent = columns(out_weight, me * strip, strip)
    tile = lax.ppermute(sent, ("seq", "shard"), route)
    slab_two = jnp.concatenate(
        [columns(in_weight, me * cols, cols), tile[:deep], tile[deep:]], axis=1
    )

    tok_blocks = seq_gather(own)
    cut_one = one // LANES // 2 * LANES
    ring_one = RingGather(slab_one, cut_one)
    while ring_one.step():
        pass
    n_bits = n_shard.bit_length() - 1
    late = lax.optimization_barrier((slab_two, cotan_own.astype(bf16), ring_one.a, ring_one.b))
    slab_two, cotan_b, ring_one.found[-2:] = (
        late[0],
        late[1],
        [(late[2], ring_one.found[-2][1], 0), (late[3], ring_one.found[-1][1], cut_one)],
    )
    ring_one = ring_one.found
    cot_blocks = seq_gather(cotan_b)
    ring_two = RingGather(slab_two, cols)

    ids = jnp.stack([me, lax.axis_index("shard")]).astype(jnp.int32)
    table = jnp.pad(
        jnp.stack([dt_bias, a_log, skip]), ((0, 5), (0, LANES - heads_all))
    )
    picks = jnp.where(jnp.arange(cols)[:, None] // hd == jnp.arange(LANES)[None, :], 1.0, 0.0)
    picks = picks.astype(bf16)

    n_one = len(ring_one)
    per_block = rows // CHUNK
    steps = n_seq // FRONT_PIECES
    kept = [
        (shaped((length, model), bf16), (rows, model)),
        (shaped((length, conv_cols), bf16), (rows, conv_cols)),
        (shaped((length, conv_cols), f32), (rows, conv_cols)),
        (shaped((length, LANES), f32), (rows, LANES)),
        (shaped((length, cols), f32), (rows, cols)),
        (shaped((chunks, cols, state), bf16), (per_block, cols, state)),
    ]

    def part(block, first, sign=1):
        return pl.BlockSpec(block, lambda i: (first + sign * i,) + (0,) * (len(block) - 1))

    stream = lambda width: pl.BlockSpec((rows, width), lambda i: (i, 0))

    carry_shapes = [shaped((cols, state), f32), shaped((HALO, conv_cols), f32)]
    front_cost = pl.CostEstimate(
        flops=steps * (2 * rows * model * one + 8 * rows * CHUNK * cols),
        bytes_accessed=steps * 12 * rows * model,
        transcendentals=steps * rows * CHUNK * heads,
    )
    constants = (norm_gain[None], conv_weight, conv_bias[None], table)
    dims = (hd, heads, cols, state, inner, n_seq, n_shard, cut_one)
    tokens, w_one, *rest = pl.pallas_call(
        functools.partial(front_kernel, dims + (None,)),
        name="front_0",
        grid=(steps,),
        in_specs=[SMEM] + [ANY] * (n_seq + n_one) + [VMEM] * 4,
        out_specs=[VMEM] * 2 + [part(block, 0) for _, block in kept] + [VMEM] * 2,
        out_shape=[shaped((length, model), bf16), shaped((model, one), bf16)]
        + [shape for shape, _ in kept]
        + carry_shapes,
        scratch_shapes=[
            pltpu.SemaphoreType.DMA((n_seq + n_one,)),
            pltpu.VMEM((rows, one), f32),
        ],
        cost_estimate=front_cost,
    )(ids, *tok_blocks, *[b for b, _, _ in ring_one], *constants)
    saved, carry = rest[:6], rest[6:]
    hops = -(-(n_shard // 2 - 1) // FRONT_PIECES)
    for j in range(1, FRONT_PIECES):
        arrived = [x for _ in range(hops) for x in ring_two.step()][-2:]
        n_skip = len(arrived) + 6
        *rest, held, halo = pl.pallas_call(
            functools.partial(front_kernel, dims + (n_skip,)),
            grid=(steps,),
            in_specs=[SMEM, part((rows, model), j * steps)] + [VMEM] * 7 + [ANY] * n_skip,
            out_specs=[part(block, j * steps) for _, block in kept] + [VMEM] * 2,
            out_shape=[shape for shape, _ in kept] + carry_shapes,
            input_output_aliases={9 + len(arrived) + i: i for i in range(6)},
            scratch_shapes=[pltpu.VMEM((rows, one), f32)],
            cost_estimate=front_cost,
        )(ids, tokens, w_one, *constants, *carry, *arrived, *saved)
        saved, carry = rest, (held, halo)
    normed, conv_in, conv_out, dt_raw, scan_out, states = saved
    while ring_two.step():
        pass
    ring_two = ring_two.found

    n_two = len(ring_two)
    wide = [shaped((length, cols), f32)] * 3
    cotan, w_z, w_o, gate, mixed, d_gated, sums = pl.pallas_call(
        functools.partial(gate_kernel, (cols, heads, hd, n_seq, n_shard)),
        name="gate",
        grid=(n_seq,),
        in_specs=[SMEM]
        + [ANY] * (n_seq + n_two)
        + [stream(model), stream(cols), stream(cols)]
        + [VMEM] * 2,
        out_specs=[VMEM] * 3
        + [stream(cols)] * 3
        + [pl.BlockSpec((8, rows), lambda i: (0, i))],
        out_shape=[
            shaped((length, model), bf16),
            shaped((model, cols), bf16),
            shaped((cols, model), bf16),
            *wide,
            shaped((8, length), f32),
        ],
        scratch_shapes=[pltpu.SemaphoreType.DMA((n_seq + 3 * n_two,))],
        cost_estimate=pl.CostEstimate(
            flops=4 * length * model * cols,
            bytes_accessed=14 * length * model,
            transcendentals=2 * length * cols,
        ),
    )(
        ids,
        *cot_blocks,
        *[b for b, _, _ in ring_two],
        normed,
        conv_out,
        scan_out,
        table,
        inner_gain[None],
    )

    sums = all_sum(sums, "seq")
    _, d_gate, d_mixed, gain_part, out_part, z_slab, o_slab = pl.pallas_call(
        functools.partial(turn_kernel, (cols, inner, n_shard, deep)),
        name="turn",
        grid=(n_seq,),
        in_specs=[SMEM]
        + [stream(cols)] * 3
        + [pl.BlockSpec((8, rows), lambda i: (0, i))]
        + [VMEM] * 4,
        out_specs=[VMEM, VMEM, stream(cols), VMEM, stream(model), VMEM, VMEM],
        out_shape=[
            shaped((length, cols), bf16),
            shaped((length, cols), bf16),
            shaped((length, cols), f32),
            shaped((1, cols), f32),
            shaped((length, model), bf16),
            shaped((n_shard, deep, cols), bf16),
            shaped((n_shard, deep, cols), bf16),
        ],
        cost_estimate=pl.CostEstimate(
            flops=6 * length * cols * model, bytes_accessed=30 * length * cols, transcendentals=0
        ),
    )(ids, gate, mixed, d_gated, sums, inner_gain[None], normed, cotan, w_o)

    halving = Halving((z_slab, o_slab))
    carry = [jnp.zeros(s, f32) for s in ((cols, state), (HALO, conv_cols), (8, conv_cols), (8, LANES))]
    hops = max(1, n_bits // BACK_PIECES)
    steps = n_seq // BACK_PIECES
    d_proj = None
    for j in reversed(range(BACK_PIECES)):
        arrived = []
        if d_proj is not None:
            for _ in range(hops):
                arrived = halving.step() or arrived
        extra = list(arrived) + ([] if d_proj is None else [d_proj])
        last = (j + 1) * steps - 1
        d_proj, *carry = pl.pallas_call(
            functools.partial(back_kernel, (hd, heads, cols, state, inner)),
            grid=(steps,),
            in_specs=[SMEM]
            + [part(block, last, -1) for _, block in kept[1:]]
            + [part((rows, cols), last, -1)]
            + [VMEM] * 7
            + [ANY] * len(extra),
            out_specs=[part((rows, one), last, -1)] + [VMEM] * 4,
            out_shape=[shaped((length, one), bf16)] + [shaped(c.shape, f32) for c in carry],
            input_output_aliases={} if d_proj is None else {13 + len(extra): 0},
            cost_estimate=pl.CostEstimate(
                flops=steps * 20 * rows * CHUNK * cols,
                bytes_accessed=steps * 14 * rows * model,
                transcendentals=steps * rows * CHUNK * heads,
            ),
        )(
            ids,
            conv_in,
            conv_out,
            dt_raw,
            scan_out,
            states,
            d_mixed,
            conv_weight,
            table,
            picks,
            *carry,
            *extra,
        )
    conv_part, head_part = carry[2:]
    a_slab, b_slab = pl.pallas_call(
        functools.partial(weight_kernel, (n_shard, deep, cut_one)),
        name="weight",
        in_specs=[VMEM] * 2,
        out_specs=[VMEM] * 2,
        out_shape=[
            shaped((n_shard, deep, cut_one), bf16),
            shaped((n_shard, deep, one - cut_one), bf16),
        ],
        cost_estimate=pl.CostEstimate(
            flops=2 * length * model * one, bytes_accessed=6 * length * model, transcendentals=0
        ),
    )(normed, d_proj)
    one_own = Halving((a_slab, b_slab)).finish()
    one_all = seq_gather(jnp.concatenate(one_own, axis=1))

    z_own, o_own = halving.finish()
    o_own = lax.ppermute(o_own, ("seq", "shard"), [(b, a) for a, b in route])
    zo_all = seq_gather(jnp.concatenate([z_own, o_own], axis=1))
    in_weight_grad, out_weight_grad = pl.pallas_call(
        functools.partial(finish_kernel, (cols, state, heads, n_seq)),
        name="finish",
        in_specs=[SMEM] + [VMEM] * (2 * n_seq),
        out_specs=[VMEM] * 2,
        out_shape=[shaped((in_weight.shape[1], deep), f32), shaped((out_rows, model), f32)],
    )(ids, *zo_all, *one_all)
    in_weight_grad = in_weight_grad.T

    block_out = own.astype(f32) + seq_scatter(out_part.reshape(n_seq, rows, model))

    d_normed, norm_part = pl.pallas_call(
        entry_kernel,
        name="entry",
        grid=(n_seq,),
        in_specs=[stream(one), stream(cols), VMEM, VMEM, stream(model), VMEM, ANY],
        out_specs=[stream(model), VMEM],
        out_shape=[shaped((length, model), bf16), shaped((1, model), f32)],
        cost_estimate=pl.CostEstimate(
            flops=3 * length * model * one, bytes_accessed=10 * length * model, transcendentals=0
        ),
    )(d_proj, d_gate, w_one, w_z, normed, norm_gain[None], a_slab)
    d_own = seq_scatter(d_normed.reshape(n_seq, rows, model))
    own_f = own.astype(f32)
    rstat = lax.rsqrt(jnp.mean(own_f * own_f, axis=-1, keepdims=True) + norm_eps)
    scaled = norm_gain * d_own
    along = jnp.mean(scaled * own_f, axis=-1, keepdims=True)
    input_grad = cotan_own + rstat * scaled - own_f * rstat * rstat * rstat * along

    def placed(array, size, start):
        wide = jnp.zeros((array.shape[0], size), f32)
        return lax.dynamic_update_slice_in_dim(wide, array, start, axis=1)

    packed = jnp.concatenate(
        [
            placed(conv_part[:, :cols], inner, me * cols),
            conv_part[:, cols:],
            placed(head_part[:, :heads], LANES, me * heads),
            placed(gain_part, inner, me * cols).reshape(8, -1),
            norm_part.reshape(8, -1),
        ],
        axis=1,
    )
    packed = all_sum(all_sum(packed, "shard"), "seq")
    head_all = packed[:, conv_dim : conv_dim + heads_all]
    gain_at = conv_dim + LANES
    gain_all = packed[:, gain_at : gain_at + inner // 8].reshape(-1)
    norm_all = packed[:, gain_at + inner // 8 :].reshape(-1)
    return (
        block_out[None],
        input_grad[None],
        norm_all,
        in_weight_grad,
        packed[:width, :conv_dim],
        packed[width, :conv_dim],
        head_all[0],
        head_all[1],
        head_all[2],
        gain_all,
        out_weight_grad,
    )


def solution(mesh):
    tokens = P("shard", "seq", None)
    rows = P("shard", None)

    return jax.shard_map(
        body,
        mesh=mesh,
        in_specs=(tokens, P(), rows, P(), P(), P(), P(), P(), P(), rows, tokens),
        out_specs=(tokens, tokens, P(), rows, P(), P(), P(), P(), P(), P(), rows),
        check_vma=False,
    )
```

time: 328 us -> 284 us (0.87)
  waiting for transfers between devices: 51.5 us -> 97.2 us
  starting transfers between devices: 89.8 us -> 53 us
  local copies, waits for them, and re-layouts: 52.3 us -> 20.9 us
  other arithmetic: 37.4 us -> 13.8 us
  Pallas kernels: 77.3 us -> 96.1 us
  matrix products: 16.1 us -> 0 us
    ppermute x27 -> x35, waiting for transfers between devices: 10.3 us -> 69 us  [swap(): return lax.ppermute(block, axis, [(i, i ^ distance) for i in range(n)])]
    ppermute x44 -> x16, starting transfers between devices: 58.5 us -> 18.2 us  [the longest x6 7.46 us: step(): self.a = lax.ppermute(self.a, 'shard', self.ahead)]
    pallas_call x4 -> x11, Pallas kernels: 77.3 us -> 96.1 us  [the longest x2 28.8 us: body(): pl.pallas_call(functools.partial(back_kernel, (hd, heads, cols, state, in...]
    dot_general x6 -> x0, matrix products: 16.1 us -> none  [the longest x5 13.6 us: dot(): lax.dot_general(left, right, (((l,), (r,)), ((), ())), preferred_element_...]
    convert_element_type x39 -> x10, other arithmetic: 17.8 us -> 3.27 us  [the longest x8 2.41 us: step(): self.slabs[i] = (keep.astype(f32) + got.astype(f32)).astype(bf16)]
    ppermute x44 -> x16, waiting for transfers between devices: 41.2 us -> 28.2 us  [the longest x6 15.4 us: step(): self.a = lax.ppermute(self.a, 'shard', self.ahead)]
    unnamed x136 -> x116, local copies, waits for them, and re-layouts: 14 us -> 4.13 us
    reshape x8 -> x2, local copies, waits for them, and re-layouts: 9.08 us -> 0.6 us  [the longest x1 0.59 us: body(): norm_all = packed[:, gain_at + inner // 8:].reshape(-1)]
  transfers between devices with their start and end apart: 73 -> 53, of which waited for: 31 -> 26; matrix products, arithmetic and copies ran while one was open for 19% -> 8% of each run, Pallas kernels for 6% -> 26%
where the time goes in v2:
time: 284 us; the launch traced here: 283 us
  waiting for transfers between devices  97.2 us (34%)
  Pallas kernels  96.1 us (34%)
  starting transfers between devices  53 us (19%)
  local copies, waits for them, and re-layouts  20.9 us (7%)
  other arithmetic  13.8 us (5%)
    ppermute x35, waiting for transfers between devices, swap(): return lax.ppermute(block, axis, [(i, i ^ distance) for i in range(n)])  69 us
    ppermute x35, starting transfers between devices, swap(): return lax.ppermute(block, axis, [(i, i ^ distance) for i in range(n)])  33.3 us
    pallas_call x2, Pallas kernels, body(): pl.pallas_call(functools.partial(back_kernel, (hd, heads, cols, state, in...  28.8 us
    pallas_call x3, Pallas kernels, body(): pl.pallas_call(functools.partial(front_kernel, dims + (n_skip,)), grid=(s...  18.5 us
    ppermute x6, waiting for transfers between devices, step(): self.a = lax.ppermute(self.a, 'shard', self.ahead)  15.4 us
    pallas_call x1, Pallas kernels, body(): pl.pallas_call(functools.partial(turn_kernel, (cols, inner, n_shard, deep...  12.5 us
    pallas_call x1, Pallas kernels, body(): pl.pallas_call(functools.partial(gate_kernel, (cols, heads, hd, n_seq, n_...  10.5 us
    ppermute x6, waiting for transfers between devices, step(): self.b = lax.ppermute(self.b, 'shard', self.back)  9.43 us
  transfers between devices with their start and end apart: 53, of which 26 were waited for; matrix products, arithmetic and copies ran while one was open for 8% of the time, Pallas kernels for 26%

profile of v2, /device:TPU:0, one launch (start us, length us, event | category | flops | bytes accessed | tf_op | source)
XLA Modules:
  0.0 282.7 jit_solution(6064071753017967036)
XLA Ops:
  3.8 3.1 %collective-permute-start.1 = (bf16[128,896]{1,0:T(8,128)(2,1)S(1)}, bf16[128,896]{1,0:T(8,128)(2,1)S(1)}, u32[]{:S(2)}, u32[]{:S(2)}) collective-permute-start(bf16[128,896]{1,0:T(8,128)(2,1)S(1)} %fusion.15.refs_4_), channel_id=1, source_target_pairs={{0,2},{2,4},{4,6},{6,7},{7,5},{5,3},{3,1},{1,0},{8,10},{10,12},{12... | collective-permute-start | bytes 688136 | tf_op jit(solution)/shard_map/ppermute | solution.py:102
  6.9 5.5 %collective-permute-done.1.refs_5_ = bf16[128,896]{1,0:T(8,128)(2,1)S(1)} collective-permute-done((bf16[128,896]{1,0:T(8,128)(2,1)S(1)}, bf16[128,896]{1,0:T(8,128)(2,1)S(1)}, u32[]{:S(2)}, u32[]{:S(2)}) %collective-permute-start.1) | collective-permute-done | bytes 229408 | tf_op jit(solution)/shard_map/ppermute | solution.py:102
  21.5 9.2 %collective-permute-done.7.refs_10_ = bf16[128,896]{1,0:T(8,128)(2,1)S(1)} collective-permute-done((bf16[128,896]{1,0:T(8,128)(2,1)S(1)}, bf16[128,896]{1,0:T(8,128)(2,1)S(1)}, u32[]{:S(2)}, u32[]{:S(2)}) %collective-permute-start.7) | collective-permute-done | bytes 229408 | tf_op jit(solution)/shard_map/ppermute | solution.py:103
  30.8 2.6 collective-permute-start.4
  40.9 5.6 %collective-permute-done.12.refs_8_.refs_5_ = bf16[128,1024]{1,0:T(8,128)(2,1)S(1)} collective-permute-done((bf16[128,1024]{1,0:T(8,128)(2,1)S(1)}, bf16[128,1024]{1,0:T(8,128)(2,1)S(1)}, u32[]{:S(2)}, u32[]{:S(2)}) %collective-permute-start.12) | collective-permute-done | bytes 262176 | tf_op jit(solution)/shard_map/ppermute | solution.py:102
  56.6 8.6 %front_0.1 = (bf16[1024,1024]{1,0:T(8,128)(2,1)}, bf16[1024,896]{1,0:T(8,128)(2,1)}, bf16[1024,1024]{1,0:T(8,128)(2,1)}, bf16[1024,768]{1,0:T(8,128)(2,1)}, f32[...) custom-call(s32[2]{0:T(128)} %pad_add_fusion.ids.refs_0_, ...), custom_call_target="tpu_custom_call" | custom-call | flops 603979776 | bytes 3145728 | tf_op jit(solution)/shard_map/front_0/pallas_call | solution.py:758
  67.6 6.2 %shard_map.194 = (bf16[1024,1024]{1,0:T(8,128)(2,1)}, bf16[1024,768]{1,0:T(8,128)(2,1)}, f32[1024,768]{1,0:T(8,128)}, f32[1024,128]{1,0:T(8,128)}, f32[1024,512]...) custom-call(s32[2]{0:T(128)} %pad_add_fusion.ids.refs_0_, ...), custom_call_target="tpu_custom_call", output_to_operand_aliasing={{0}: (11, {}), {1}: (12, {}), {2}: (13, {}), {3}: (14, {}),... | custom-call | flops 603979776 | bytes 3145728 | tf_op jit(solution)/shard_map/pallas_call | solution.py:778
  73.8 6.2 %shard_map.195 = (bf16[1024,1024]{1,0:T(8,128)(2,1)}, bf16[1024,768]{1,0:T(8,128)(2,1)}, f32[1024,768]{1,0:T(8,128)}, f32[1024,128]{1,0:T(8,128)}, f32[1024,512]...) custom-call(s32[2]{0:T(128)} %pad_add_fusion.ids.refs_0_, ...), custom_call_target="tpu_custom_call", output_to_operand_aliasing={{0}: (11, {}), {1}: (12, {}), {2}: (13, {}), {3}: (14, {}),... | custom-call | flops 603979776 | bytes 3145728 | tf_op jit(solution)/shard_map/pallas_call | solution.py:778
  80.0 6.2 %shard_map.196 = (bf16[1024,1024]{1,0:T(8,128)(2,1)}, bf16[1024,768]{1,0:T(8,128)(2,1)}, f32[1024,768]{1,0:T(8,128)}, f32[1024,128]{1,0:T(8,128)}, f32[1024,512]...) custom-call(s32[2]{0:T(128)} %pad_add_fusion.ids.refs_0_, ...), custom_call_target="tpu_custom_call", output_to_operand_aliasing={{0}: (11, {}), {1}: (12, {}), {2}: (13, {}), {3}: (14, {}),... | custom-call | flops 603979776 | bytes 3145728 | tf_op jit(solution)/shard_map/pallas_call | solution.py:778
  86.9 10.5 %gate.1 = (bf16[1024,1024]{1,0:T(8,128)(2,1)}, bf16[1024,512]{1,0:T(8,128)(2,1)}, bf16[512,1024]{1,0:T(8,128)(2,1)}, f32[1024,512]{1,0:T(8,128)}, f32[1024,512]{...) custom-call(s32[2]{0:T(128)} %pad_add_fusion.ids.refs_0_, bf16[256,1024]{1,0:T(8,128)(2,1)} %copy-done.11, ...), custom_call_target="tpu_custom_call" | custom-call | flops 2147483648 | bytes 14680064 | tf_op jit(solution)/shard_map/gate/pallas_call | solution.py:796
  100.3 3.3 %collective-permute-done.24 = f32[8,1024]{1,0:T(8,128)S(1)} collective-permute-done((f32[8,1024]{1,0:T(8,128)S(1)}, f32[8,1024]{1,0:T(8,128)S(1)}, u32[]{:S(2)}, u32[]{:S(2)}) %collective-permute-start.24) | collective-permute-done | bytes 32800 | tf_op jit(solution)/shard_map/ppermute | solution.py:27
  104.2 12.5 %turn.1 = (bf16[1024,512]{1,0:T(8,128)(2,1)}, bf16[1024,512]{1,0:T(8,128)(2,1)}, f32[1024,512]{1,0:T(8,128)}, f32[1,512]{1,0:T(1,128)}, bf16[1024,1024]{1,0:T(8,...) custom-call(s32[2]{0:T(128)} %pad_add_fusion.ids.refs_0_, f32[1024,512]{1,0:T(8,128)} %get-tuple-element.107.refs_0_, ...), custom_call_target="tpu_custom_call" | custom-call | flops 3221225472 | bytes 15728640 | tf_op jit(solution)/shard_map/turn/pallas_call | solution.py:832
  128.4 14.7 %shard_map.197 = (bf16[1024,896]{1,0:T(8,128)(2,1)}, f32[512,128]{1,0:T(8,128)}, f32[8,768]{1,0:T(8,128)}, f32[8,768]{1,0:T(8,128)}, f32[8,128]{1,0:T(8,128)}) custom-call(s32[2]{0:T(128)} %pad_add_fusion.ids.refs_0_, bf16[1024,768]{1,0:T(8,128)(2,1)} %get-tuple-element.114.refs_1_, f32[1024,768]{1,0:T(8,128)} %get-tuple-element.105.refs_14_.refs_2_, ...), custom_call_target="tpu_custom_call" | custom-call | flops 671088640 | bytes 7340032 | tf_op jit(solution)/shard_map/pallas_call | solution.py:867
  145.0 14.2 %shard_map.198 = (bf16[1024,896]{1,0:T(8,128)(2,1)}, f32[512,128]{1,0:T(8,128)}, f32[8,768]{1,0:T(8,128)}, f32[8,768]{1,0:T(8,128)}, f32[8,128]{1,0:T(8,128)}) custom-call(s32[2]{0:T(128)} %pad_add_fusion.ids.refs_0_, bf16[1024,768]{1,0:T(8,128)(2,1)} %get-tuple-element.114.refs_1_, ...), custom_call_target="tpu_custom_call", output_to_operand_aliasing={{0}: (16, {})} | custom-call | flops 671088640 | bytes 7340032 | tf_op jit(solution)/shard_map/pallas_call | solution.py:867
  159.2 5.6 %weight.1 = (bf16[8,128,384]{2,1,0:T(8,128)(2,1)}, bf16[8,128,512]{2,1,0:T(8,128)(2,1)}) custom-call(bf16[1024,1024]{1,0:T(8,128)(2,1)} %get-tuple-element.104.refs_13_.refs_5_.normed, bf16[1024,896]{1,0:T(8,128)(2,1)} %get-tuple-element.125.d_proj), custom_call_target="tpu_custom_call" | custom-call | flops 1879048192 | bytes 6291456 | tf_op jit(solution)/shard_map/weight/pallas_call | solution.py:898
  164.8 7.8 %entry.1 = (bf16[1024,1024]{1,0:T(8,128)(2,1)}, f32[1,1024]{1,0:T(1,128)}) custom-call(bf16[1024,896]{1,0:T(8,128)(2,1)} %get-tuple-element.125.d_proj, bf16[1024,512]{1,0:T(8,128)(2,1)} %get-tuple-element.126.d_gate, bf16[1024,896]{1,0:T(8,128)(2,1)} %get-tuple-element.79.refs_1_.w_one, bf16[1024,512]{1,0:T(8,128)(2,1)} %get-tuple-element.127.w_z, ...), custom_call_target="tpu_custom_call" | custom-call | flops 2818572288 | bytes 10485760 | tf_op jit(solution)/shard_map/entry/pallas_call | solution.py:928
  178.0 2.6 collective-permute-done.31
  181.4 5.6 %collective-permute-done.32 = f32[8,2816]{1,0:T(8,128)S(1)} collective-permute-done((f32[8,2816]{1,0:T(8,128)S(1)}, f32[8,2816]{1,0:T(8,128)S(1)}, u32[]{:S(2)}, u32[]{:S(2)}) %collective-permute-start.32) | collective-permute-done | bytes 90144 | tf_op jit(solution)/shard_map/ppermute | solution.py:27
  190.9 10.1 %collective-permute-done.33 = f32[8,2816]{1,0:T(8,128)S(1)} collective-permute-done((f32[8,2816]{1,0:T(8,128)S(1)}, f32[8,2816]{1,0:T(8,128)S(1)}, u32[]{:S(2)}, u32[]{:S(2)}) %collective-permute-start.33) | collective-permute-done | bytes 90144 | tf_op jit(solution)/shard_map/ppermute | solution.py:27
  202.9 3.4 %collective-permute-start.37 = (bf16[1,128,512]{2,1,0:T(8,128)(2,1)S(1)}, bf16[1,128,512]{2,1,0:T(8,128)(2,1)S(1)}, u32[]{:S(2)}, u32[]{:S(2)}) collective-permute-start(bf16[1,128,512]{2,1,0:T(8,128)(2,1)S(1)} %constant_dynamic-slice_fusion.3), channel_id=1, source_target_pairs={{0,4},{1,5},{2,6},{3,7},{4,0},{5,1},{6,2},{7,3},{8,12},{9,13},{10,... | collective-permute-start | bytes 393224 | tf_op jit(solution)/shard_map/ppermute | solution.py:27
  206.4 6.3 %collective-permute-done.37 = bf16[1,128,512]{2,1,0:T(8,128)(2,1)S(1)} collective-permute-done((bf16[1,128,512]{2,1,0:T(8,128)(2,1)S(1)}, bf16[1,128,512]{2,1,0:T(8,128)(2,1)S(1)}, u32[]{:S(2)}, u32[]{:S(2)}) %collective-permute-start.37) | collective-permute-done | bytes 131104 | tf_op jit(solution)/shard_map/ppermute | solution.py:27
  214.6 2.7 collective-permute-done.35
  221.6 3.1 %collective-permute-start.41 = (bf16[128,1024]{1,0:T(8,128)(2,1)S(1)}, bf16[128,1024]{1,0:T(8,128)(2,1)S(1)}, u32[]{:S(2)}, u32[]{:S(2)}) collective-permute-start(bf16[128,1024]{1,0:T(8,128)(2,1)S(1)} %pad_maximum_fusion.1.refs_0_), channel_id=1, source_target_pairs={{0,8},{8,0},{16,24},{24,16},{1,9},{9,1},{17,25},{25,17},{2,10},{10... | collective-permute-start | bytes 786440 | tf_op jit(solution)/shard_map/ppermute | solution.py:27
  224.7 2.7 collective-permute-start.42
  228.9 7.0 %collective-permute-done.48 = bf16[2,128,512]{2,1,0:T(8,128)(2,1)S(1)} collective-permute-done((bf16[2,128,512]{2,1,0:T(8,128)(2,1)S(1)}, bf16[2,128,512]{2,1,0:T(8,128)(2,1)S(1)}, u32[]{:S(2)}, u32[]{:S(2)}) %collective-permute-start.48) | collective-permute-done | bytes 262176 | tf_op jit(solution)/shard_map/ppermute | solution.py:27
  236.1 6.7 %collective-permute-done.46 = bf16[1,128,384]{2,1,0:T(8,128)(2,1)S(1)} collective-permute-done((bf16[1,128,384]{2,1,0:T(8,128)(2,1)S(1)}, bf16[1,128,384]{2,1,0:T(8,128)(2,1)S(1)}, u32[]{:S(2)}, u32[]{:S(2)}) %collective-permute-start.46) | collective-permute-done | bytes 98336 | tf_op jit(solution)/shard_map/ppermute | solution.py:27
  243.0 5.9 %collective-permute-done.49 = bf16[1,128,512]{2,1,0:T(8,128)(2,1)S(1)} collective-permute-done((bf16[1,128,512]{2,1,0:T(8,128)(2,1)S(1)}, bf16[1,128,512]{2,1,0:T(8,128)(2,1)S(1)}, u32[]{:S(2)}, u32[]{:S(2)}) %collective-permute-start.49) | collective-permute-done | bytes 131104 | tf_op jit(solution)/shard_map/ppermute | solution.py:27
  249.0 2.6 collective-permute-start.51
  258.4 2.5 collective-permute-start.26
  263.0 3.6 %finish.1 = (f32[4384,128]{1,0:T(8,128)}, f32[256,1024]{1,0:T(8,128)}) custom-call(s32[2]{0:T(128)} %pad_add_fusion.ids.refs_0_, bf16[128,1024]{1,0:T(8,128)(2,1)} %copy-done.20, bf16[128,1024]{1,0:T(8,128)(2,1)} %copy-done.30, bf16[128,1024]{1,0:T(8,128)(2,1)} %copy-done.31, bf16[128,1024]{1,0:T(8,128)(2,1)} %copy-done.32, bf16[128,896]{1,0:T(8,128)(2,1)} %copy-done.25, ...), custom_call_target="tpu_custom_call" | custom-call | tf_op jit(solution)/shard_map/finish/pallas_call | solution.py:917
  270.2 9.0 %collective-permute-done.26 = bf16[1,256,1024]{2,1,0:T(8,128)(2,1)} collective-permute-done((bf16[1,256,1024]{2,1,0:T(8,128)(2,1)}, bf16[1,256,1024]{2,1,0:T(8,128)(2,1)}, u32[]{:S(2)}, u32[]{:S(2)}) %collective-permute-start.26) | collective-permute-done | bytes 524320 | tf_op jit(solution)/shard_map/ppermute | solution.py:27
  279.3 3.4 %fusion.3 = (f32[1,256,1024]{2,1,0:T(8,128)}, f32[1,256,1024]{2,1,0:T(8,128)}) fusion(bf16[1,256,1024]{2,1,0:T(8,128)(2,1)S(1)} %copy-done.4, f32[1,256,1024]{2,1,0:T(8,128)} %param.21, bf16[1,256,1024]{2,1,0:T(8,128)(2,1)} %copy-done.12, f32[2,256,1024]{2,1,0:T(8,128)S(1)} %convert_add_fusion, s32[]{:T(128)S(6)} %select_n.128, ...), kind=kLoop, calls=%fused_computation.9 | loop fusion | flops 3670016 | bytes 6821892 | tf_op jit(solution)/shard_map/sub | solution.py:944
  (276 shorter events, 82.2 us)
Async XLA Ops:
  3.8 8.6 %collective-permute-start.1 = (bf16[128,896]{1,0:T(8,128)(2,1)S(1)}, bf16[128,896]{1,0:T(8,128)(2,1)S(1)}, u32[]{:S(2)}, u32[]{:S(2)}) collective-permute-start(bf16[128,896]{1,0:T(8,128)(2,1)S(1)} %fusion.15.refs_4_), channel_id=1, source_target_pairs={{0,2},{2,4},{4,6},{6,7},{7,5},{5,3},{3,1},{1,0},{8,10},{10,12},{12... | collective-permute-start | bytes 688136 | tf_op jit(solution)/shard_map/ppermute | solution.py:102
  14.4 34.1 %collective-permute-start.20 = (bf16[256,1024]{1,0:T(8,128)(2,1)}, bf16[256,1024]{1,0:T(8,128)(2,1)}, u32[]{:S(2)}, u32[]{:S(2)}) collective-permute-start(bf16[256,1024]{1,0:T(8,128)(2,1)} %bitcast.102), channel_id=1, source_target_pairs={{0,8},{8,0},{16,24},{24,16},{1,9},{9,1},{17,25},{25,17},{2,10},{10... | collective-permute-start | bytes 1572872 | tf_op jit(solution)/shard_map/ppermute | solution.py:27
  14.4 26.5 %collective-permute-start.21 = (bf16[256,1024]{1,0:T(8,128)(2,1)}, bf16[256,1024]{1,0:T(8,128)(2,1)}, u32[]{:S(2)}, u32[]{:S(2)}) collective-permute-start(bf16[256,1024]{1,0:T(8,128)(2,1)} %bitcast.103), channel_id=1, source_target_pairs={{0,16},{8,24},{16,0},{24,8},{1,17},{9,25},{17,1},{25,9},{2,18},{10... | collective-permute-start | bytes 1572872 | tf_op jit(solution)/shard_map/ppermute | solution.py:27
  16.2 14.5 %collective-permute-start = (bf16[256,256]{1,0:T(8,128)(2,1)S(1)}, bf16[256,256]{1,0:T(8,128)(2,1)S(1)}, u32[]{:S(2)}, u32[]{:S(2)}) collective-permute-start(bf16[256,256]{1,0:T(8,128)(2,1)S(1)} %constant_dynamic-slice_fusion.6), channel_id=1, source_target_pairs={{0,0},{8,2},{16,4},{24,6},{1,1},{9,3},{17,5},{25,7},{2,8},{10,10},... | collective-permute-start | bytes 393224 | tf_op jit(solution)/shard_map/ppermute | solution.py:705
  19.2 11.6 %collective-permute-start.3 = (bf16[128,896]{1,0:T(8,128)(2,1)S(1)}, bf16[128,896]{1,0:T(8,128)(2,1)S(1)}, u32[]{:S(2)}, u32[]{:S(2)}) collective-permute-start(bf16[128,896]{1,0:T(8,128)(2,1)S(1)} %collective-permute-done.2.refs_7_), channel_id=1, source_target_pairs={{0,2},{2,4},{4,6},{6,7},{7,5},{5,3},{3,1},{1,0},{8,10},{10,12},{12... | collective-permute-start | bytes 688136 | tf_op jit(solution)/shard_map/ppermute | solution.py:102
  20.7 9.9 %collective-permute-start.7 = (bf16[128,896]{1,0:T(8,128)(2,1)S(1)}, bf16[128,896]{1,0:T(8,128)(2,1)S(1)}, u32[]{:S(2)}, u32[]{:S(2)}) collective-permute-start(bf16[128,896]{1,0:T(8,128)(2,1)S(1)} %collective-permute-done.6.refs_8_), channel_id=1, source_target_pairs={{2,0},{4,2},{6,4},{7,6},{5,7},{3,5},{1,3},{0,1},{10,8},{12,10},{14... | collective-permute-start | bytes 688136 | tf_op jit(solution)/shard_map/ppermute | solution.py:103
  36.8 13.7 %collective-permute-start.10 = (bf16[256,1024]{1,0:T(8,128)(2,1)S(1)}, bf16[256,1024]{1,0:T(8,128)(2,1)S(1)}, u32[]{:S(2)}, u32[]{:S(2)}) collective-permute-start(bf16[256,1024]{1,0:T(8,128)(2,1)S(1)} %convert_bitcast_fusion.refs_0_), channel_id=1, source_target_pairs={{0,16},{8,24},{16,0},{24,8},{1,17},{9,25},{17,1},{25,9},{2,18},{10... | collective-permute-start | bytes 1572872 | tf_op jit(solution)/shard_map/ppermute | solution.py:27
  40.9 15.6 %collective-permute-start.22 = (bf16[256,1024]{1,0:T(8,128)(2,1)}, bf16[256,1024]{1,0:T(8,128)(2,1)}, u32[]{:S(2)}, u32[]{:S(2)}) collective-permute-start(bf16[256,1024]{1,0:T(8,128)(2,1)} %collective-permute-done.21.refs_2_), channel_id=1, source_target_pairs={{0,8},{8,0},{16,24},{24,16},{1,9},{9,1},{17,25},{25,17},{2,10},{10... | collective-permute-start | bytes 1572872 | tf_op jit(solution)/shard_map/ppermute | solution.py:27
  48.6 37.6 %collective-permute-start.9 = (bf16[256,1024]{1,0:T(8,128)(2,1)S(1)}, bf16[256,1024]{1,0:T(8,128)(2,1)}, u32[]{:S(2)}, u32[]{:S(2)}) collective-permute-start(bf16[256,1024]{1,0:T(8,128)(2,1)S(1)} %convert_bitcast_fusion.refs_0_), channel_id=1, source_target_pairs={{0,8},{8,0},{16,24},{24,16},{1,9},{9,1},{17,25},{25,17},{2,10},{10... | collective-permute-start | bytes 1572872 | tf_op jit(solution)/shard_map/ppermute | solution.py:27
  50.5 35.7 %collective-permute-start.11 = (bf16[256,1024]{1,0:T(8,128)(2,1)S(1)}, bf16[256,1024]{1,0:T(8,128)(2,1)}, u32[]{:S(2)}, u32[]{:S(2)}) collective-permute-start(bf16[256,1024]{1,0:T(8,128)(2,1)S(1)} %collective-permute-done.10.refs_2_), channel_id=1, source_target_pairs={{0,8},{8,0},{16,24},{24,16},{1,9},{9,1},{17,25},{25,17},{2,10},{10... | collective-permute-start | bytes 1572872 | tf_op jit(solution)/shard_map/ppermute | solution.py:27
  53.3 11.9 %collective-permute-start.16 = (bf16[128,1024]{1,0:T(8,128)(2,1)S(1)}, bf16[128,1024]{1,0:T(8,128)(2,1)S(1)}, u32[]{:S(2)}, u32[]{:S(2)}) collective-permute-start(bf16[128,1024]{1,0:T(8,128)(2,1)S(1)} %collective-permute-done.14.refs_8_.refs_7_), channel_id=1, source_target_pairs={{0,2},{2,4},{4,6},{6,7},{7,5},{5,3},{3,1},{1,0},{8,10},{10,12},{12... | collective-permute-start | bytes 786440 | tf_op jit(solution)/shard_map/ppermute | solution.py:102
  53.6 12.1 %collective-permute-start.17 = (bf16[128,1024]{1,0:T(8,128)(2,1)S(1)}, bf16[128,1024]{1,0:T(8,128)(2,1)S(1)}, u32[]{:S(2)}, u32[]{:S(2)}) collective-permute-start(bf16[128,1024]{1,0:T(8,128)(2,1)S(1)} %collective-permute-done.15.refs_9_.refs_8_), channel_id=1, source_target_pairs={{2,0},{4,2},{6,4},{7,6},{5,7},{3,5},{1,3},{0,1},{10,8},{12,10},{14... | collective-permute-start | bytes 786440 | tf_op jit(solution)/shard_map/ppermute | solution.py:103
  65.3 20.9 %collective-permute-start.18 = (bf16[128,512]{1,0:T(8,128)(2,1)S(1)}, bf16[128,512]{1,0:T(8,128)(2,1)S(1)}, u32[]{:S(2)}, u32[]{:S(2)}) collective-permute-start(bf16[128,512]{1,0:T(8,128)(2,1)S(1)} %slice.76), channel_id=1, source_target_pairs={{0,2},{2,4},{4,6},{6,7},{7,5},{5,3},{3,1},{1,0},{8,10},{10,12},{12... | collective-permute-start | bytes 393224 | tf_op jit(solution)/shard_map/ppermute | solution.py:97
  65.7 20.5 %collective-permute-start.19 = (bf16[128,512]{1,0:T(8,128)(2,1)S(1)}, bf16[128,512]{1,0:T(8,128)(2,1)S(1)}, u32[]{:S(2)}, u32[]{:S(2)}) collective-permute-start(bf16[128,512]{1,0:T(8,128)(2,1)S(1)} %slice.77), channel_id=1, source_target_pairs={{2,0},{4,2},{6,4},{7,6},{5,7},{3,5},{1,3},{0,1},{10,8},{12,10},{14... | collective-permute-start | bytes 393224 | tf_op jit(solution)/shard_map/ppermute | solution.py:98
  118.8 24.4 %collective-permute-start.27 = (bf16[4,128,512]{2,1,0:T(8,128)(2,1)}, bf16[4,128,512]{2,1,0:T(8,128)(2,1)S(1)}, u32[]{:S(2)}, u32[]{:S(2)}) collective-permute-start(bf16[4,128,512]{2,1,0:T(8,128)(2,1)} %dynamic-slice_bitcast_fusion.4), channel_id=1, source_target_pairs={{0,1},{1,0},{2,3},{3,2},{4,5},{5,4},{6,7},{7,6},{8,9},{9,8},{10,11... | collective-permute-start | bytes 1572872 | tf_op jit(solution)/shard_map/ppermute | solution.py:27
  122.9 21.2 %collective-permute-start.28 = (bf16[4,128,512]{2,1,0:T(8,128)(2,1)}, bf16[4,128,512]{2,1,0:T(8,128)(2,1)S(1)}, u32[]{:S(2)}, u32[]{:S(2)}) collective-permute-start(bf16[4,128,512]{2,1,0:T(8,128)(2,1)} %dynamic-slice_bitcast_fusion.3), channel_id=1, source_target_pairs={{0,2},{1,3},{2,0},{3,1},{4,6},{5,7},{6,4},{7,5},{8,10},{9,11},{10,... | collective-permute-start | bytes 1572872 | tf_op jit(solution)/shard_map/ppermute | solution.py:27
  125.3 129.0 %collective-permute-start.25 = (bf16[2,256,1024]{2,1,0:T(8,128)(2,1)}, bf16[2,256,1024]{2,1,0:T(8,128)(2,1)}, u32[]{:S(2)}, u32[]{:S(2)}) collective-permute-start(bf16[2,256,1024]{2,1,0:T(8,128)(2,1)} %dynamic-slice_bitcast_fusion.1), channel_id=1, source_target_pairs={{0,8},{8,0},{16,24},{24,16},{1,9},{9,1},{17,25},{25,17},{2,10},{10... | collective-permute-start | bytes 3145736 | tf_op jit(solution)/shard_map/ppermute | solution.py:27
  174.1 77.5 %collective-permute-start.29 = (bf16[2,256,1024]{2,1,0:T(8,128)(2,1)S(1)}, bf16[2,256,1024]{2,1,0:T(8,128)(2,1)}, u32[]{:S(2)}, u32[]{:S(2)}) collective-permute-start(bf16[2,256,1024]{2,1,0:T(8,128)(2,1)S(1)} %dynamic-slice_bitcast_fusion), channel_id=1, source_target_pairs={{0,8},{8,0},{16,24},{24,16},{1,9},{9,1},{17,25},{25,17},{2,10},{10... | collective-permute-start | bytes 3145736 | tf_op jit(solution)/shard_map/ppermute | solution.py:27
  175.1 12.5 %collective-permute-start.38 = (bf16[2,128,512]{2,1,0:T(8,128)(2,1)S(1)}, bf16[2,128,512]{2,1,0:T(8,128)(2,1)S(1)}, u32[]{:S(2)}, u32[]{:S(2)}) collective-permute-start(bf16[2,128,512]{2,1,0:T(8,128)(2,1)S(1)} %dynamic-slice_bitcast_fusion.7), channel_id=1, source_target_pairs={{0,1},{1,0},{2,3},{3,2},{4,5},{5,4},{6,7},{7,6},{8,9},{9,8},{10,11... | collective-permute-start | bytes 786440 | tf_op jit(solution)/shard_map/ppermute | solution.py:27
  177.2 12.5 %collective-permute-start.36 = (bf16[2,128,512]{2,1,0:T(8,128)(2,1)S(1)}, bf16[2,128,512]{2,1,0:T(8,128)(2,1)S(1)}, u32[]{:S(2)}, u32[]{:S(2)}) collective-permute-start(bf16[2,128,512]{2,1,0:T(8,128)(2,1)S(1)} %dynamic-slice_bitcast_fusion.8), channel_id=1, source_target_pairs={{0,2},{1,3},{2,0},{3,1},{4,6},{5,7},{6,4},{7,5},{8,10},{9,11},{10,... | collective-permute-start | bytes 786440 | tf_op jit(solution)/shard_map/ppermute | solution.py:27
  186.9 37.7 %collective-permute-start.47 = (bf16[4,128,512]{2,1,0:T(8,128)(2,1)S(1)}, bf16[4,128,512]{2,1,0:T(8,128)(2,1)S(1)}, u32[]{:S(2)}, u32[]{:S(2)}) collective-permute-start(bf16[4,128,512]{2,1,0:T(8,128)(2,1)S(1)} %dynamic-slice_bitcast_fusion.2), channel_id=1, source_target_pairs={{0,2},{1,3},{2,0},{3,1},{4,6},{5,7},{6,4},{7,5},{8,10},{9,11},{10,... | collective-permute-start | bytes 1572872 | tf_op jit(solution)/shard_map/ppermute | solution.py:27
  187.6 13.3 %collective-permute-start.33 = (f32[8,2816]{1,0:T(8,128)S(1)}, f32[8,2816]{1,0:T(8,128)S(1)}, u32[]{:S(2)}, u32[]{:S(2)}) collective-permute-start(f32[8,2816]{1,0:T(8,128)S(1)} %add.227), channel_id=1, source_target_pairs={{0,4},{1,5},{2,6},{3,7},{4,0},{5,1},{6,2},{7,3},{8,12},{9,13},{10,... | collective-permute-start | bytes 270344 | tf_op jit(solution)/shard_map/ppermute | solution.py:27
  189.8 13.2 %collective-permute-start.39 = (bf16[1,128,512]{2,1,0:T(8,128)(2,1)S(1)}, bf16[1,128,512]{2,1,0:T(8,128)(2,1)S(1)}, u32[]{:S(2)}, u32[]{:S(2)}) collective-permute-start(bf16[1,128,512]{2,1,0:T(8,128)(2,1)S(1)} %constant_dynamic-slice_fusion.2), channel_id=1, source_target_pairs={{0,4},{1,5},{2,6},{3,7},{4,0},{5,1},{6,2},{7,3},{8,12},{9,13},{10,... | collective-permute-start | bytes 393224 | tf_op jit(solution)/shard_map/ppermute | solution.py:27
  202.3 11.2 %collective-permute-start.44 = (bf16[4,128,384]{2,1,0:T(8,128)(2,1)S(1)}, bf16[4,128,384]{2,1,0:T(8,128)(2,1)S(1)}, u32[]{:S(2)}, u32[]{:S(2)}) collective-permute-start(bf16[4,128,384]{2,1,0:T(8,128)(2,1)S(1)} %dynamic-slice_bitcast_fusion.5), channel_id=1, source_target_pairs={{0,1},{1,0},{2,3},{3,2},{4,5},{5,4},{6,7},{7,6},{8,9},{9,8},{10,11... | collective-permute-start | bytes 1179656 | tf_op jit(solution)/shard_map/ppermute | solution.py:27
  202.9 9.8 %collective-permute-start.37 = (bf16[1,128,512]{2,1,0:T(8,128)(2,1)S(1)}, bf16[1,128,512]{2,1,0:T(8,128)(2,1)S(1)}, u32[]{:S(2)}, u32[]{:S(2)}) collective-permute-start(bf16[1,128,512]{2,1,0:T(8,128)(2,1)S(1)} %constant_dynamic-slice_fusion.3), channel_id=1, source_target_pairs={{0,4},{1,5},{2,6},{3,7},{4,0},{5,1},{6,2},{7,3},{8,12},{9,13},{10,... | collective-permute-start | bytes 393224 | tf_op jit(solution)/shard_map/ppermute | solution.py:27
  217.2 11.3 %collective-permute-start.45 = (bf16[2,128,384]{2,1,0:T(8,128)(2,1)S(1)}, bf16[2,128,384]{2,1,0:T(8,128)(2,1)S(1)}, u32[]{:S(2)}, u32[]{:S(2)}) collective-permute-start(bf16[2,128,384]{2,1,0:T(8,128)(2,1)S(1)} %dynamic-slice_bitcast_fusion.9), channel_id=1, source_target_pairs={{0,2},{1,3},{2,0},{3,1},{4,6},{5,7},{6,4},{7,5},{8,10},{9,11},{10,... | collective-permute-start | bytes 589832 | tf_op jit(solution)/shard_map/ppermute | solution.py:27
  221.6 36.9 %collective-permute-start.41 = (bf16[128,1024]{1,0:T(8,128)(2,1)S(1)}, bf16[128,1024]{1,0:T(8,128)(2,1)S(1)}, u32[]{:S(2)}, u32[]{:S(2)}) collective-permute-start(bf16[128,1024]{1,0:T(8,128)(2,1)S(1)} %pad_maximum_fusion.1.refs_0_), channel_id=1, source_target_pairs={{0,8},{8,0},{16,24},{24,16},{1,9},{9,1},{17,25},{25,17},{2,10},{10... | collective-permute-start | bytes 786440 | tf_op jit(solution)/shard_map/ppermute | solution.py:27
  224.7 18.2 %collective-permute-start.42 = (bf16[128,1024]{1,0:T(8,128)(2,1)S(1)}, bf16[128,1024]{1,0:T(8,128)(2,1)S(1)}, u32[]{:S(2)}, u32[]{:S(2)}) collective-permute-start(bf16[128,1024]{1,0:T(8,128)(2,1)S(1)} %pad_maximum_fusion.1.refs_0_), channel_id=1, source_target_pairs={{0,16},{8,24},{16,0},{24,8},{1,17},{9,25},{17,1},{25,9},{2,18},{10... | collective-permute-start | bytes 786440 | tf_op jit(solution)/shard_map/ppermute | solution.py:27
  242.9 18.6 %collective-permute-start.43 = (bf16[128,1024]{1,0:T(8,128)(2,1)S(1)}, bf16[128,1024]{1,0:T(8,128)(2,1)S(1)}, u32[]{:S(2)}, u32[]{:S(2)}) collective-permute-start(bf16[128,1024]{1,0:T(8,128)(2,1)S(1)} %collective-permute-done.42.refs_2_), channel_id=1, source_target_pairs={{0,8},{8,0},{16,24},{24,16},{1,9},{9,1},{17,25},{25,17},{2,10},{10... | collective-permute-start | bytes 786440 | tf_op jit(solution)/shard_map/ppermute | solution.py:27
  249.0 8.6 %collective-permute-start.51 = (bf16[128,896]{1,0:T(8,128)(2,1)S(1)}, bf16[128,896]{1,0:T(8,128)(2,1)S(1)}, u32[]{:S(2)}, u32[]{:S(2)}) collective-permute-start(bf16[128,896]{1,0:T(8,128)(2,1)S(1)} %pad_maximum_fusion.2.refs_4_), channel_id=1, source_target_pairs={{0,16},{8,24},{16,0},{24,8},{1,17},{9,25},{17,1},{25,9},{2,18},{10... | collective-permute-start | bytes 688136 | tf_op jit(solution)/shard_map/ppermute | solution.py:27
  254.1 15.0 %collective-permute-start.30 = (bf16[1,256,1024]{2,1,0:T(8,128)(2,1)}, bf16[1,256,1024]{2,1,0:T(8,128)(2,1)S(1)}, u32[]{:S(2)}, u32[]{:S(2)}) collective-permute-start(bf16[1,256,1024]{2,1,0:T(8,128)(2,1)} %dynamic-slice_convert_fusion), channel_id=1, source_target_pairs={{0,16},{8,24},{16,0},{24,8},{1,17},{9,25},{17,1},{25,9},{2,18},{10... | collective-permute-start | bytes 1572872 | tf_op jit(solution)/shard_map/ppermute | solution.py:27
  258.4 20.8 %collective-permute-start.26 = (bf16[1,256,1024]{2,1,0:T(8,128)(2,1)}, bf16[1,256,1024]{2,1,0:T(8,128)(2,1)}, u32[]{:S(2)}, u32[]{:S(2)}) collective-permute-start(bf16[1,256,1024]{2,1,0:T(8,128)(2,1)} %dynamic-slice_convert_fusion.1), channel_id=1, source_target_pairs={{0,16},{8,24},{16,0},{24,8},{1,17},{9,25},{17,1},{25,9},{2,18},{10... | collective-permute-start | bytes 1572872 | tf_op jit(solution)/shard_map/ppermute | solution.py:27
  (74 other events, 887.7 us)

commit v3 on v2

--- a/solution.py
+++ b/solution.py
@@ -12,8 +12,11 @@
 f32 = jnp.float32
 norm_eps = 1e-05
 LANES = 128
+SEQ = "seq"
+SHARD = "shard"
 CHUNK = 128
 HALO = 8
+CONV, HEAD, GAIN, NORM = range(4)
 FRONT_PIECES = 4
 BACK_PIECES = 2
 
@@ -28,19 +31,19 @@
 
 
 def seq_gather(block):
-    n = lax.axis_size("seq")
+    n = lax.axis_size(SEQ)
     blocks = {0: block}
     d = n // 2
     while d >= 1:
         for o in list(blocks):
-            blocks[o ^ d] = swap(blocks[o], "seq", d)
+            blocks[o ^ d] = swap(blocks[o], SEQ, d)
         d //= 2
     return [blocks[o] for o in range(n)]
 
 
 def seq_scatter(parts):
-    n = lax.axis_size("seq")
-    me = lax.axis_index("seq")
+    n = lax.axis_size(SEQ)
+    me = lax.axis_index(SEQ)
     d = 1
     while d < n:
         m = parts.shape[0]
@@ -48,9 +51,11 @@
         bit = (me // d) % 2
         keep = lax.dynamic_index_in_dim(pairs, bit, 1, keepdims=False)
         send = lax.dynamic_index_in_dim(pairs, 1 - bit, 1, keepdims=False)
-        got = swap(send.astype(bf16), "seq", d)
+        got = swap(send.astype(bf16), SEQ, d)
         parts = keep.astype(f32) + got.astype(f32)
         d *= 2
+        if d < n:
+            parts = parts.astype(bf16)
     return parts[0]
 
 
@@ -81,12 +86,12 @@
 
 class RingGather:
     def __init__(self, block, cut):
-        n = lax.axis_size("shard")
+        n = lax.axis_size(SHARD)
         self.n, self.cut, self.hop = n, cut, 0
         self.ahead, self.back = ring_routes(n)
-        self.place = ring_place(lax.axis_index("shard"), n)
+        self.place = ring_place(lax.axis_index(SHARD), n)
         self.a = self.b = block
-        self.found = [(block, lax.axis_index("shard"), 0)]
+        self.found = [(block, lax.axis_index(SHARD), 0)]
 
     def step(self):
         if self.hop == self.n // 2:
@@ -94,13 +99,13 @@
         self.hop += 1
         k, n = self.hop, self.n
         if k == n // 2:
-            self.a = lax.ppermute(self.a[:, : self.cut], "shard", self.ahead)
-            self.b = lax.ppermute(self.b[:, self.cut :], "shard", self.back)
+            self.a = lax.ppermute(self.a[:, : self.cut], SHARD, self.ahead)
+            self.b = lax.ppermute(self.b[:, self.cut :], SHARD, self.back)
             owner = ring_index(self.place - k, n)
             self.found += [(self.a, owner, 0), (self.b, owner, self.cut)]
         else:
-            self.a = lax.ppermute(self.a, "shard", self.ahead)
-            self.b = lax.ppermute(self.b, "shard", self.back)
+            self.a = lax.ppermute(self.a, SHARD, self.ahead)
+            self.b = lax.ppermute(self.b, SHARD, self.back)
             self.found.append((self.a, ring_index(self.place - k, n), 0))
             self.found.append((self.b, ring_index(self.place + k, n), 0))
         return [self.a, self.b]
@@ -119,22 +124,34 @@
 
 
 class Halving:
-    def __init__(self, slabs):
-        self.slabs = list(slabs)
-        self.orders = bit_orders(lax.axis_size("shard"))
+    def __init__(self, halves, rider=None):
+        self.halves = list(halves)
+        self.slabs = [None] * len(self.halves)
+        self.orders = bit_orders(lax.axis_size(SHARD))
         self.hop = 0
+        self.rider = rider
 
     def step(self):
         if self.hop == len(self.orders[0]):
             return []
-        me = lax.axis_index("shard")
+        me = lax.axis_index(SHARD)
         for i, slab in enumerate(self.slabs):
             b = self.orders[i][self.hop]
-            pair = slab.reshape((2, slab.shape[0] // 2) + slab.shape[1:])
-            bit = (me >> b) & 1
-            keep = lax.dynamic_index_in_dim(pair, bit, 0, keepdims=False)
-            send = lax.dynamic_index_in_dim(pair, 1 - bit, 0, keepdims=False)
-            got = swap(send, "shard", 1 << b)
+            if slab is None:
+                keep, send = self.halves[i]
+            else:
+                pair = slab.reshape((2, slab.shape[0] // 2) + slab.shape[1:])
+                bit = (me >> b) & 1
+                keep = lax.dynamic_index_in_dim(pair, bit, 0, keepdims=False)
+                send = lax.dynamic_index_in_dim(pair, 1 - bit, 0, keepdims=False)
+                if i == 0 and self.rider is not None:
+                    flat = send.reshape(-1, send.shape[2])
+                    send = jnp.concatenate([flat, self.rider], axis=0)
+            got = swap(send, SHARD, 1 << b)
+            if i == 0 and self.rider is not None:
+                rows = keep.shape[0] * keep.shape[1]
+                self.rider = two_parts(joined(got[rows:]) + joined(self.rider))
+                got = got[:rows].reshape(keep.shape)
             self.slabs[i] = (keep.astype(f32) + got.astype(f32)).astype(bf16)
         self.hop += 1
         return self.slabs
@@ -143,6 +160,21 @@
         while self.step():
             pass
         return [s[0] for s in self.slabs]
+
+
+def two_parts(x):
+    high = lax.reduce_precision(x, 8, 7)
+    return jnp.concatenate([high.astype(bf16), (x - high).astype(bf16)], axis=0)
+
+
+def joined(parts):
+    n = parts.shape[0] // 2
+    return parts[:n].astype(f32) + parts[n:].astype(f32)
+
+
+def put(halves, shard, owner, bits, value, at=slice(None)):
+    half = ((shard >> bits[0]) & 1) ^ ((owner >> bits[0]) & 1)
+    halves[half, slot(owner, bits[1:]), :, at] = value
 
 
 def sigmoid(v):
@@ -364,7 +396,7 @@
     lane = lax.broadcasted_iota(jnp.int32, (size, LANES), 1)
     z = dot(normed[...], wz[...], 1, 0)
     dg = dot(cotan[pl.ds(pl.multiple_of(step * size, size), size), :], wo[...], 1, 1)
-    v = conv_out[...]
+    v = conv_out[...].astype(f32)
     mixed = scan_out[...] + skip * (v * sigmoid(v))
     gi = mixed * (z * sigmoid(z))
     gate[...] = z
@@ -411,7 +443,9 @@
 def turn_kernel(dims, ids, *refs):
     cols, inner, _, _ = dims
     gate, mixed_in, d_gated, sums, gain_all, normed, cotan, w_o = refs[:8]
-    gated, d_gate, d_mixed, gain_grad, out_part, z_slab, o_slab = refs[8:]
+    w_z = refs[8]
+    gated, d_gate, d_mixed, gain_grad, out_part, norm_z = refs[9:15]
+    outs, halves = refs[15:19], refs[19:]
     step = pl.program_id(0)
     gain = own_columns(gain_all, ids[0], cols, inner)
 
@@ -424,11 +458,11 @@
     stat = jnp.transpose(sums[...])
     scale = lax.rsqrt(stat[:, 0:1] / inner + norm_eps)
     slope = scale * scale * scale * (stat[:, 1:2] / inner)
-    z = gate[...]
+    z = gate[...].astype(f32)
     sig = sigmoid(z)
-    mixed = mixed_in[...]
+    mixed = mixed_in[...].astype(f32)
     gi = mixed * (z * sig)
-    dg = d_gated[...]
+    dg = d_gated[...].astype(f32)
     scaled = gi * scale
     gated_c = (scaled * gain).astype(bf16)
     gated[at, :] = gated_c
@@ -440,13 +474,14 @@
 
     @pl.when(step == pl.num_programs(0) - 1)
     def _():
-        turn_slabs(dims, gated, d_gate, normed, cotan, z_slab, o_slab)
-
-
-def turn_slabs(dims, gated, d_gate, normed, cotan, z_slab, o_slab):
+        turn_slabs(dims, ids[1], gated, d_gate, normed, cotan, w_z, norm_z, *halves)
+        hand_over(halves, outs)
+
+
+def turn_slabs(dims, shard, gated, d_gate, normed, cotan, w_z, norm_z, z_halves, o_halves):
     cols, _, shards, deep = dims
     first, second = bit_orders(shards)
-    rows_slab(normed, d_gate[...], z_slab, None, deep, first, None, 0)
+    rows_slab(shard, normed, d_gate[...], z_halves, None, deep, first, None, 0, w_z, norm_z)
     model = cotan.shape[1]
     strip = cols // 2
     bands = shards * strip // model
@@ -457,51 +492,88 @@
             part = dot(left, cotan[:, a * strip : (a + 1) * strip], 0, 0).astype(bf16)
             for i in range(size // deep):
                 r, t = divmod(g * size // deep + i, 2)
-                o_slab[slot(a * bands + r, second), :, t * strip : (t + 1) * strip] = part[
-                    i * deep : (i + 1) * deep, :
-                ]
-
-
-def rows_slab(left, right, a_slab, b_slab, deep, first, second, cut):
+                value = part[i * deep : (i + 1) * deep, :]
+                at = slice(t * strip, (t + 1) * strip)
+                put(o_halves, shard, a * bands + r, second, value, at)
+
+
+def rows_slab(shard, left, right, a_halves, b_halves, deep, first, second, cut, weight, norms):
     size = max(deep, LANES)
     for g in range(left.shape[1] // size):
-        part = dot(left[:, g * size : (g + 1) * size], right, 0, 0).astype(bf16)
+        at = slice(g * size, (g + 1) * size)
+        full = dot(left[:, at], right, 0, 0)
+        along = jnp.sum(full * weight[at, :].astype(f32), axis=1, keepdims=True)
+        norms[:, at] = jnp.transpose(jnp.broadcast_to(along, (size, LANES)))[:8, :]
+        part = full.astype(bf16)
         for i in range(size // deep):
             owner = g * size // deep + i
             mine = part[i * deep : (i + 1) * deep, :]
-            if b_slab is None:
-                a_slab[slot(owner, first)] = mine
+            if b_halves is None:
+                put(a_halves, shard, owner, first, mine)
             else:
-                a_slab[slot(owner, first)] = mine[:, :cut]
-                b_slab[slot(owner, second)] = mine[:, cut:]
-
-
-def weight_kernel(dims, normed, d_proj, a_slab, b_slab):
-    shards, deep, cut = dims
+                put(a_halves, shard, owner, first, mine[:, :cut])
+                put(b_halves, shard, owner, second, mine[:, cut:])
+
+
+def hand_over(halves, outs):
+    for i, half in enumerate(halves):
+        outs[2 * i][...] = half[0]
+        sent = outs[2 * i + 1]
+        if len(sent.shape) == 2:
+            rows = half.shape[2]
+            for j in range(half.shape[1]):
+                sent[j * rows : (j + 1) * rows, :] = half[1, j]
+        else:
+            sent[...] = half[1]
+
+
+def small_tiles(width, conv_cols, cols, model):
+    found = [(CONV, k, c) for k in range(width + 1) for c in range(0, conv_cols, LANES)]
+    found += [(HEAD, k, 0) for k in range(3)]
+    found += [(GAIN, 0, c) for c in range(0, cols, LANES)]
+    return found + [(NORM, 0, c) for c in range(0, model, LANES)]
+
+
+def rider_rows(tiles, cut):
+    rows = -(-tiles // (cut // LANES))
+    return -(-rows // 16) * 16
+
+
+def weight_kernel(dims, ids, normed, d_proj, w_one, gain, norm_z, conv, head, inner_gain, *refs):
+    shards, deep, cut, width = dims
+    outs, rider = refs[:4], refs[4]
+    halves, norms, packed = refs[5:7], refs[7], refs[8]
     first, second = bit_orders(shards)
-    rows_slab(normed, d_proj[...], a_slab, b_slab, deep, first, second, cut)
-
-
-def entry_kernel(d_proj, d_gate, w_one, w_z, normed, gain, after, d_normed, norm_grad):
-    step = pl.program_id(0)
-
-    @pl.when(step == 0)
-    def _():
-        norm_grad[...] = jnp.zeros_like(norm_grad)
-
+    rows_slab(
+        ids[1], normed, d_proj[...], *halves, deep, first, second, cut, w_one, norms
+    )
+    norm = (norms[0:1, :] + norm_z[0:1, :]) / gain[...]
+    packed[...] = jnp.zeros_like(packed)
+    per = cut // LANES
+    kinds = {CONV: conv, HEAD: head, GAIN: inner_gain}
+    tiles = small_tiles(width, conv.shape[1], inner_gain.shape[1], normed.shape[1])
+    for i, (kind, r, c) in enumerate(tiles):
+        tile = norm[:, c : c + LANES] if kind == NORM else kinds[kind][r : r + 1, c : c + LANES]
+        at = (i % per) * LANES
+        packed[i // per : i // per + 1, at : at + LANES] = tile
+    high = packed[...].astype(bf16)
+    n = high.shape[0]
+    rider[:n, :] = high
+    rider[n:, :] = (packed[...] - high.astype(f32)).astype(bf16)
+    hand_over(halves, outs)
+    sent = outs[1]
+    sent[sent.shape[0] - rider.shape[0] :, :] = rider[...]
+
+
+def entry_kernel(d_proj, d_gate, w_one, w_z, after, d_normed):
     part = dot(d_proj[...], w_one[...], 1, 1) + dot(d_gate[...], w_z[...], 1, 1)
     d_normed[...] = part.astype(bf16)
-    norm_grad[...] += jnp.sum(part * normed[...].astype(f32), axis=0, keepdims=True)
-
-    @pl.when(step == pl.num_programs(0) - 1)
-    def _():
-        norm_grad[...] = norm_grad[...] / gain[...]
 
 
 def finish_kernel(dims, ids, *refs):
-    cols, state, heads, n_seq = dims
+    cols, state, heads, n_seq, cut, width = dims
     zo, one = refs[:n_seq], refs[n_seq : 2 * n_seq]
-    in_grad, out_grad = refs[2 * n_seq :]
+    in_grad, out_grad, conv_w, conv_b, dt_bias, a_log, skip, gain, norm = refs[2 * n_seq :]
     inner = cols * n_seq
     strip = cols // 2
     deep = in_grad.shape[1]
@@ -513,28 +585,57 @@
         block = pl.ds(pl.multiple_of(q * cols, LANES), cols)
         in_grad[block, :] = jnp.transpose(zo[o][:, :cols].astype(f32))
         block = pl.ds(pl.multiple_of(inner + q * cols, LANES), cols)
-        in_grad[block, :] = jnp.transpose(one[o][:, :cols].astype(f32))
-        band = one[o][:, cols:conv_cols].astype(f32)
+        in_grad[block, :] = jnp.transpose(one[o][:deep, :cols].astype(f32))
+        band = one[o][:deep, cols:conv_cols].astype(f32)
         shared = band if shared is None else shared + band
-        turned = pltpu.roll(one[o][:, conv_cols:].astype(f32), q * heads, 1)
+        turned = pltpu.roll(one[o][:deep, conv_cols:].astype(f32), q * heads, 1)
         steps = turned if steps is None else steps + turned
         block = pl.ds(pl.multiple_of(q * strip, LANES), strip)
         out_grad[:deep, block] = zo[o][:, cols : cols + strip].astype(f32)
         out_grad[deep:, block] = zo[o][:, cols + strip :].astype(f32)
     in_grad[2 * inner : 2 * inner + 2 * state, :] = jnp.transpose(shared)
     in_grad[2 * inner + 2 * state :, :] = jnp.transpose(steps)[: heads * n_seq, :]
+    riders = [joined(ref[deep:, :cut]) for ref in one]
+    per = cut // LANES
+    table = {HEAD: (dt_bias, a_log, skip)}
+    for i, (kind, r, c) in enumerate(small_tiles(width, conv_cols, cols, norm.shape[1])):
+        row, at = i // per, (i % per) * LANES
+        pieces = [x[row : row + 1, at : at + LANES] for x in riders]
+        if kind == NORM:
+            norm[:, c : c + LANES] = sum(pieces)
+        elif kind == HEAD:
+            rolled = [
+                pltpu.roll(jnp.broadcast_to(x, (8, LANES)), (ids[0] ^ o) * heads, 1)
+                for o, x in enumerate(pieces)
+            ]
+            table[kind][r][...] = sum(rolled)[0:1, : heads * n_seq]
+        elif kind == CONV and c >= cols:
+            place = slice(inner + c - cols, inner + c - cols + LANES)
+            if r < width:
+                conv_w[r : r + 1, place] = sum(pieces)
+            else:
+                conv_b[:, place] = sum(pieces)
+        else:
+            for o, x in enumerate(pieces):
+                place = pl.ds(pl.multiple_of((ids[0] ^ o) * cols + c, LANES), LANES)
+                if kind == GAIN:
+                    gain[:, place] = x
+                elif r < width:
+                    conv_w[r : r + 1, place] = x
+                else:
+                    conv_b[:, place] = x
 
 
 def back_kernel(dims, *refs):
-    hd, heads, cols, state, inner = dims
-    ids, conv_in, conv_out, dt_raw, scan_out, states, d_mixed, conv_w_all, table, picks = refs[:10]
+    hd, heads, cols, state, inner, fresh = dims
+    ids, conv_in, conv_out, dt_raw, scan_out, states, d_mixed, conv_w_all, table = refs[:9]
     d_proj, held, halo, conv_grad, head_grad = refs[-5:]
     conv_cols = cols + 2 * state
 
     @pl.when(pl.program_id(0) == 0)
     def _():
-        for start, carried in zip(refs[10:14], (held, halo, conv_grad, head_grad)):
-            carried[...] = start[...]
+        for i, carried in enumerate((held, halo, conv_grad, head_grad)):
+            carried[...] = jnp.zeros_like(carried) if fresh else refs[9 + i][...]
 
     conv_w = own_columns(conv_w_all, ids[0], cols, inner)
     width = conv_w.shape[0]
@@ -547,12 +648,16 @@
     upper = jnp.where(row <= col, 1.0, 0.0).astype(bf16)
     per = LANES // hd
     chunks = conv_in.shape[0] // CHUNK
+    channel = lax.broadcasted_iota(jnp.int32, (cols, LANES), 0)
+    head = lax.broadcasted_iota(jnp.int32, (cols, LANES), 1)
+    mine = (channel >= head * hd) & (channel < (head + 1) * hd)
+    picks = jnp.where(mine, 1.0, 0.0).astype(bf16)
 
     @pl.loop(0, chunks)
     def _(turn):
         c = chunks - 1 - turn
         at = pl.ds(pl.multiple_of(c * CHUNK, CHUNK), CHUNK)
-        v = conv_out[at, :]
+        v = conv_out[at, :].astype(f32)
         sig = sigmoid(v)
         active = v * sig
         raw = dt_raw[at, :]
@@ -606,7 +711,7 @@
             jnp.sum(dm * x, axis=0, keepdims=True),
             jnp.where(first_row == 1, jnp.sum(carried, axis=0, keepdims=True), 0.0),
         )
-        by_head = exact(jnp.concatenate([change, x * d_xd, sums], axis=0), picks[...], 1, 0)
+        by_head = exact(jnp.concatenate([change, x * d_xd, sums], axis=0), picks, 1, 0)
         change_h = by_head[:CHUNK]
         step_h = by_head[CHUNK : 2 * CHUNK]
         skip_h = by_head[2 * CHUNK : 2 * CHUNK + 1]
@@ -661,9 +766,9 @@
     out_weight,
     out_grad,
 ):
-    n_seq = lax.axis_size("seq")
-    n_shard = lax.axis_size("shard")
-    me = lax.axis_index("seq")
+    n_seq = lax.axis_size(SEQ)
+    n_shard = lax.axis_size(SHARD)
+    me = lax.axis_index(SEQ)
     own = hidden_in[0]
     cotan_own = out_grad[0]
     rows, model = own.shape
@@ -702,7 +807,7 @@
     ]
     out_rows = out_weight.shape[0]
     sent = columns(out_weight, me * strip, strip)
-    tile = lax.ppermute(sent, ("seq", "shard"), route)
+    tile = lax.ppermute(sent, (SEQ, SHARD), route)
     slab_two = jnp.concatenate(
         [columns(in_weight, me * cols, cols), tile[:deep], tile[deep:]], axis=1
     )
@@ -723,13 +828,10 @@
     cot_blocks = seq_gather(cotan_b)
     ring_two = RingGather(slab_two, cols)
 
-    ids = jnp.stack([me, lax.axis_index("shard")]).astype(jnp.int32)
+    ids = jnp.stack([me, lax.axis_index(SHARD)]).astype(jnp.int32)
     table = jnp.pad(
         jnp.stack([dt_bias, a_log, skip]), ((0, 5), (0, LANES - heads_all))
     )
-    picks = jnp.where(jnp.arange(cols)[:, None] // hd == jnp.arange(LANES)[None, :], 1.0, 0.0)
-    picks = picks.astype(bf16)
-
     n_one = len(ring_one)
     per_block = rows // CHUNK
     steps = n_seq // FRONT_PIECES
@@ -757,7 +859,7 @@
     dims = (hd, heads, cols, state, inner, n_seq, n_shard, cut_one)
     tokens, w_one, *rest = pl.pallas_call(
         functools.partial(front_kernel, dims + (None,)),
-        name="front_0",
+        name="f0",
         grid=(steps,),
         in_specs=[SMEM] + [ANY] * (n_seq + n_one) + [VMEM] * 4,
         out_specs=[VMEM] * 2 + [part(block, 0) for _, block in kept] + [VMEM] * 2,
@@ -828,32 +930,34 @@
         inner_gain[None],
     )
 
-    sums = all_sum(sums, "seq")
-    _, d_gate, d_mixed, gain_part, out_part, z_slab, o_slab = pl.pallas_call(
+    sums = all_sum(sums, SEQ)
+    gated, d_gate, d_mixed, gain_part, out_part, norm_z, *halves = pl.pallas_call(
         functools.partial(turn_kernel, (cols, inner, n_shard, deep)),
         name="turn",
         grid=(n_seq,),
         in_specs=[SMEM]
         + [stream(cols)] * 3
         + [pl.BlockSpec((8, rows), lambda i: (0, i))]
-        + [VMEM] * 4,
-        out_specs=[VMEM, VMEM, stream(cols), VMEM, stream(model), VMEM, VMEM],
+        + [VMEM] * 5,
+        out_specs=[VMEM, VMEM, stream(cols), VMEM, stream(model)] + [VMEM] * 5,
         out_shape=[
             shaped((length, cols), bf16),
             shaped((length, cols), bf16),
             shaped((length, cols), f32),
             shaped((1, cols), f32),
             shaped((length, model), bf16),
-            shaped((n_shard, deep, cols), bf16),
-            shaped((n_shard, deep, cols), bf16),
-        ],
+            shaped((8, model), f32),
+        ]
+        + [shaped((n_shard // 2, deep, cols), bf16)] * 4,
+        scratch_shapes=[pltpu.VMEM((2, n_shard // 2, deep, cols), bf16)] * 2,
         cost_estimate=pl.CostEstimate(
             flops=6 * length * cols * model, bytes_accessed=30 * length * cols, transcendentals=0
         ),
-    )(ids, gate, mixed, d_gated, sums, inner_gain[None], normed, cotan, w_o)
-
-    halving = Halving((z_slab, o_slab))
-    carry = [jnp.zeros(s, f32) for s in ((cols, state), (HALO, conv_cols), (8, conv_cols), (8, LANES))]
+    )(ids, gate, mixed, d_gated, sums, inner_gain[None], normed, cotan, w_o, w_z)
+
+    halving = Halving((halves[:2], halves[2:]))
+    carry = []
+    carry_shapes += [shaped((8, conv_cols), f32), shaped((8, LANES), f32)]
     hops = max(1, n_bits // BACK_PIECES)
     steps = n_seq // BACK_PIECES
     d_proj = None
@@ -865,16 +969,16 @@
         extra = list(arrived) + ([] if d_proj is None else [d_proj])
         last = (j + 1) * steps - 1
         d_proj, *carry = pl.pallas_call(
-            functools.partial(back_kernel, (hd, heads, cols, state, inner)),
+            functools.partial(back_kernel, (hd, heads, cols, state, inner, d_proj is None)),
             grid=(steps,),
             in_specs=[SMEM]
             + [part(block, last, -1) for _, block in kept[1:]]
             + [part((rows, cols), last, -1)]
-            + [VMEM] * 7
+            + [VMEM] * (2 + len(carry))
             + [ANY] * len(extra),
             out_specs=[part((rows, one), last, -1)] + [VMEM] * 4,
-            out_shape=[shaped((length, one), bf16)] + [shaped(c.shape, f32) for c in carry],
-            input_output_aliases={} if d_proj is None else {13 + len(extra): 0},
+            out_shape=[shaped((length, one), bf16)] + carry_shapes,
+            input_output_aliases={} if d_proj is None else {12 + len(extra): 0},
             cost_estimate=pl.CostEstimate(
                 flops=steps * 20 * rows * CHUNK * cols,
                 bytes_accessed=steps * 14 * rows * model,
@@ -890,52 +994,73 @@
             d_mixed,
             conv_weight,
             table,
-            picks,
             *carry,
             *extra,
         )
     conv_part, head_part = carry[2:]
-    a_slab, b_slab = pl.pallas_call(
-        functools.partial(weight_kernel, (n_shard, deep, cut_one)),
+    n_rider = 2 * rider_rows(len(small_tiles(width, conv_cols, cols, model)), cut_one)
+    half = n_shard // 2
+    *halves, rider = pl.pallas_call(
+        functools.partial(weight_kernel, (n_shard, deep, cut_one, width)),
         name="weight",
-        in_specs=[VMEM] * 2,
-        out_specs=[VMEM] * 2,
+        in_specs=[SMEM] + [VMEM] * 8,
+        out_specs=[VMEM] * 5,
         out_shape=[
-            shaped((n_shard, deep, cut_one), bf16),
-            shaped((n_shard, deep, one - cut_one), bf16),
+            shaped((half, deep, cut_one), bf16),
+            shaped((half * deep + n_rider, cut_one), bf16),
+            shaped((half, deep, one - cut_one), bf16),
+            shaped((half, deep, one - cut_one), bf16),
+            shaped((n_rider, cut_one), bf16),
+        ],
+        scratch_shapes=[
+            pltpu.VMEM((2, half, deep, cut_one), bf16),
+            pltpu.VMEM((2, half, deep, one - cut_one), bf16),
+            pltpu.VMEM((8, model), f32),
+            pltpu.VMEM((n_rider // 2, cut_one), f32),
         ],
         cost_estimate=pl.CostEstimate(
             flops=2 * length * model * one, bytes_accessed=6 * length * model, transcendentals=0
         ),
-    )(normed, d_proj)
-    one_own = Halving((a_slab, b_slab)).finish()
-    one_all = seq_gather(jnp.concatenate(one_own, axis=1))
+    )(ids, normed, d_proj, w_one, norm_gain[None], norm_z, conv_part, head_part, gain_part)
+    grads = Halving((halves[:2], halves[2:]), rider)
+    one_own = jnp.concatenate(grads.finish(), axis=1)
+    rider = jnp.pad(grads.rider, ((0, 0), (0, one - cut_one)))
+    one_all = seq_gather(jnp.concatenate([one_own, rider], axis=0))
 
     z_own, o_own = halving.finish()
-    o_own = lax.ppermute(o_own, ("seq", "shard"), [(b, a) for a, b in route])
+    o_own = lax.ppermute(o_own, (SEQ, SHARD), [(b, a) for a, b in route])
     zo_all = seq_gather(jnp.concatenate([z_own, o_own], axis=1))
-    in_weight_grad, out_weight_grad = pl.pallas_call(
-        functools.partial(finish_kernel, (cols, state, heads, n_seq)),
+    in_weight_grad, out_weight_grad, conv_w_grad, *rows_out = pl.pallas_call(
+        functools.partial(finish_kernel, (cols, state, heads, n_seq, cut_one, width)),
         name="finish",
         in_specs=[SMEM] + [VMEM] * (2 * n_seq),
-        out_specs=[VMEM] * 2,
-        out_shape=[shaped((in_weight.shape[1], deep), f32), shaped((out_rows, model), f32)],
+        out_specs=[VMEM] * 9,
+        out_shape=[
+            shaped((in_weight.shape[1], deep), f32),
+            shaped((out_rows, model), f32),
+            shaped((width, conv_dim), f32),
+            shaped((1, conv_dim), f32),
+            *[shaped((1, heads_all), f32)] * 3,
+            shaped((1, inner), f32),
+            shaped((1, model), f32),
+        ],
     )(ids, *zo_all, *one_all)
     in_weight_grad = in_weight_grad.T
 
-    block_out = own.astype(f32) + seq_scatter(out_part.reshape(n_seq, rows, model))
-
-    d_normed, norm_part = pl.pallas_call(
+    out_sum = seq_scatter(out_part.reshape(n_seq, rows, model))
+    block_out = own.astype(f32) + out_sum
+
+    d_normed = pl.pallas_call(
         entry_kernel,
-        name="entry",
+        name="e",
         grid=(n_seq,),
-        in_specs=[stream(one), stream(cols), VMEM, VMEM, stream(model), VMEM, ANY],
-        out_specs=[stream(model), VMEM],
-        out_shape=[shaped((length, model), bf16), shaped((1, model), f32)],
+        in_specs=[stream(one), stream(cols), VMEM, VMEM, ANY],
+        out_specs=stream(model),
+        out_shape=shaped((length, model), bf16),
         cost_estimate=pl.CostEstimate(
             flops=3 * length * model * one, bytes_accessed=10 * length * model, transcendentals=0
         ),
-    )(d_proj, d_gate, w_one, w_z, normed, norm_gain[None], a_slab)
+    )(d_proj, d_gate, w_one, w_z, halves[0])
     d_own = seq_scatter(d_normed.reshape(n_seq, rows, model))
     own_f = own.astype(f32)
     rstat = lax.rsqrt(jnp.mean(own_f * own_f, axis=-1, keepdims=True) + norm_eps)
@@ -943,43 +1068,25 @@
     along = jnp.mean(scaled * own_f, axis=-1, keepdims=True)
     input_grad = cotan_own + rstat * scaled - own_f * rstat * rstat * rstat * along
 
-    def placed(array, size, start):
-        wide = jnp.zeros((array.shape[0], size), f32)
-        return lax.dynamic_update_slice_in_dim(wide, array, start, axis=1)
-
-    packed = jnp.concatenate(
-        [
-            placed(conv_part[:, :cols], inner, me * cols),
-            conv_part[:, cols:],
-            placed(head_part[:, :heads], LANES, me * heads),
-            placed(gain_part, inner, me * cols).reshape(8, -1),
-            norm_part.reshape(8, -1),
-        ],
-        axis=1,
-    )
-    packed = all_sum(all_sum(packed, "shard"), "seq")
-    head_all = packed[:, conv_dim : conv_dim + heads_all]
-    gain_at = conv_dim + LANES
-    gain_all = packed[:, gain_at : gain_at + inner // 8].reshape(-1)
-    norm_all = packed[:, gain_at + inner // 8 :].reshape(-1)
+    conv_b_grad, dt_grad, a_log_grad, skip_grad, gain_grad, norm_grad = (r[0] for r in rows_out)
     return (
         block_out[None],
         input_grad[None],
-        norm_all,
+        norm_grad,
         in_weight_grad,
-        packed[:width, :conv_dim],
-        packed[width, :conv_dim],
-        head_all[0],
-        head_all[1],
-        head_all[2],
-        gain_all,
+        conv_w_grad,
+        conv_b_grad,
+        dt_grad,
+        a_log_grad,
+        skip_grad,
+        gain_grad,
         out_weight_grad,
     )
 
 
 def solution(mesh):
-    tokens = P("shard", "seq", None)
-    rows = P("shard", None)
+    tokens = P(SHARD, SEQ, None)
+    rows = P(SHARD, None)
 
     return jax.shard_map(
         body,

time: 284 us -> 265 us (0.933)
  waiting for transfers between devices: 97.2 us -> 89.5 us
  local copies, waits for them, and re-layouts: 20.9 us -> 14.1 us
    ppermute x35 -> x30, waiting for transfers between devices: 69 us -> 62.3 us  [swap(): return lax.ppermute(block, axis, [(i, i ^ distance) for i in range(n)])]
    squeeze x12 -> x6, local copies, waits for them, and re-layouts: 4.13 us -> 0.12 us  [step(): send = lax.dynamic_index_in_dim(pair, 1 - bit, 0, keepdims=False)]
    ppermute x35 -> x30, starting transfers between devices: 33.3 us -> 30 us  [swap(): return lax.ppermute(block, axis, [(i, i ^ distance) for i in range(n)])]
    add x2 -> x0, other arithmetic: 3.21 us -> none  [seq_scatter(): parts = keep.astype(f32) + got.astype(f32)]
    squeeze x2 -> x4, local copies, waits for them, and re-layouts: 2.49 us -> 5.37 us  [seq_scatter(): send = lax.dynamic_index_in_dim(pairs, 1 - bit, 1, keepdims=False)]
  transfers between devices with their start and end apart: 53 -> 48, of which waited for: 26 -> 21; matrix products, arithmetic and copies ran while one was open for 8% -> 6% of each run, Pallas kernels for 26% -> 28%
where the time goes in v3:
time: 265 us; the launch traced here: 264 us
  Pallas kernels  96.6 us (36%)
  waiting for transfers between devices  89.5 us (34%)
  starting transfers between devices  50.5 us (19%)
  local copies, waits for them, and re-layouts  14.1 us (5%)
  other arithmetic  12.3 us (5%)
    ppermute x30, waiting for transfers between devices, swap(): return lax.ppermute(block, axis, [(i, i ^ distance) for i in range(n)])  62.3 us
    ppermute x30, starting transfers between devices, swap(): return lax.ppermute(block, axis, [(i, i ^ distance) for i in range(n)])  30 us
    pallas_call x2, Pallas kernels, body(): pl.pallas_call(functools.partial(back_kernel, (hd, heads, cols, state, in...  28.6 us
    pallas_call x3, Pallas kernels, body(): pl.pallas_call(functools.partial(front_kernel, dims + (n_skip,)), grid=(s...  18.5 us
    ppermute x6, waiting for transfers between devices, step(): self.a = lax.ppermute(self.a, SHARD, self.ahead)  14.6 us
    pallas_call x1, Pallas kernels, body(): pl.pallas_call(functools.partial(turn_kernel, (cols, inner, n_shard, deep...  13 us
    pallas_call x1, Pallas kernels, body(): pl.pallas_call(functools.partial(gate_kernel, (cols, heads, hd, n_seq, n_...  10.5 us
    ppermute x6, waiting for transfers between devices, step(): self.b = lax.ppermute(self.b, SHARD, self.back)  9.51 us
  transfers between devices with their start and end apart: 48, of which 21 were waited for; matrix products, arithmetic and copies ran while one was open for 6% of the time, Pallas kernels for 28%

profile of v3, /device:TPU:0, one launch (start us, length us, event | category | flops | bytes accessed | tf_op | source)
XLA Modules:
  0.0 264.4 jit_solution(7739570000164023421)
XLA Ops:
  3.7 3.1 %collective-permute-start.1 = (bf16[128,896]{1,0:T(8,128)(2,1)S(1)}, bf16[128,896]{1,0:T(8,128)(2,1)S(1)}, u32[]{:S(2)}, u32[]{:S(2)}) collective-permute-start(bf16[128,896]{1,0:T(8,128)(2,1)S(1)} %fusion.14.refs_4_), channel_id=1, source_target_pairs={{0,2},{2,4},{4,6},{6,7},{7,5},{5,3},{3,1},{1,0},{8,10},{10,12},{12... | collective-permute-start | bytes 688136 | tf_op jit(solution)/shard_map/ppermute | solution.py:107
  7.4 5.0 %collective-permute-done.1.refs_5_ = bf16[128,896]{1,0:T(8,128)(2,1)S(1)} collective-permute-done((bf16[128,896]{1,0:T(8,128)(2,1)S(1)}, bf16[128,896]{1,0:T(8,128)(2,1)S(1)}, u32[]{:S(2)}, u32[]{:S(2)}) %collective-permute-start.1) | collective-permute-done | bytes 229408 | tf_op jit(solution)/shard_map/ppermute | solution.py:107
  21.4 9.3 %collective-permute-done.7.refs_10_ = bf16[128,896]{1,0:T(8,128)(2,1)S(1)} collective-permute-done((bf16[128,896]{1,0:T(8,128)(2,1)S(1)}, bf16[128,896]{1,0:T(8,128)(2,1)S(1)}, u32[]{:S(2)}, u32[]{:S(2)}) %collective-permute-start.7) | collective-permute-done | bytes 229408 | tf_op jit(solution)/shard_map/ppermute | solution.py:108
  30.9 2.5 collective-permute-start.4
  36.4 2.4 collective-permute-start.10
  41.1 5.4 %collective-permute-done.12.refs_8_.refs_5_ = bf16[128,1024]{1,0:T(8,128)(2,1)S(1)} collective-permute-done((bf16[128,1024]{1,0:T(8,128)(2,1)S(1)}, bf16[128,1024]{1,0:T(8,128)(2,1)S(1)}, u32[]{:S(2)}, u32[]{:S(2)}) %collective-permute-start.12) | collective-permute-done | bytes 262176 | tf_op jit(solution)/shard_map/ppermute | solution.py:107
  57.2 8.6 %f0.1 = (bf16[1024,1024]{1,0:T(8,128)(2,1)}, bf16[1024,896]{1,0:T(8,128)(2,1)}, bf16[1024,1024]{1,0:T(8,128)(2,1)}, bf16[1024,768]{1,0:T(8,128)(2,1)}, f32[1024,...) custom-call(s32[2]{0:T(128)} %pad_add_fusion.ids.refs_0_, ...), custom_call_target="tpu_custom_call" | custom-call | flops 603979776 | bytes 3145728 | tf_op jit(solution)/shard_map/f0/pallas_call | solution.py:860
  68.9 6.2 %shard_map.194 = (bf16[1024,1024]{1,0:T(8,128)(2,1)}, bf16[1024,768]{1,0:T(8,128)(2,1)}, f32[1024,768]{1,0:T(8,128)}, f32[1024,128]{1,0:T(8,128)}, f32[1024,512]...) custom-call(s32[2]{0:T(128)} %pad_add_fusion.ids.refs_0_, ...), custom_call_target="tpu_custom_call", output_to_operand_aliasing={{0}: (11, {}), {1}: (12, {}), {2}: (13, {}), {3}: (14, {}),... | custom-call | flops 603979776 | bytes 3145728 | tf_op jit(solution)/shard_map/pallas_call | solution.py:880
  75.1 6.2 %shard_map.195 = (bf16[1024,1024]{1,0:T(8,128)(2,1)}, bf16[1024,768]{1,0:T(8,128)(2,1)}, f32[1024,768]{1,0:T(8,128)}, f32[1024,128]{1,0:T(8,128)}, f32[1024,512]...) custom-call(s32[2]{0:T(128)} %pad_add_fusion.ids.refs_0_, ...), custom_call_target="tpu_custom_call", output_to_operand_aliasing={{0}: (11, {}), {1}: (12, {}), {2}: (13, {}), {3}: (14, {}),... | custom-call | flops 603979776 | bytes 3145728 | tf_op jit(solution)/shard_map/pallas_call | solution.py:880
  81.3 6.2 %shard_map.196 = (bf16[1024,1024]{1,0:T(8,128)(2,1)}, bf16[1024,768]{1,0:T(8,128)(2,1)}, f32[1024,768]{1,0:T(8,128)}, f32[1024,128]{1,0:T(8,128)}, f32[1024,512]...) custom-call(s32[2]{0:T(128)} %pad_add_fusion.ids.refs_0_, ...), custom_call_target="tpu_custom_call", output_to_operand_aliasing={{0}: (11, {}), {1}: (12, {}), {2}: (13, {}), {3}: (14, {}),... | custom-call | flops 603979776 | bytes 3145728 | tf_op jit(solution)/shard_map/pallas_call | solution.py:880
  88.2 10.5 %gate.1 = (bf16[1024,1024]{1,0:T(8,128)(2,1)}, bf16[1024,512]{1,0:T(8,128)(2,1)}, bf16[512,1024]{1,0:T(8,128)(2,1)}, f32[1024,512]{1,0:T(8,128)}, f32[1024,512]{...) custom-call(s32[2]{0:T(128)} %pad_add_fusion.ids.refs_0_, bf16[256,1024]{1,0:T(8,128)(2,1)} %copy-done.8, ...), custom_call_target="tpu_custom_call" | custom-call | flops 2147483648 | bytes 14680064 | tf_op jit(solution)/shard_map/gate/pallas_call | solution.py:898
  101.6 3.3 %collective-permute-done.24 = f32[8,1024]{1,0:T(8,128)S(1)} collective-permute-done((f32[8,1024]{1,0:T(8,128)S(1)}, f32[8,1024]{1,0:T(8,128)S(1)}, u32[]{:S(2)}, u32[]{:S(2)}) %collective-permute-start.24) | collective-permute-done | bytes 32800 | tf_op jit(solution)/shard_map/ppermute | solution.py:30
  105.5 13.0 %turn.1 = (bf16[1024,512]{1,0:T(8,128)(2,1)}, bf16[1024,512]{1,0:T(8,128)(2,1)}, f32[1024,512]{1,0:T(8,128)}, f32[1,512]{1,0:T(1,128)}, bf16[1024,1024]{1,0:T(8,...) custom-call(s32[2]{0:T(128)} %pad_add_fusion.ids.refs_0_, ...), custom_call_target="tpu_custom_call" | custom-call | flops 3221225472 | bytes 15728640 | tf_op jit(solution)/shard_map/turn/pallas_call | solution.py:934
  119.0 2.2 collective-permute-start.27
  121.2 2.3 dynamic-slice_bitcast_fusion.1
  123.5 14.3 %shard_map.197 = (bf16[1024,896]{1,0:T(8,128)(2,1)}, f32[512,128]{1,0:T(8,128)}, f32[8,768]{1,0:T(8,128)}, f32[8,768]{1,0:T(8,128)}, f32[8,128]{1,0:T(8,128)}) custom-call(s32[2]{0:T(128)} %pad_add_fusion.ids.refs_0_, bf16[1024,768]{1,0:T(8,128)(2,1)} %get-tuple-element.126.refs_1_, f32[1024,768]{1,0:T(8,128)} %get-tuple-element.116.refs_14_.refs_2_, ...), custom_call_target="tpu_custom_call" | custom-call | flops 671088640 | bytes 7340032 | tf_op jit(solution)/shard_map/pallas_call | solution.py:971
  139.8 14.3 %shard_map.198 = (bf16[1024,896]{1,0:T(8,128)(2,1)}, f32[512,128]{1,0:T(8,128)}, f32[8,768]{1,0:T(8,128)}, f32[8,768]{1,0:T(8,128)}, f32[8,128]{1,0:T(8,128)}) custom-call(s32[2]{0:T(128)} %pad_add_fusion.ids.refs_0_, bf16[1024,768]{1,0:T(8,128)(2,1)} %get-tuple-element.126.refs_1_, ...), custom_call_target="tpu_custom_call", output_to_operand_aliasing={{0}: (15, {})} | custom-call | flops 671088640 | bytes 7340032 | tf_op jit(solution)/shard_map/pallas_call | solution.py:971
  154.1 6.4 %weight.1 = (bf16[4,128,384]{2,1,0:T(8,128)(2,1)}, bf16[544,384]{1,0:T(8,128)(2,1)}, bf16[4,128,512]{2,1,0:T(8,128)(2,1)}, bf16[4,128,512]{2,1,0:T(8,128)(2,1)}, bf16[32,384]{1,0:T(8,128)(2,1)}) custom-call(s32[2]{0:T(128)} %pad_add_fusion.ids.refs_0_, bf16[1024,1024]{1,0:T(8,128)(2,1)} %get-tuple-element.115.refs_13_.refs_5_.normed, ...), custom_call_target="tpu_custom_call" | custom-call | flops 1879048192 | bytes 6291456 | tf_op jit(solution)/shard_map/weight/pallas_call | solution.py:1003
  160.5 7.2 %e.1 = bf16[1024,1024]{1,0:T(8,128)(2,1)} custom-call(bf16[1024,896]{1,0:T(8,128)(2,1)} %get-tuple-element.139.d_proj, bf16[1024,512]{1,0:T(8,128)(2,1)} %get-tuple-element.140.d_gate, bf16[1024,896]{1,0:T(8,128)(2,1)} %get-tuple-element.90.refs_1_.w_one, bf16[1024,512]{1,0:T(8,128)(2,1)} %get-tuple-element.124.refs_8_.w_z, ...), custom_call_target="tpu_custom_call" | custom-call | flops 2818572288 | bytes 10485760 | tf_op jit(solution)/shard_map/e/pallas_call | solution.py:1053
  173.0 6.0 %collective-permute-done.31 = bf16[2,128,512]{2,1,0:T(8,128)(2,1)S(1)} collective-permute-done((bf16[2,128,512]{2,1,0:T(8,128)(2,1)S(1)}, bf16[2,128,512]{2,1,0:T(8,128)(2,1)S(1)}, u32[]{:S(2)}, u32[]{:S(2)}) %collective-permute-start.31) | collective-permute-done | bytes 262176 | tf_op jit(solution)/shard_map/ppermute | solution.py:30
  180.9 9.7 %collective-permute-done.34 = bf16[1,128,512]{2,1,0:T(8,128)(2,1)S(1)} collective-permute-done((bf16[1,128,512]{2,1,0:T(8,128)(2,1)S(1)}, bf16[1,128,512]{2,1,0:T(8,128)(2,1)S(1)}, u32[]{:S(2)}, u32[]{:S(2)}) %collective-permute-start.34) | collective-permute-done | bytes 131104 | tf_op jit(solution)/shard_map/ppermute | solution.py:30
  190.5 3.4 %collective-permute-start.32 = (bf16[1,128,512]{2,1,0:T(8,128)(2,1)S(1)}, bf16[1,128,512]{2,1,0:T(8,128)(2,1)S(1)}, u32[]{:S(2)}, u32[]{:S(2)}) collective-permute-start(bf16[1,128,512]{2,1,0:T(8,128)(2,1)S(1)} %constant_dynamic-slice_fusion.3), channel_id=1, source_target_pairs={{0,4},{1,5},{2,6},{3,7},{4,0},{5,1},{6,2},{7,3},{8,12},{9,13},{10,... | collective-permute-start | bytes 393224 | tf_op jit(solution)/shard_map/ppermute | solution.py:30
  194.0 5.7 %collective-permute-done.32 = bf16[1,128,512]{2,1,0:T(8,128)(2,1)S(1)} collective-permute-done((bf16[1,128,512]{2,1,0:T(8,128)(2,1)S(1)}, bf16[1,128,512]{2,1,0:T(8,128)(2,1)S(1)}, u32[]{:S(2)}, u32[]{:S(2)}) %collective-permute-start.32) | collective-permute-done | bytes 131104 | tf_op jit(solution)/shard_map/ppermute | solution.py:30
  202.5 9.2 %collective-permute-done.40 = bf16[288,384]{1,0:T(8,128)(2,1)S(1)} collective-permute-done((bf16[288,384]{1,0:T(8,128)(2,1)S(1)}, bf16[288,384]{1,0:T(8,128)(2,1)S(1)}, u32[]{:S(2)}, u32[]{:S(2)}) %collective-permute-start.40) | collective-permute-done | bytes 221216 | tf_op jit(solution)/shard_map/ppermute | solution.py:30
  215.4 4.8 %collective-permute-done.41 = bf16[160,384]{1,0:T(8,128)(2,1)S(1)} collective-permute-done((bf16[160,384]{1,0:T(8,128)(2,1)S(1)}, bf16[160,384]{1,0:T(8,128)(2,1)S(1)}, u32[]{:S(2)}, u32[]{:S(2)}) %collective-permute-start.41) | collective-permute-done | bytes 122912 | tf_op jit(solution)/shard_map/ppermute | solution.py:30
  220.6 2.7 %collective-permute-start.44 = (bf16[1,128,512]{2,1,0:T(8,128)(2,1)S(1)}, bf16[1,128,512]{2,1,0:T(8,128)(2,1)S(1)}, u32[]{:S(2)}, u32[]{:S(2)}) collective-permute-start(bf16[1,128,512]{2,1,0:T(8,128)(2,1)S(1)} %constant_dynamic-slice_fusion), channel_id=1, source_target_pairs={{0,4},{1,5},{2,6},{3,7},{4,0},{5,1},{6,2},{7,3},{8,12},{9,13},{10,... | collective-permute-start | bytes 393224 | tf_op jit(solution)/shard_map/ppermute | solution.py:30
  223.3 5.2 %collective-permute-done.44 = bf16[1,128,512]{2,1,0:T(8,128)(2,1)S(1)} collective-permute-done((bf16[1,128,512]{2,1,0:T(8,128)(2,1)S(1)}, bf16[1,128,512]{2,1,0:T(8,128)(2,1)S(1)}, u32[]{:S(2)}, u32[]{:S(2)}) %collective-permute-start.44) | collective-permute-done | bytes 131104 | tf_op jit(solution)/shard_map/ppermute | solution.py:30
  228.7 3.5 %collective-permute-start.46 = (bf16[160,896]{1,0:T(8,128)(2,1)S(1)}, bf16[160,896]{1,0:T(8,128)(2,1)}, u32[]{:S(2)}, u32[]{:S(2)}) collective-permute-start(bf16[160,896]{1,0:T(8,128)(2,1)S(1)} %pad_maximum_fusion.refs_4_), channel_id=1, source_target_pairs={{0,16},{8,24},{16,0},{24,8},{1,17},{9,25},{17,1},{25,9},{2,18},{10... | collective-permute-start | bytes 860168 | tf_op jit(solution)/shard_map/ppermute | solution.py:30
  234.1 5.9 %collective-permute-done.46.refs_6_ = bf16[160,896]{1,0:T(8,128)(2,1)} collective-permute-done((bf16[160,896]{1,0:T(8,128)(2,1)S(1)}, bf16[160,896]{1,0:T(8,128)(2,1)}, u32[]{:S(2)}, u32[]{:S(2)}) %collective-permute-start.46) | collective-permute-done | bytes 286752 | tf_op jit(solution)/shard_map/ppermute | solution.py:30
  246.1 3.7 %finish.1 = (f32[4384,128]{1,0:T(8,128)}, f32[256,1024]{1,0:T(8,128)}, f32[4,2304]{1,0:T(4,128)}, f32[1,2304]{1,0:T(1,128)}, f32[1,32]{1,0:T(1,128)}, /*index=5*...) custom-call(s32[2]{0:T(128)} %pad_add_fusion.ids.refs_0_, bf16[128,1024]{1,0:T(8,128)(2,1)} %copy-done.20, ...), custom_call_target="tpu_custom_call" | custom-call | tf_op jit(solution)/shard_map/finish/pallas_call | solution.py:1033
  252.4 8.7 %collective-permute-done.26 = bf16[1,256,1024]{2,1,0:T(8,128)(2,1)} collective-permute-done((bf16[1,256,1024]{2,1,0:T(8,128)(2,1)}, bf16[1,256,1024]{2,1,0:T(8,128)(2,1)}, u32[]{:S(2)}, u32[]{:S(2)}) %collective-permute-start.26) | collective-permute-done | bytes 524320 | tf_op jit(solution)/shard_map/ppermute | solution.py:30
  261.1 3.3 %fusion.5 = (f32[1,256,1024]{2,1,0:T(8,128)}, f32[1,256,1024]{2,1,0:T(8,128)}) fusion(bf16[1,256,1024]{2,1,0:T(8,128)(2,1)S(1)} %copy-done.2, f32[1,256,1024]{2,1,0:T(8,128)S(1)} %copy-done.6, bf16[1,256,1024]{2,1,0:T(8,128)(2,1)} %copy-done.9, f32[256]{0:T(256)S(1)} %get-tuple-element.174, f32[1024]{0:T(1024)S(1)} %copy-done.33, ...), kind=kLoop, calls=%fused_computation.11 | loop fusion | flops 4194304 | bytes 5773316 | tf_op jit(solution)/shard_map/sub | solution.py:1069
  (222 shorter events, 62.8 us)
Async XLA Ops:
  14.7 33.9 %collective-permute-start.20 = (bf16[256,1024]{1,0:T(8,128)(2,1)}, bf16[256,1024]{1,0:T(8,128)(2,1)}, u32[]{:S(2)}, u32[]{:S(2)}) collective-permute-start(bf16[256,1024]{1,0:T(8,128)(2,1)} %bitcast.76), channel_id=1, source_target_pairs={{0,8},{8,0},{16,24},{24,16},{1,9},{9,1},{17,25},{25,17},{2,10},{10... | collective-permute-start | bytes 1572872 | tf_op jit(solution)/shard_map/ppermute | solution.py:30
  14.7 26.4 %collective-permute-start.21 = (bf16[256,1024]{1,0:T(8,128)(2,1)}, bf16[256,1024]{1,0:T(8,128)(2,1)}, u32[]{:S(2)}, u32[]{:S(2)}) collective-permute-start(bf16[256,1024]{1,0:T(8,128)(2,1)} %bitcast.77), channel_id=1, source_target_pairs={{0,16},{8,24},{16,0},{24,8},{1,17},{9,25},{17,1},{25,9},{2,18},{10... | collective-permute-start | bytes 1572872 | tf_op jit(solution)/shard_map/ppermute | solution.py:30
  16.3 14.5 %collective-permute-start = (bf16[256,256]{1,0:T(8,128)(2,1)S(1)}, bf16[256,256]{1,0:T(8,128)(2,1)S(1)}, u32[]{:S(2)}, u32[]{:S(2)}) collective-permute-start(bf16[256,256]{1,0:T(8,128)(2,1)S(1)} %constant_dynamic-slice_fusion.8), channel_id=1, source_target_pairs={{0,0},{8,2},{16,4},{24,6},{1,1},{9,3},{17,5},{25,7},{2,8},{10,10},... | collective-permute-start | bytes 393224 | tf_op jit(solution)/shard_map/ppermute | solution.py:810
  19.1 11.7 %collective-permute-start.3 = (bf16[128,896]{1,0:T(8,128)(2,1)S(1)}, bf16[128,896]{1,0:T(8,128)(2,1)S(1)}, u32[]{:S(2)}, u32[]{:S(2)}) collective-permute-start(bf16[128,896]{1,0:T(8,128)(2,1)S(1)} %collective-permute-done.2.refs_7_), channel_id=1, source_target_pairs={{0,2},{2,4},{4,6},{6,7},{7,5},{5,3},{3,1},{1,0},{8,10},{10,12},{12... | collective-permute-start | bytes 688136 | tf_op jit(solution)/shard_map/ppermute | solution.py:107
  20.7 10.0 %collective-permute-start.7 = (bf16[128,896]{1,0:T(8,128)(2,1)S(1)}, bf16[128,896]{1,0:T(8,128)(2,1)S(1)}, u32[]{:S(2)}, u32[]{:S(2)}) collective-permute-start(bf16[128,896]{1,0:T(8,128)(2,1)S(1)} %collective-permute-done.6.refs_8_), channel_id=1, source_target_pairs={{2,0},{4,2},{6,4},{7,6},{5,7},{3,5},{1,3},{0,1},{10,8},{12,10},{14... | collective-permute-start | bytes 688136 | tf_op jit(solution)/shard_map/ppermute | solution.py:108
  36.4 14.2 %collective-permute-start.10 = (bf16[256,1024]{1,0:T(8,128)(2,1)S(1)}, bf16[256,1024]{1,0:T(8,128)(2,1)}, u32[]{:S(2)}, u32[]{:S(2)}) collective-permute-start(bf16[256,1024]{1,0:T(8,128)(2,1)S(1)} %convert_bitcast_fusion.refs_0_), channel_id=1, source_target_pairs={{0,16},{8,24},{16,0},{24,8},{1,17},{9,25},{17,1},{25,9},{2,18},{10... | collective-permute-start | bytes 1572872 | tf_op jit(solution)/shard_map/ppermute | solution.py:30
  41.1 16.1 %collective-permute-start.22 = (bf16[256,1024]{1,0:T(8,128)(2,1)}, bf16[256,1024]{1,0:T(8,128)(2,1)}, u32[]{:S(2)}, u32[]{:S(2)}) collective-permute-start(bf16[256,1024]{1,0:T(8,128)(2,1)} %collective-permute-done.21.refs_2_), channel_id=1, source_target_pairs={{0,8},{8,0},{16,24},{24,16},{1,9},{9,1},{17,25},{25,17},{2,10},{10... | collective-permute-start | bytes 1572872 | tf_op jit(solution)/shard_map/ppermute | solution.py:30
  48.6 38.9 %collective-permute-start.9 = (bf16[256,1024]{1,0:T(8,128)(2,1)S(1)}, bf16[256,1024]{1,0:T(8,128)(2,1)}, u32[]{:S(2)}, u32[]{:S(2)}) collective-permute-start(bf16[256,1024]{1,0:T(8,128)(2,1)S(1)} %convert_bitcast_fusion.refs_0_), channel_id=1, source_target_pairs={{0,8},{8,0},{16,24},{24,16},{1,9},{9,1},{17,25},{25,17},{2,10},{10... | collective-permute-start | bytes 1572872 | tf_op jit(solution)/shard_map/ppermute | solution.py:30
  50.6 36.9 %collective-permute-start.11 = (bf16[256,1024]{1,0:T(8,128)(2,1)}, bf16[256,1024]{1,0:T(8,128)(2,1)}, u32[]{:S(2)}, u32[]{:S(2)}) collective-permute-start(bf16[256,1024]{1,0:T(8,128)(2,1)} %collective-permute-done.10.refs_2_), channel_id=1, source_target_pairs={{0,8},{8,0},{16,24},{24,16},{1,9},{9,1},{17,25},{25,17},{2,10},{10... | collective-permute-start | bytes 1572872 | tf_op jit(solution)/shard_map/ppermute | solution.py:30
  53.3 12.6 %collective-permute-start.16 = (bf16[128,1024]{1,0:T(8,128)(2,1)S(1)}, bf16[128,1024]{1,0:T(8,128)(2,1)S(1)}, u32[]{:S(2)}, u32[]{:S(2)}) collective-permute-start(bf16[128,1024]{1,0:T(8,128)(2,1)S(1)} %collective-permute-done.14.refs_8_.refs_7_), channel_id=1, source_target_pairs={{0,2},{2,4},{4,6},{6,7},{7,5},{5,3},{3,1},{1,0},{8,10},{10,12},{12... | collective-permute-start | bytes 786440 | tf_op jit(solution)/shard_map/ppermute | solution.py:107
  53.7 13.4 %collective-permute-start.17 = (bf16[128,1024]{1,0:T(8,128)(2,1)S(1)}, bf16[128,1024]{1,0:T(8,128)(2,1)S(1)}, u32[]{:S(2)}, u32[]{:S(2)}) collective-permute-start(bf16[128,1024]{1,0:T(8,128)(2,1)S(1)} %collective-permute-done.15.refs_9_.refs_8_), channel_id=1, source_target_pairs={{2,0},{4,2},{6,4},{7,6},{5,7},{3,5},{1,3},{0,1},{10,8},{12,10},{14... | collective-permute-start | bytes 786440 | tf_op jit(solution)/shard_map/ppermute | solution.py:108
  66.6 20.9 %collective-permute-start.18 = (bf16[128,512]{1,0:T(8,128)(2,1)}, bf16[128,512]{1,0:T(8,128)(2,1)S(1)}, u32[]{:S(2)}, u32[]{:S(2)}) collective-permute-start(bf16[128,512]{1,0:T(8,128)(2,1)} %slice.85), channel_id=1, source_target_pairs={{0,2},{2,4},{4,6},{6,7},{7,5},{5,3},{3,1},{1,0},{8,10},{10,12},{12... | collective-permute-start | bytes 393224 | tf_op jit(solution)/shard_map/ppermute | solution.py:102
  67.1 20.4 %collective-permute-start.19 = (bf16[128,512]{1,0:T(8,128)(2,1)S(1)}, bf16[128,512]{1,0:T(8,128)(2,1)S(1)}, u32[]{:S(2)}, u32[]{:S(2)}) collective-permute-start(bf16[128,512]{1,0:T(8,128)(2,1)S(1)} %slice.86), channel_id=1, source_target_pairs={{2,0},{4,2},{6,4},{7,6},{5,7},{3,5},{1,3},{0,1},{10,8},{12,10},{14... | collective-permute-start | bytes 393224 | tf_op jit(solution)/shard_map/ppermute | solution.py:103
  118.5 19.3 %collective-permute-start.28 = (bf16[4,128,512]{2,1,0:T(8,128)(2,1)}, bf16[4,128,512]{2,1,0:T(8,128)(2,1)S(1)}, u32[]{:S(2)}, u32[]{:S(2)}) collective-permute-start(bf16[4,128,512]{2,1,0:T(8,128)(2,1)} %get-tuple-element.137), channel_id=1, source_target_pairs={{0,2},{1,3},{2,0},{3,1},{4,6},{5,7},{6,4},{7,5},{8,10},{9,11},{10,... | collective-permute-start | bytes 1572872 | tf_op jit(solution)/shard_map/ppermute | solution.py:30
  119.0 19.1 %collective-permute-start.27 = (bf16[4,128,512]{2,1,0:T(8,128)(2,1)}, bf16[4,128,512]{2,1,0:T(8,128)(2,1)S(1)}, u32[]{:S(2)}, u32[]{:S(2)}) collective-permute-start(bf16[4,128,512]{2,1,0:T(8,128)(2,1)} %get-tuple-element.135), channel_id=1, source_target_pairs={{0,1},{1,0},{2,3},{3,2},{4,5},{5,4},{6,7},{7,6},{8,9},{9,8},{10,11... | collective-permute-start | bytes 1572872 | tf_op jit(solution)/shard_map/ppermute | solution.py:30
  123.5 110.5 %collective-permute-start.25 = (bf16[2,256,1024]{2,1,0:T(8,128)(2,1)}, bf16[2,256,1024]{2,1,0:T(8,128)(2,1)}, u32[]{:S(2)}, u32[]{:S(2)}) collective-permute-start(bf16[2,256,1024]{2,1,0:T(8,128)(2,1)} %dynamic-slice_bitcast_fusion.1), channel_id=1, source_target_pairs={{0,8},{8,0},{16,24},{24,16},{1,9},{9,1},{17,25},{25,17},{2,10},{10... | collective-permute-start | bytes 3145736 | tf_op jit(solution)/shard_map/ppermute | solution.py:30
  138.0 33.7 %collective-permute-start.33 = (bf16[2,128,512]{2,1,0:T(8,128)(2,1)S(1)}, bf16[2,128,512]{2,1,0:T(8,128)(2,1)S(1)}, u32[]{:S(2)}, u32[]{:S(2)}) collective-permute-start(bf16[2,128,512]{2,1,0:T(8,128)(2,1)S(1)} %dynamic-slice_bitcast_fusion.3), channel_id=1, source_target_pairs={{0,1},{1,0},{2,3},{3,2},{4,5},{5,4},{6,7},{7,6},{8,9},{9,8},{10,11... | collective-permute-start | bytes 786440 | tf_op jit(solution)/shard_map/ppermute | solution.py:30
  169.2 63.0 %collective-permute-start.29 = (bf16[2,256,1024]{2,1,0:T(8,128)(2,1)S(1)}, bf16[2,256,1024]{2,1,0:T(8,128)(2,1)S(1)}, u32[]{:S(2)}, u32[]{:S(2)}) collective-permute-start(bf16[2,256,1024]{2,1,0:T(8,128)(2,1)S(1)} %dynamic-slice_bitcast_fusion), channel_id=1, source_target_pairs={{0,8},{8,0},{16,24},{24,16},{1,9},{9,1},{17,25},{25,17},{2,10},{10... | collective-permute-start | bytes 3145736 | tf_op jit(solution)/shard_map/ppermute | solution.py:30
  169.8 9.2 %collective-permute-start.31 = (bf16[2,128,512]{2,1,0:T(8,128)(2,1)S(1)}, bf16[2,128,512]{2,1,0:T(8,128)(2,1)S(1)}, u32[]{:S(2)}, u32[]{:S(2)}) collective-permute-start(bf16[2,128,512]{2,1,0:T(8,128)(2,1)S(1)} %dynamic-slice_bitcast_fusion.4), channel_id=1, source_target_pairs={{0,2},{1,3},{2,0},{3,1},{4,6},{5,7},{6,4},{7,5},{8,10},{9,11},{10,... | collective-permute-start | bytes 786440 | tf_op jit(solution)/shard_map/ppermute | solution.py:30
  170.7 29.9 %collective-permute-start.39 = (bf16[544,384]{1,0:T(8,128)(2,1)S(1)}, bf16[544,384]{1,0:T(8,128)(2,1)S(1)}, u32[]{:S(2)}, u32[]{:S(2)}) collective-permute-start(bf16[544,384]{1,0:T(8,128)(2,1)S(1)} %copy-done.42), channel_id=1, source_target_pairs={{0,1},{1,0},{2,3},{3,2},{4,5},{5,4},{6,7},{7,6},{8,9},{9,8},{10,11... | collective-permute-start | bytes 1253384 | tf_op jit(solution)/shard_map/ppermute | solution.py:30
  171.7 30.6 %collective-permute-start.42 = (bf16[4,128,512]{2,1,0:T(8,128)(2,1)S(1)}, bf16[4,128,512]{2,1,0:T(8,128)(2,1)S(1)}, u32[]{:S(2)}, u32[]{:S(2)}) collective-permute-start(bf16[4,128,512]{2,1,0:T(8,128)(2,1)S(1)} %copy-done.41), channel_id=1, source_target_pairs={{0,2},{1,3},{2,0},{3,1},{4,6},{5,7},{6,4},{7,5},{8,10},{9,11},{10,... | collective-permute-start | bytes 1572872 | tf_op jit(solution)/shard_map/ppermute | solution.py:30
  179.1 11.5 %collective-permute-start.34 = (bf16[1,128,512]{2,1,0:T(8,128)(2,1)S(1)}, bf16[1,128,512]{2,1,0:T(8,128)(2,1)S(1)}, u32[]{:S(2)}, u32[]{:S(2)}) collective-permute-start(bf16[1,128,512]{2,1,0:T(8,128)(2,1)S(1)} %constant_dynamic-slice_fusion.2), channel_id=1, source_target_pairs={{0,4},{1,5},{2,6},{3,7},{4,0},{5,1},{6,2},{7,3},{8,12},{9,13},{10,... | collective-permute-start | bytes 393224 | tf_op jit(solution)/shard_map/ppermute | solution.py:30
  190.5 9.1 %collective-permute-start.32 = (bf16[1,128,512]{2,1,0:T(8,128)(2,1)S(1)}, bf16[1,128,512]{2,1,0:T(8,128)(2,1)S(1)}, u32[]{:S(2)}, u32[]{:S(2)}) collective-permute-start(bf16[1,128,512]{2,1,0:T(8,128)(2,1)S(1)} %constant_dynamic-slice_fusion.3), channel_id=1, source_target_pairs={{0,4},{1,5},{2,6},{3,7},{4,0},{5,1},{6,2},{7,3},{8,12},{9,13},{10,... | collective-permute-start | bytes 393224 | tf_op jit(solution)/shard_map/ppermute | solution.py:30
  199.7 14.2 %collective-permute-start.35 = (bf16[128,512]{1,0:T(8,128)(2,1)S(1)}, bf16[128,512]{1,0:T(8,128)(2,1)S(1)}, u32[]{:S(2)}, u32[]{:S(2)}) collective-permute-start(bf16[128,512]{1,0:T(8,128)(2,1)S(1)} %fusion.17), channel_id=1, source_target_pairs={{0,0},{2,8},{4,16},{6,24},{1,1},{3,9},{5,17},{7,25},{8,2},{10,10},... | collective-permute-start | bytes 393224 | tf_op jit(solution)/shard_map/ppermute | solution.py:1031
  200.9 10.8 %collective-permute-start.40 = (bf16[288,384]{1,0:T(8,128)(2,1)S(1)}, bf16[288,384]{1,0:T(8,128)(2,1)S(1)}, u32[]{:S(2)}, u32[]{:S(2)}) collective-permute-start(bf16[288,384]{1,0:T(8,128)(2,1)S(1)} %pad_maximum_fusion.3), channel_id=1, source_target_pairs={{0,2},{1,3},{2,0},{3,1},{4,6},{5,7},{6,4},{7,5},{8,10},{9,11},{10,... | collective-permute-start | bytes 663560 | tf_op jit(solution)/shard_map/ppermute | solution.py:30
  213.9 19.6 %collective-permute-start.37 = (bf16[128,1024]{1,0:T(8,128)(2,1)S(1)}, bf16[128,1024]{1,0:T(8,128)(2,1)}, u32[]{:S(2)}, u32[]{:S(2)}) collective-permute-start(bf16[128,1024]{1,0:T(8,128)(2,1)S(1)} %pad_maximum_fusion.2.refs_0_), channel_id=1, source_target_pairs={{0,16},{8,24},{16,0},{24,8},{1,17},{9,25},{17,1},{25,9},{2,18},{10... | collective-permute-start | bytes 786440 | tf_op jit(solution)/shard_map/ppermute | solution.py:30
  228.7 11.3 %collective-permute-start.46 = (bf16[160,896]{1,0:T(8,128)(2,1)S(1)}, bf16[160,896]{1,0:T(8,128)(2,1)}, u32[]{:S(2)}, u32[]{:S(2)}) collective-permute-start(bf16[160,896]{1,0:T(8,128)(2,1)S(1)} %pad_maximum_fusion.refs_4_), channel_id=1, source_target_pairs={{0,16},{8,24},{16,0},{24,8},{1,17},{9,25},{17,1},{25,9},{2,18},{10... | collective-permute-start | bytes 860168 | tf_op jit(solution)/shard_map/ppermute | solution.py:30
  233.4 17.8 %collective-permute-start.30 = (bf16[1,256,1024]{2,1,0:T(8,128)(2,1)}, bf16[1,256,1024]{2,1,0:T(8,128)(2,1)S(1)}, u32[]{:S(2)}, u32[]{:S(2)}) collective-permute-start(bf16[1,256,1024]{2,1,0:T(8,128)(2,1)} %constant_dynamic-slice_fusion.4), channel_id=1, source_target_pairs={{0,16},{8,24},{16,0},{24,8},{1,17},{9,25},{17,1},{25,9},{2,18},{10... | collective-permute-start | bytes 1572872 | tf_op jit(solution)/shard_map/ppermute | solution.py:30
  233.5 9.9 %collective-permute-start.36 = (bf16[128,1024]{1,0:T(8,128)(2,1)S(1)}, bf16[128,1024]{1,0:T(8,128)(2,1)S(1)}, u32[]{:S(2)}, u32[]{:S(2)}) collective-permute-start(bf16[128,1024]{1,0:T(8,128)(2,1)S(1)} %pad_maximum_fusion.2.refs_0_), channel_id=1, source_target_pairs={{0,8},{8,0},{16,24},{24,16},{1,9},{9,1},{17,25},{25,17},{2,10},{10... | collective-permute-start | bytes 786440 | tf_op jit(solution)/shard_map/ppermute | solution.py:30
  233.5 12.6 %collective-permute-start.38 = (bf16[128,1024]{1,0:T(8,128)(2,1)}, bf16[128,1024]{1,0:T(8,128)(2,1)}, u32[]{:S(2)}, u32[]{:S(2)}) collective-permute-start(bf16[128,1024]{1,0:T(8,128)(2,1)} %collective-permute-done.37.refs_2_), channel_id=1, source_target_pairs={{0,8},{8,0},{16,24},{24,16},{1,9},{9,1},{17,25},{25,17},{2,10},{10... | collective-permute-start | bytes 786440 | tf_op jit(solution)/shard_map/ppermute | solution.py:30
  234.0 12.1 %collective-permute-start.45 = (bf16[160,896]{1,0:T(8,128)(2,1)S(1)}, bf16[160,896]{1,0:T(8,128)(2,1)}, u32[]{:S(2)}, u32[]{:S(2)}) collective-permute-start(bf16[160,896]{1,0:T(8,128)(2,1)S(1)} %pad_maximum_fusion.refs_4_), channel_id=1, source_target_pairs={{0,8},{8,0},{16,24},{24,16},{1,9},{9,1},{17,25},{25,17},{2,10},{10... | collective-permute-start | bytes 860168 | tf_op jit(solution)/shard_map/ppermute | solution.py:30
  244.1 17.0 %collective-permute-start.26 = (bf16[1,256,1024]{2,1,0:T(8,128)(2,1)}, bf16[1,256,1024]{2,1,0:T(8,128)(2,1)}, u32[]{:S(2)}, u32[]{:S(2)}) collective-permute-start(bf16[1,256,1024]{2,1,0:T(8,128)(2,1)} %constant_dynamic-slice_fusion.5), channel_id=1, source_target_pairs={{0,16},{8,24},{16,0},{24,8},{1,17},{9,25},{17,1},{25,9},{2,18},{10... | collective-permute-start | bytes 1572872 | tf_op jit(solution)/shard_map/ppermute | solution.py:30
  (59 other events, 731.1 us)
